TPU v7x, 32 devices: a whole 2x2x4 slice. The times are simulated.
32 devices in a mesh: seq: 8 (over y, x, core), stream: 4 (over z).
Axes of the slice: x: 2, y: 2, z: 4, core: 2. Of those that a mesh axis runs over, the one named last changes fastest.
Arguments:
- inputs: bfloat16 [4, 8192, 768], P('stream', 'seq'), may hold values from -11 to 11
- resets: int32 [4, 8192], P('stream', 'seq'), may hold values 0 or 1
- norm_gains: bfloat16 [768, 2], P(('seq', 'stream')), may hold values from 0.5 to 1.5
- norm_biases: bfloat16 [768, 2], P(('seq', 'stream')), may hold values from -1.25 to 1.25
- w_qkv: bfloat16 [768, 2304], P(('seq', 'stream')), may hold values from -1 to 1
- w_feat: bfloat16 [768, 128], P(('seq', 'stream')), may hold values from -0.75 to 0.75
- w_out: bfloat16 [768, 768], P(('seq', 'stream')), may hold values from -0.875 to 0.875
- w_fc: bfloat16 [768, 3072], P(('seq', 'stream')), may hold values from -1 to 1
- w_proj: bfloat16 [3072, 768], P(('seq', 'stream')), may hold values from -0.109375 to 0.109375
- cotangent: bfloat16 [4, 8192, 768], P('stream', 'seq'), may hold values from -6 to 6
Outputs:
- outputs: bfloat16 [4, 8192, 768], P('stream', 'seq')
- input_grad: float32 [4, 8192, 768], P('stream', 'seq')
- grad_gains: float32 [768, 2], P(('seq', 'stream'))
- grad_biases: float32 [768, 2], P(('seq', 'stream'))
- grad_qkv: float32 [768, 2304], P(('seq', 'stream'))
- grad_feat: float32 [768, 128], P(('seq', 'stream'))
- grad_out: float32 [768, 768], P(('seq', 'stream'))
- grad_fc: float32 [768, 3072], P(('seq', 'stream'))
- grad_proj: float32 [3072, 768], P(('seq', 'stream'))
- branch_rms: float32 [4, 3], P('stream')
Inputs may be any that keep to these rules, and one draw needn't show every extreme that they name: `resets`: A stream's first token starts a document whether it is marked or not.
All inputs are finite; a program needn't handle non-finite values. No bound on the sum of `resets` on one device may be relied on, other than what follows from the above.
Results may differ from a plain program's by a relative error of at most 0.015.
Values may be sent and summed in bfloat16 or wider, within the bound.
No kernel may reach another device: no remote copies, remote signals or barrier semaphores. Data moves between devices by JAX's collectives and lax.ppermute only.
A program may use at most 256 MiB of HBM per device.

v0:
```python
import functools

import jax
import jax.numpy as jnp
from jax import lax
from jax.experimental import pallas as pl
from jax.experimental.pallas import tpu as pltpu
from jax.sharding import PartitionSpec as P

BT = 256
GF = 6
TK = 512
TM = 256
epsilon = 1e-05
f32 = jnp.float32
bf16 = jnp.bfloat16
GC = 0.7978845608028654
GA = 0.044715


def mm(a, b):
    return jnp.dot(a, b, preferred_element_type=f32)


def mm_t(a, b):
    return lax.dot_general(a, b, (((1,), (1,)), ((), ())), preferred_element_type=f32)


def mm_f(a, b):
    return lax.dot_general(a, b, (((0,), (0,)), ((), ())), preferred_element_type=f32)


def xor_send(arr, size, mask):
    return lax.ppermute(arr, "seq", [(i, i ^ mask) for i in range(size)])


def after(arr, *deps):
    return lax.optimization_barrier((arr,) + deps)[0]


def stream_send(shard, depth):
    return [shard] + [
        lax.ppermute(shard, "stream", [(i, (i + d) % depth) for i in range(depth)])
        for d in range(1, depth)
    ]


def stream_rows(pieces, depth):
    shard = pieces[0]
    ring = pieces[::-1]
    place = lax.axis_index("stream")
    rows = shard.shape[0]
    both = jnp.concatenate(ring + ring, axis=0)
    return lax.dynamic_slice_in_dim(both, (depth - 1 - place) * rows, depth * rows, 0)


class Spread:
    def __init__(self, block, size, flip):
        self.size = size
        bits = [1 << b for b in range(1, size.bit_length() - 1)]
        self.bits = bits[::-1] if flip else bits
        self.block = block
        self.found = {0: block}

    def near(self, *deps):
        block = after(self.block, *deps) if deps else self.block
        for bit in self.bits:
            self.found[bit] = xor_send(block, self.size, bit)
        return self

    def near_all(self):
        for r in range(2, self.size, 2):
            self.found[r] = xor_send(self.block, self.size, r)
        return self

    def far(self, *deps):
        for bit in self.bits:
            for r in list(self.found):
                if r ^ bit not in self.found and r < 2 * max(self.bits):
                    src = self.found[r]
                    self.found[r ^ bit] = xor_send(after(src, *deps) if deps else src, self.size, bit)
        return self

    def far_halves(self):
        one, two = self.bits[:2]
        half = self.block.shape[1] // 2
        self.cuts = [self.found[one][:, :half], self.found[two][:, half:]]
        left = xor_send(self.cuts[0], self.size, two)
        right = xor_send(self.cuts[1], self.size, one)
        self.found[one ^ two] = jnp.concatenate([left, right], axis=1)
        return self.far()

    def cores(self, *deps):
        parts = [self.found[2 * r] for r in range(self.size // 2)]
        if deps:
            parts = lax.optimization_barrier(tuple(parts) + deps)[: len(parts)]
        stack = jnp.stack(parts)
        return [stack, xor_send(stack, self.size, 1)]


def beside(parts):
    return parts[0] if len(parts) == 1 else jnp.concatenate(parts, axis=-1)


class Reduce:
    def __init__(self, grads, size, depth, order=None, rest=None):
        self.size, self.depth = size, depth
        nbits = size.bit_length() - 1
        self.rest = list(range(nbits))[::-1] if rest is None else list(rest)
        self.order = list(range(nbits)) if order is None else list(order)
        self.cur = [
            g.reshape([2] * len(self.rest) + [g.shape[0] // 2 ** len(self.rest), g.shape[1]])
            if g.ndim == 2
            else g
            for g in grads
        ]

    def send(self):
        place = lax.axis_index("seq")
        bit = self.order.pop(0)
        axis = self.rest.index(bit)
        own = (place >> bit) & 1
        self.out = beside([lax.dynamic_index_in_dim(c, 1 - own, axis, False) for c in self.cur])
        self.kept = [lax.dynamic_index_in_dim(c, own, axis, False) for c in self.cur]
        self.flight = xor_send(self.out, self.size, 1 << bit)
        self.rest.pop(axis)
        return self

    def add(self, *deps):
        got = after(self.flight, *deps) if deps else self.flight
        self.cur = [(beside(self.kept).astype(f32) + got.astype(f32)).astype(bf16)]
        return self

    def cut(self, at):
        (cur,) = self.cur
        parts = [
            Reduce([cur[..., :at]], self.size, self.depth, self.order, self.rest),
            Reduce([cur[..., at:]], self.size, self.depth, self.order[::-1], self.rest),
        ]
        return parts

    def send_stream(self):
        while self.order:
            self.send().add()
        depth = self.depth
        level = lax.axis_index("stream")
        cur = beside(self.cur)
        self.out = cur
        cur = cur.reshape(depth, cur.shape[0] // depth, cur.shape[1])
        self.total = lax.dynamic_index_in_dim(cur, level, 0, False).astype(f32)
        self.flights = []
        for d in range(1, depth):
            piece = lax.dynamic_index_in_dim(cur, (level + d) % depth, 0, False)
            self.flights.append(
                lax.ppermute(piece, "stream", [(i, (i + d) % depth) for i in range(depth)])
            )
        return self

    def done(self, *deps):
        total = self.total
        for f in self.flights:
            total = total + (after(f, *deps) if deps else f).astype(f32)
        return total


def lanes(shape):
    return lax.broadcasted_iota(jnp.int32, shape, len(shape) - 1)


def block_ones(width, part):
    r = lax.broadcasted_iota(jnp.int32, (width, width), 0) // part
    c = lax.broadcasted_iota(jnp.int32, (width, width), 1) // part
    return jnp.where(r == c, 1.0, 0.0).astype(bf16)


def fetch_start(stacks, dest, me, sems, col=0, width=None, at=0):
    half = stacks[0].shape[0]
    rows = dest.shape[0] // (2 * half)
    width = width or stacks[0].shape[2]
    copies = []
    for c, ref in enumerate(stacks):
        for r in range(half):
            off = pl.multiple_of((me ^ (2 * r + c)) * rows, 8)
            copy = pltpu.make_async_copy(
                ref.at[r, :, pl.ds(col, width)],
                dest.at[pl.ds(off, rows), pl.ds(at, width)],
                sems.at[2 * r + c],
            )
            copy.start()
            copies.append(copy)
    return copies


def pair_maps(feat_ref, dest, pairs, which):
    width = 128
    lane = lanes((width, width))
    row = lax.broadcasted_iota(jnp.int32, (width, width), 0)
    for p in range(pairs):
        both = feat_ref[pl.ds(p * width, width), :].astype(f32)
        half = width // 2
        other = pltpu.roll(both, half, 1)
        if which == 0:
            signed = jnp.where(lane < half, both, -other)
        else:
            signed = jnp.where(lane < half, other, -both)
        dest[p, :, pl.ds(0, width)] = jnp.where(row < half, signed, 0.0).astype(bf16)
        dest[p, :, pl.ds(width, width)] = jnp.where(row >= half, signed, 0.0).astype(bf16)


def features(logits_of, ones):
    halves = [one[:, j * 128 : (j + 1) * 128] for one in logits_of for j in range(2)]
    low = lanes(halves[0].shape) < 64
    tops = [
        (
            jnp.max(jnp.where(low, one, -jnp.inf), axis=1, keepdims=True),
            jnp.max(jnp.where(low, -jnp.inf, one), axis=1, keepdims=True),
        )
        for one in halves
    ]
    exps = [jnp.exp(one - jnp.where(low, *top)) for one, top in zip(halves, tops)]
    exps = [jnp.concatenate(exps[2 * i : 2 * i + 2], axis=1) for i in range(len(logits_of))]
    sums = [mm(e.astype(bf16), ones) for e in exps]
    return [(e / t).astype(bf16) for e, t in zip(exps, sums)]


def augmented(two):
    low = lanes(two.shape) < 64
    one = jnp.ones_like(two)
    return jnp.where(low, two, one), jnp.where(low, one, two)


def pack_states(get, dest, pairs, zsum):
    shape = (128, 128)
    lane = lanes(shape)
    low = lane < 64
    zt = jnp.zeros(shape, f32)
    for p in range(pairs):
        a, b = get(2 * p), get(2 * p + 1)
        dest[p] = jnp.where(low, a, b).astype(bf16)
        if zsum:
            za = jnp.sum(jnp.where(low, 0.0, a), axis=1, keepdims=True)
            zb = jnp.sum(jnp.where(low, b, 0.0), axis=1, keepdims=True)
        else:
            za, zb = a, b
        zt = jnp.where(lane == 64 + 2 * p, za, zt)
        zt = jnp.where(lane == 2 * p + 1, zb, zt)
    dest[pairs] = zt.astype(bf16)


def unpack_states(me, keep_ref, blocks, put, base, count, pairs, back):
    shape = (128, 128)
    lane = lanes(shape)
    low = lane < 64
    size = 2 * blocks.shape[1]
    coefs = [None]
    for r in range(1, size):
        j = me ^ r
        c = jnp.where(j > me if back else j < me, 1.0, 0.0)
        for i in range(size):
            between = ((i > me) & (i < j)) if back else ((i > j) & (i < me))
            c = c * jnp.where(between, keep_ref[i], 1.0)
        coefs.append(c)

    def total(i):
        acc = jnp.zeros(shape, f32)
        for r in range(1, size):
            acc = acc + coefs[r] * blocks[r % 2, r // 2, i].astype(f32)
        return acc

    zt = total(pairs)
    for q in range(count):
        p = base + q
        two = total(p)
        za = jnp.sum(jnp.where(lane == 64 + 2 * p, zt, 0.0), axis=1, keepdims=True)
        zb = jnp.sum(jnp.where(lane == 2 * p + 1, zt, 0.0), axis=1, keepdims=True)
        if back:
            put(2 * q, jnp.where(low, two, jnp.where(lane == 64, za, 0.0)))
            put(2 * q + 1, jnp.where(low, jnp.where(lane == 0, zb, 0.0), two))
        else:
            put(2 * q, jnp.where(low, two, za))
            put(2 * q + 1, jnp.where(low, zb, two))


def normed(values, gain, bias):
    mean = jnp.mean(values, axis=1, keepdims=True)
    cent = values - mean
    rstd = lax.rsqrt(jnp.mean(cent * cent, axis=1, keepdims=True) + epsilon)
    hat = cent * rstd
    return hat * gain + bias, hat, rstd


def normed_back(grad, hat, rstd, gain):
    dhat = grad * gain
    return rstd * (
        dhat
        - jnp.mean(dhat, axis=1, keepdims=True)
        - hat * jnp.mean(dhat * hat, axis=1, keepdims=True)
    )


def keys_body(n_seq, pairs, me_ref, cend_ref, x_ref, cnt_ref, *refs):
    width = x_ref.shape[1]
    wl = refs[:2]
    (h_ref, k_ref, v_ref, phi_ref, st_ref, gb_ref, feat_ref, w1, maps, state, sems) = refs[2:]
    step = pl.program_id(0)

    @pl.when(step == 0)
    def _():
        me = me_ref[0]
        copies = fetch_start(wl, w1, me, sems.at[0], width, 2 * width + 256)
        for c in copies:
            c.wait()
        gb_ref[...] = w1[:, pl.ds(2 * width + 128, 128)].astype(f32).T[:8]
        feat_ref[...] = w1[:, pl.ds(2 * width, 128)]
        pair_maps(feat_ref, maps, pairs, 1)
        state[...] = jnp.zeros_like(state)

    gb = gb_ref[...]
    out, _, _ = normed(x_ref[...].astype(f32), gb[0:1], gb[2:3])
    h1 = out.astype(bf16)
    h_ref[...] = h1
    keys = mm(h1, w1[:, pl.ds(0, width)]).astype(bf16)
    vals = mm(h1, w1[:, pl.ds(width, width)]).astype(bf16)
    k_ref[...] = keys
    v_ref[...] = vals
    ones = block_ones(256, 64)
    last = cend_ref[cend_ref.shape[0] - 1]
    used = jnp.where(cnt_ref[...] == last, 1.0, 0.0).astype(bf16)
    for g in range(0, pairs, GF):
        group = range(g, min(g + GF, pairs))
        phis = features([mm(keys[:, p * 128 : (p + 1) * 128], maps[p]) for p in group], ones)
        for p, phi in zip(group, phis):
            phi_ref[:, pl.ds(p * 256, 256)] = phi
            va, vb = augmented(vals[:, p * 128 : (p + 1) * 128])
            state[2 * p] += mm_f(phi[:, :128], va * used)
            state[2 * p + 1] += mm_f(phi[:, 128:], vb * used)

    @pl.when(step == pl.num_programs(0) - 1)
    def _():
        pack_states(lambda h: state[h], st_ref, pairs, False)


def local_body(base, pairs, me_ref, cend_ref, h_ref, phik_ref, v_ref, cnt_ref, row_ref, feat_ref, *refs):
    wq = refs[:2]
    (q_ref, phiq_ref, num_ref, den_ref, srel_ref, state, w1, maps, sems) = refs[-9:]
    step = pl.program_id(0)
    width = h_ref.shape[1]

    @pl.when(step == 0)
    def _():
        copies = fetch_start(wq, w1, me_ref[0], sems, 0, width)
        pair_maps(feat_ref, maps, pairs, 0)
        if base:
            state[...] = refs[2][...]
        else:
            state[...] = jnp.zeros_like(state)
        for c in copies:
            c.wait()

    queries = mm(h_ref[...], w1[...]).astype(bf16)
    q_ref[...] = queries
    ones = block_ones(256, 64)
    size = h_ref.shape[0]
    cnt = cnt_ref[...]
    first, last = cend_ref[base + step], cend_ref[base + step + 1]
    row_id = lax.broadcasted_iota(jnp.int32, (size, size), 0)
    mask = (row_id >= lanes((size, size))) & (cnt == row_ref[...])
    before = jnp.where(cnt == first, 1.0, 0.0)
    after = jnp.where(cnt == last, 1.0, 0.0).astype(bf16)
    keep = jnp.where(first == last, 1.0, 0.0)
    low = lanes((size, 128)) < 64
    for g in range(0, pairs, GF):
        group = range(g, min(g + GF, pairs))
        phis = features([mm(queries[:, p * 128 : (p + 1) * 128], maps[p]) for p in group], ones)
        for p, phi in zip(group, phis):
            phiq_ref[:, pl.ds(p * 256, 256)] = phi
        pqs = [phi[:, j * 128 : (j + 1) * 128] for phi in phis for j in range(2)]
        heads = [2 * p + j for p in group for j in range(2)]
        pks = [phik_ref[:, pl.ds(h * 128, 128)] for h in heads]
        scores = [jnp.where(mask, mm_t(pq, pk), 0.0).astype(bf16) for pq, pk in zip(pqs, pks)]
        val_of = [v for p in group for v in augmented(v_ref[:, p * 128 : (p + 1) * 128])]
        res = []
        for h, pq, pk, sc, val in zip(heads, pqs, pks, scores, val_of):
            st = state[h]
            st_b = st.astype(bf16)
            srel_ref[0, h] = st_b
            res.append(mm(sc, val) + before * mm(pq, st_b))
            state[h] = keep * st + mm_f(pk, val * after)
        for i, p in enumerate(group):
            two = pl.ds(p * 128, 128)
            num_ref[:, two] = jnp.where(low, res[2 * i], res[2 * i + 1])
            den_ref[:, two] = pltpu.roll(jnp.where(low, res[2 * i + 1], res[2 * i]), 64, 1)


def middle_body(
    n_seq, pairs, me_ref, keep_ref, x_ref, dy_ref, num_ref, den_ref, phiq_ref, cnt_ref, gb_ref, *refs
):
    width = x_ref.shape[1]
    wf, wp, sts = (refs[2 * i : 2 * i + 2] for i in range(3))
    (
        y_ref, o_ref, h_ref, a_ref, df_ref, dat_ref, dr_ref, dd_ref, sin_ref, gst_ref, sum_ref,
        w_out, w_fc, w_proj, rden, state, stv, sems,
    ) = refs[6:]
    step = pl.program_id(0)
    chunk = 768
    hidden = w_fc.shape[1]
    size = x_ref.shape[0]

    @pl.when(step == 0)
    def _():
        me = me_ref[0]
        st_copies = []
        for c in range(2):
            st_copies.append(pltpu.make_async_copy(sts[c], stv.at[c], sems.at[3, c]))
            st_copies[c].start()
        copies = fetch_start(wf, w_out, me, sems.at[0], hidden, width)
        copies += fetch_start(wf, w_fc, me, sems.at[1], 0, hidden)
        copies += fetch_start(wp, w_proj, me, sems.at[2])
        for c in st_copies:
            c.wait()

        def put(h, value):
            sin_ref[h] = value.astype(bf16)

        unpack_states(me, keep_ref, stv, put, 0, pairs, pairs, False)
        state[...] = jnp.zeros_like(state)
        sum_ref[...] = jnp.zeros_like(sum_ref)
        for c in copies:
            c.wait()

    gb = gb_ref[...]
    low = lanes((size, 128)) < 64
    start = jnp.where(cnt_ref[...] == 0.0, 1.0, 0.0)
    start_b = start.astype(bf16)
    res = [mm(phiq_ref[:, pl.ds(h * 128, 128)], sin_ref[h]) for h in range(2 * pairs)]
    for p in range(pairs):
        two = pl.ds(p * 128, 128)
        ra, rb = res[2 * p], res[2 * p + 1]
        num = num_ref[:, two] + start * jnp.where(low, ra, rb)
        den = den_ref[:, two] + start * pltpu.roll(jnp.where(low, rb, ra), 64, 1)
        inv = 1.0 / den
        rden[:, two] = inv
        o_ref[:, two] = (num * inv).astype(bf16)
    x = x_ref[...].astype(f32)
    attn = mm(o_ref[...], w_out[...])
    mid = x + attn
    out, hat, rstd = normed(mid, gb[1:2], gb[3:4])
    h2 = out.astype(bf16)
    h_ref[...] = h2
    dy_b = dy_ref[...]
    branch = jnp.zeros((size, width), f32)
    dh2 = jnp.zeros((size, width), f32)
    for c in range(w_fc.shape[1] // chunk):
        cols = pl.ds(c * chunk, chunk)
        fc = mm(h2, w_fc[:, cols])
        square = fc * fc
        tan = jnp.tanh(fc * (GC + GC * GA * square))
        half = 0.5 + 0.5 * tan
        act = (fc * half).astype(bf16)
        a_ref[:, cols] = act
        branch = branch + mm(act, w_proj[cols, :])
        slope = half + fc * (1.0 - half) * half * (2.0 * GC + 6.0 * GC * GA * square)
        dfc = (mm_t(dy_b, w_proj[cols, :]) * slope).astype(bf16)
        df_ref[:, cols] = dfc
        dh2 = dh2 + mm_t(dfc, w_fc[:, cols])
    y = mid + branch
    y_ref[...] = y.astype(bf16)
    sum_ref[0:1] += jnp.sum(attn * attn, axis=0, keepdims=True)
    sum_ref[1:2] += jnp.sum(branch * branch, axis=0, keepdims=True)
    sum_ref[2:3] += jnp.sum(y * y, axis=0, keepdims=True)
    sum_ref[3:4] += jnp.sum(dh2 * hat, axis=0, keepdims=True)
    sum_ref[4:5] += jnp.sum(dh2, axis=0, keepdims=True)
    dr = dy_b.astype(f32) + normed_back(dh2, hat, rstd, gb[1:2])
    dr_ref[...] = dr
    dat = dr.astype(bf16)
    dat_ref[...] = dat
    d_o = mm_t(dat, w_out[...])
    ones = block_ones(256, 64)
    lane = lanes((size, 128))
    quads = range(pairs // 2)
    fours = [pl.ds(q * 256, 256) for q in quads]
    d_os = [d_o[:, q * 256 : (q + 1) * 256] for q in quads]
    prods = [d * o_ref[:, c].astype(f32) for d, c in zip(d_os, fours)]
    his = [a.astype(bf16) for a in prods]
    los = [(a - hi.astype(f32)).astype(bf16) for a, hi in zip(prods, his)]
    ddens = [-(mm(hi, ones) + mm(lo, ones)) * rden[:, c] for hi, lo, c in zip(his, los, fours)]
    dnums = [(d * rden[:, c]).astype(bf16) for d, c in zip(d_os, fours)]
    near = lane & 63
    for p in range(pairs):
        sub = slice((p % 2) * 128, (p % 2 + 1) * 128)
        dd = pltpu.roll(ddens[p // 2][:, sub], 64, 1)
        dhi = dd.astype(bf16)
        dlo = (dd - dhi.astype(f32)).astype(bf16)
        aux = jnp.where(near == 0, dhi.astype(f32), jnp.where(near == 1, dlo.astype(f32), 0.0)).astype(bf16)
        dn = dnums[p // 2][:, sub]
        dd_ref[:, pl.ds(p * 256, 128)] = jnp.where(low, dn, aux)
        dd_ref[:, pl.ds(p * 256 + 128, 128)] = jnp.where(low, aux, dn)
    for h in range(2 * pairs):
        own = pl.ds(h * 128, 128)
        state[h] += mm_f(phiq_ref[:, own], dd_ref[:, own] * start_b)

    @pl.when(step == pl.num_programs(0) - 1)
    def _():
        pack_states(lambda h: state[h], gst_ref, pairs, True)
        total = jnp.sum(sum_ref[...], axis=1, keepdims=True)
        high = total.astype(bf16).astype(f32)
        place = lanes((8, 128))
        tile = jnp.where(place == 126, high, jnp.where(place == 127, total - high, 0.0))
        tile = jnp.concatenate([tile, jnp.zeros_like(tile)], axis=0)
        top = gst_ref[pairs, pl.ds(0, 16), :].astype(f32)
        gst_ref[pairs, pl.ds(0, 16), :] = (top + tile).astype(bf16)


def back_body(
    base, pairs, all_pairs, me_ref, keep_ref, cend_ref, q_ref, k_ref, v_ref, phiq_ref, phik_ref, dd_ref, srel_ref, sin_ref,
    cnt_ref, row_ref, feat_ref, *refs
):
    sts = refs[:2]
    (dqkv_ref, gfeat_ref, mapq, mapk, state, gq, gk, stv, sems) = refs[2:]
    step = pl.program_id(0)
    nblk = pl.num_programs(0)
    here = nblk - 1 - step

    @pl.when(step == 0)
    def _():
        copies = []
        for c in range(2):
            copies.append(pltpu.make_async_copy(sts[c], stv.at[c], sems.at[c]))
            copies[c].start()
        pair_maps(feat_ref, mapq, pairs, 0)
        pair_maps(feat_ref, mapk, pairs, 1)
        gq[...] = jnp.zeros_like(gq)
        gk[...] = jnp.zeros_like(gk)
        for c in copies:
            c.wait()

        def put(h, value):
            state[h] = value

        unpack_states(me_ref[0], keep_ref, stv, put, base, pairs, all_pairs, True)

    size = q_ref.shape[0]
    width = q_ref.shape[1]
    cnt = cnt_ref[...]
    first, last = cend_ref[here], cend_ref[here + 1]
    row_id = lax.broadcasted_iota(jnp.int32, (size, size), 0)
    col_id = lanes((size, size))
    same = cnt == row_ref[...]
    mask = (row_id >= col_id) & same
    mask_t = (col_id >= row_id) & same
    before = jnp.where(cnt == first, 1.0, 0.0).astype(bf16)
    after = jnp.where(cnt == last, 1.0, 0.0).astype(bf16)
    keep = jnp.where(first == last, 1.0, 0.0)
    opened = jnp.where(first == 0.0, 1.0, 0.0)
    ones = block_ones(256, 64)
    low = lanes((size, 128)) < 64
    heads = range(2 * pairs)
    cols = [pl.ds(h * 128, 128) for h in heads]
    vals = [v for p in range(pairs) for v in augmented(v_ref[:, pl.ds(p * 128, 128)])]
    scores_t = [
        jnp.where(mask_t, mm_t(phik_ref[:, c], phiq_ref[:, c]), 0.0).astype(bf16) for c in cols
    ]
    dsc = [jnp.where(mask, mm_t(dd_ref[:, c], v), 0.0).astype(bf16) for c, v in zip(cols, vals)]
    dsc_t = [jnp.where(mask_t, mm_t(v, dd_ref[:, c]), 0.0).astype(bf16) for c, v in zip(cols, vals)]
    sts = [
        (srel_ref[0, h].astype(f32) + opened * sin_ref[h].astype(f32)).astype(bf16) for h in heads
    ]
    dsts = [state[h].astype(bf16) for h in heads]
    ddws = [dd_ref[:, c] * before for c in cols]
    dphi_q = [mm(dsc[h], phik_ref[:, cols[h]]) + mm_t(ddws[h], sts[h]) for h in heads]
    dphi_k = [mm(dsc_t[h], phiq_ref[:, cols[h]]) + mm_t(vals[h] * after, dsts[h]) for h in heads]
    dvs = [mm(scores_t[h], dd_ref[:, cols[h]]) + mm(phik_ref[:, cols[h]] * after, dsts[h]) for h in heads]
    for h in heads:
        state[h] = keep * state[h] + mm_f(phiq_ref[:, cols[h]], ddws[h])
    for p in range(pairs):
        dqkv_ref[:, pl.ds(2 * width + p * 128, 128)] = jnp.where(low, dvs[2 * p], dvs[2 * p + 1]).astype(bf16)
    for phi_ref, dphi, rows_ref, maps, acc, base_col in (
        (phiq_ref, dphi_q, q_ref, mapq, gq, 0),
        (phik_ref, dphi_k, k_ref, mapk, gk, width),
    ):
        phis = [phi_ref[:, pl.ds(p * 256, 256)].astype(f32) for p in range(pairs)]
        dphis = [jnp.concatenate(dphi[2 * p : 2 * p + 2], axis=1) for p in range(pairs)]
        totals = [mm((phi * d).astype(bf16), ones) for phi, d in zip(phis, dphis)]
        dlogs = [(phi * (d - t)).astype(bf16) for phi, d, t in zip(phis, dphis, totals)]
        for p in range(pairs):
            two = pl.ds(p * 128, 128)
            dqkv_ref[:, pl.ds(base_col + p * 128, 128)] = mm_t(dlogs[p], maps[p]).astype(bf16)
            acc[p] += mm_f(rows_ref[:, two], dlogs[p])

    @pl.when(step == nblk - 1)
    def _():
        lane = lanes((128, 128))
        row = lax.broadcasted_iota(jnp.int32, (128, 128), 0)
        for p in range(pairs):
            outs = []
            for acc in (gq, gk):
                one = jnp.where(row < 64, acc[p, :, :128], acc[p, :, 128:])
                outs.append(one - pltpu.roll(one, 64, 1))
            gfeat_ref[pl.ds(p * 128, 128), :] = jnp.where(lane < 64, outs[0], -outs[1]).astype(bf16)


def enter_body(groups, me_ref, x_ref, dr_ref, gb_ref, *refs):
    width = x_ref.shape[1]
    grads = refs[:groups]
    wl = refs[groups : groups + 2]
    (dx_ref, sum_ref, w1, sems) = refs[groups + 2 :]

    @pl.when(pl.program_id(0) == 0)
    def _():
        me = me_ref[0]
        copies = fetch_start(wl, w1, me, sems.at[0], 0, 3 * width)
        sum_ref[...] = jnp.zeros_like(sum_ref)
        for c in copies:
            c.wait()

    gb = gb_ref[...]
    _, hat, rstd = normed(x_ref[...].astype(f32), gb[0:1], gb[2:3])
    part = width // groups
    dh = jnp.zeros(x_ref.shape, f32)
    for g in range(groups):
        for i in range(3):
            dh = dh + mm_t(grads[g][:, pl.ds(i * part, part)], w1[:, pl.ds(i * width + g * part, part)])
    dx_ref[...] = dr_ref[...] + normed_back(dh, hat, rstd, gb[0:1])
    sum_ref[0:1] += jnp.sum(dh * hat, axis=0, keepdims=True)
    sum_ref[1:2] += jnp.sum(dh, axis=0, keepdims=True)


def whole(*_):
    return pl.BlockSpec(memory_space=pl.ANY)


def smem():
    return pl.BlockSpec(memory_space=pltpu.SMEM)


def rows_spec(size, cols, back=None):
    if back is None:
        return pl.BlockSpec((size, cols), lambda i: (i, 0))
    return pl.BlockSpec((size, cols), lambda i: (back - 1 - i, 0))


def full_spec(shape):
    zeros = (0,) * len(shape)
    return pl.BlockSpec(shape, lambda i: zeros)


def sds(shape, kind):
    return jax.ShapeDtypeStruct(shape, kind)


def cparams():
    return pltpu.CompilerParams(
        dimension_semantics=("arbitrary",), vmem_limit_bytes=58 * 1024 * 1024
    )


def cost(micros):
    return pl.CostEstimate(
        flops=int(micros * 5e8), transcendentals=0, bytes_accessed=int(micros * 1e6)
    )


def dma(*shape):
    return pltpu.SemaphoreType.DMA(shape)


def shards(n_seq, depth, inputs, resets, norm_gains, norm_biases, w_qkv, w_feat, w_out, w_fc, w_proj, cotangent):
    tokens, width = inputs.shape[1], inputs.shape[2]
    hidden = w_fc.shape[1]
    head_dim = w_feat.shape[1] // 2
    heads = width // head_dim
    pairs = heads // 2
    rows = w_qkv.shape[0]
    nblk = tokens // BT
    x, dy = inputs[0], cotangent[0]
    me = lax.axis_index("seq")
    me_arr = me.reshape(1).astype(jnp.int32)

    marks = resets[0].reshape(nblk, BT).astype(bf16)
    flag = jnp.where(jnp.max(resets) == 0, 1.0, 0.0).astype(bf16)
    upper = jnp.triu(jnp.ones((BT, BT), bf16))
    inner = jnp.dot(marks, upper, preferred_element_type=f32)
    ends = jnp.cumsum(inner[:, -1])
    cend = jnp.concatenate([jnp.zeros((1,), f32), ends])
    counts = inner + cend[:-1, None]
    cnt_col = counts.reshape(tokens, 1)
    cnt_row = counts.reshape(1, tokens)

    norms = jnp.concatenate(
        [norm_gains, norm_biases, jnp.broadcast_to(flag, (rows, 1)), jnp.zeros((rows, 123), bf16)],
        axis=1,
    )
    first = stream_rows(stream_send(jnp.concatenate([w_qkv, w_feat, norms], axis=1), depth), depth)
    first = Spread(first, n_seq, False).near()
    up = jnp.concatenate([w_fc, w_out], axis=1)
    first.far_halves()
    up = stream_send(after(up, first.block), depth)
    first_blocks = first.cores()
    up = stream_rows([after(a, first_blocks[0]) for a in up], depth)
    up = Spread(up, n_seq, True).near(first_blocks[0])
    proj_pieces = stream_send(after(w_proj, first_blocks[1], up.block), depth)
    me_first = after(me_arr, up.block)

    packed = (pairs + 1, 128, 128)
    full = (heads, 128, 128)
    h_one, keys, vals, phi_k, state, gb, feat_all = pl.pallas_call(
        functools.partial(keys_body, n_seq, pairs),
        name="keys",
        cost_estimate=cost(22),
        grid=(tokens // TK,),
        in_specs=[smem(), smem(), rows_spec(TK, width), rows_spec(TK, 1)] + [whole()] * 2,
        out_specs=[rows_spec(TK, width)] * 3
        + [rows_spec(TK, 2 * width), full_spec(packed), full_spec((8, width)), full_spec((width, 128))],
        out_shape=[sds((tokens, width), bf16)] * 3
        + [sds((tokens, 2 * width), bf16), sds(packed, bf16), sds((8, width), f32), sds((width, 128), bf16)],
        scratch_shapes=[
            pltpu.VMEM((width, 2 * width + 256), bf16),
            pltpu.VMEM((pairs, 128, 256), bf16),
            pltpu.VMEM(full, f32),
            dma(2, n_seq),
        ],
        compiler_params=cparams(),
    )(me_first, cend, x, cnt_col, *first_blocks)
    level = lax.axis_index("stream")
    flags = gb[4].reshape(n_seq, depth, rows)[:, :, 0]
    keeps = lax.dynamic_index_in_dim(flags, level, 1, False)
    spread = Spread(state, n_seq, False).near_all()
    up.far(gb)
    proj = Spread(stream_rows([after(a, gb) for a in proj_pieces], depth), n_seq, False).near()
    part_blk = nblk // 2
    local = []
    for part in range(2):
        base = part * part_blk

        def here(size, cols):
            return pl.BlockSpec((size, cols), lambda i: (base + i, 0))

        blocks_out = [
            sds((tokens, width), bf16), sds((tokens, 2 * width), bf16), sds((tokens, width), f32),
            sds((tokens, width), f32), sds((nblk,) + full, bf16),
        ]
        if part:
            me_two = after(me_arr, up_blocks[0], *[proj.found[b] for b in proj.bits], *spread.found.values())
        else:
            me_two = after(me_arr, proj.block, state, after(up.found[up.bits[0]], gb))
        local = pl.pallas_call(
            functools.partial(local_body, base, pairs),
            name="local",
            cost_estimate=cost(15),
            grid=(part_blk,),
            in_specs=[
                smem(), smem(), here(BT, width), here(BT, 2 * width), here(BT, width), here(BT, 1),
                pl.BlockSpec((1, BT), lambda i: (0, base + i)), full_spec((width, 128)),
            ]
            + [whole()] * 2
            + ([full_spec(full)] + [whole()] * 5 if part else []),
            out_specs=[
                here(BT, width), here(BT, 2 * width), here(BT, width), here(BT, width),
                pl.BlockSpec((1,) + full, lambda i: (base + i, 0, 0, 0)), full_spec(full),
            ],
            out_shape=blocks_out + [sds(full, f32)],
            scratch_shapes=[
                pltpu.VMEM((width, width), bf16),
                pltpu.VMEM((pairs, 128, 256), bf16),
                dma(n_seq),
            ],
            input_output_aliases={11 + i: i for i in range(5)} if part else {},
            compiler_params=cparams(),
        )(
            me_two, cend, h_one, phi_k, vals, cnt_col, cnt_row, feat_all, *first_blocks,
            *([local[5]] + list(local[:5]) if part else []),
        )
        if part == 0:
            event = local[5]
            proj.far(event)
            up_blocks = up.cores(event)
    queries, phi_q, num, den, srel, event = local
    states = spread.cores(event)
    proj_blocks = proj.cores(event)

    y, att, h_two, act, d_fc, d_att, d_mid, dd, s_in, g_state, sums = pl.pallas_call(
        functools.partial(middle_body, n_seq, pairs),
        name="middle",
        cost_estimate=cost(43),
        grid=(tokens // TM,),
        in_specs=[
            smem(), smem(), rows_spec(TM, width), rows_spec(TM, width), rows_spec(TM, width),
            rows_spec(TM, width), rows_spec(TM, 2 * width), rows_spec(TM, 1), full_spec((8, width)),
        ]
        + [whole()] * 6,
        out_specs=[
            rows_spec(TM, width), rows_spec(TM, width), rows_spec(TM, width), rows_spec(TM, hidden),
            rows_spec(TM, hidden), rows_spec(TM, width), rows_spec(TM, width), rows_spec(TM, 2 * width),
            full_spec(full), full_spec(packed), full_spec((8, width)),
        ],
        out_shape=[
            sds((tokens, width), bf16), sds((tokens, width), bf16), sds((tokens, width), bf16),
            sds((tokens, hidden), bf16), sds((tokens, hidden), bf16), sds((tokens, width), bf16),
            sds((tokens, width), f32), sds((tokens, 2 * width), bf16), sds(full, bf16), sds(packed, bf16),
            sds((8, width), f32),
        ],
        scratch_shapes=[
            pltpu.VMEM((width, width), bf16),
            pltpu.VMEM((width, hidden), bf16),
            pltpu.VMEM((hidden, width), bf16),
            pltpu.VMEM((TM, width), f32),
            pltpu.VMEM(full, f32),
            pltpu.VMEM((2, n_seq // 2) + packed, bf16),
            dma(4, n_seq),
        ],
        compiler_params=cparams(),
    )(
        me_arr, keeps, x, dy, num, den, phi_q, cnt_col, gb,
        *up_blocks, *proj_blocks, *states,
    )

    spread = Spread(g_state, n_seq, True).near_all()
    norm_two = jnp.stack([sums[3], sums[4]], axis=1).astype(bf16)
    norm_two = jnp.concatenate([norm_two, jnp.zeros((width, 126), bf16)], axis=1)
    nbits = n_seq.bit_length() - 1
    g_fc = mm_f(h_two, d_fc).astype(bf16)
    g_out = mm_f(att, d_att).astype(bf16)
    red_fc = Reduce([g_fc, g_out, norm_two], n_seq, depth, [0] + list(range(1, nbits))[::-1]).send()
    g_states = spread.cores(red_fc.out)
    g_proj = mm_f(after(act, red_fc.out, g_states[0]), dy).astype(bf16)
    red_proj = Reduce([g_proj], n_seq, depth).send()
    red_fc.add(red_proj.out).send()
    red_proj.add(red_fc.out).send()
    me_back = after(me_arr, red_proj.out, red_fc.out)
    squares = sum(
        jnp.sum(stack[:, pairs, :3, 126:].astype(f32), axis=(0, 2)) for stack in g_states
    )
    branch_rms = jnp.sqrt(squares / (tokens * n_seq * width)).reshape(1, 3)

    groups = 2
    some = pairs // groups
    part = some * 128
    d_qkv, g_feat = [], []
    for g in range(groups):

        def spec(cols):
            return pl.BlockSpec((BT, cols), lambda i: (nblk - 1 - i, g))

        def one_group(shape):
            return pl.BlockSpec(shape, lambda i: (g,) + (0,) * (len(shape) - 1))

        one = (2 * some, 128, 128)
        d_one, g_one = pl.pallas_call(
            functools.partial(back_body, g * some, some, pairs),
            name="back",
            cost_estimate=cost(19),
            grid=(nblk,),
            in_specs=[
                smem(), smem(), smem(), spec(part), spec(part), spec(part), spec(2 * part), spec(2 * part),
                spec(2 * part), pl.BlockSpec((1,) + one, lambda i: (nblk - 1 - i, g, 0, 0)), one_group(one),
                rows_spec(BT, 1, nblk), pl.BlockSpec((1, BT), lambda i: (0, nblk - 1 - i)),
                one_group((part, 128)),
            ]
            + [whole()] * 2,
            out_specs=[rows_spec(BT, 3 * part, nblk), full_spec((part, 128))],
            out_shape=[sds((tokens, 3 * part), bf16), sds((part, 128), bf16)],
            scratch_shapes=[
                pltpu.VMEM((some, 128, 256), bf16),
                pltpu.VMEM((some, 128, 256), bf16),
                pltpu.VMEM(one, f32),
                pltpu.VMEM((some, 128, 256), f32),
                pltpu.VMEM((some, 128, 256), f32),
                pltpu.VMEM((2, n_seq // 2) + packed, bf16),
                dma(n_seq),
            ],
            compiler_params=cparams(),
        )(
            me_back, keeps, cend, queries, keys, vals, phi_q, phi_k, dd, srel, s_in, cnt_col, cnt_row,
            feat_all, *g_states,
        )
        d_qkv.append(d_one)
        g_feat.append(g_one)
        if g == 0:
            red_proj.add(d_one).send()
            me_back = after(me_arr, red_proj.out)

    last = d_qkv[-1]
    g_qkv = [mm_f(h_one, d).astype(bf16) for d in d_qkv]
    red_two = Reduce(g_qkv + [jnp.concatenate(g_feat, axis=0)], n_seq, depth).send()
    red_fc.add(red_two.out).send()
    red_proj.add(red_fc.out).send_stream()
    me_late = after(me_arr, red_proj.out, red_fc.out)
    dx, sums_one = pl.pallas_call(
        functools.partial(enter_body, groups),
        name="enter",
        cost_estimate=cost(11),
        grid=(tokens // TM,),
        in_specs=[smem(), rows_spec(TM, width), rows_spec(TM, width), full_spec((8, width))]
        + [rows_spec(TM, 3 * part)] * groups
        + [whole()] * 2,
        out_specs=[rows_spec(TM, width), full_spec((8, width))],
        out_shape=[sds((tokens, width), f32), sds((8, width), f32)],
        scratch_shapes=[pltpu.VMEM((width, 3 * width), bf16), dma(2, n_seq)],
        compiler_params=cparams(),
    )(me_late, x, d_mid, gb, *d_qkv, *first_blocks)
    norm_one = jnp.stack([sums_one[0], sums_one[1]], axis=1).astype(bf16)
    norm_one = jnp.concatenate([norm_one, jnp.zeros((width, 126), bf16)], axis=1)
    red_norm = Reduce([norm_one], n_seq, depth).send()
    red_a, red_b = red_two.add(dx).cut((groups * 3 * part + 256) // 2)
    red_a.send()
    red_norm.add(red_a.out)
    red_b.cur = [beside(red_b.cur + red_norm.cur)]
    red_b.send()
    red_fc.add(red_a.out, red_b.out).send_stream()
    grad_proj = red_proj.done(red_fc.out)
    while red_a.order:
        red_a.add().send()
        red_b.add().send()
    tail = Reduce(red_a.add().cur + red_b.add().cur, n_seq, depth, [], []).send_stream()
    grad_up = red_fc.done(tail.out)
    tail = tail.done()
    grads = [tail[:, g * 3 * part : (g + 1) * 3 * part] for g in range(groups)]
    grad_feat = tail[:, groups * 3 * part : groups * 3 * part + 128]
    norm_one = tail[:, groups * 3 * part + 128 :]
    grad_fc = grad_up[:, :hidden]
    grad_out = grad_up[:, hidden:]
    grad_qkv = jnp.concatenate(
        [grads[g][:, i * part : (i + 1) * part] for i in range(3) for g in range(groups)], axis=1
    )
    return (
        y[None],
        dx[None],
        jnp.concatenate([norm_one[:, 0:1], grad_out[:, width : width + 1]], axis=1),
        jnp.concatenate([norm_one[:, 1:2], grad_out[:, width + 1 : width + 2]], axis=1),
        grad_qkv,
        grad_feat,
        grad_out[:, :width],
        grad_fc,
        grad_proj,
        branch_rms,
    )


def solution(mesh):
    both = P(("seq", "stream"), None)
    acts = P("stream", "seq", None)
    placed = (acts, P("stream", "seq"), both, both, both, both, both, both, both, acts)
    return jax.shard_map(
        functools.partial(shards, mesh.shape["seq"], mesh.shape["stream"]),
        mesh=mesh,
        in_specs=placed,
        out_specs=(acts, acts, both, both, both, both, both, both, both, P("stream", None)),
        check_vma=False,
    )
```

profile of v0, /device:TPU:9, one launch (start us, length us, event | category | flops | bytes accessed | tf_op | source)
XLA Modules:
  0.0 337.5 jit_solution(6400924513826338619)
XLA Ops:
  2.1 1.3 reduce_max.9
  5.3 2.5 collective-permute-start.1
  7.7 2.2 collective-permute-start.2
  11.2 3.5 %collective-permute-done.1 = bf16[24,2560]{1,0:T(8,128)(2,1)S(1)} collective-permute-done((bf16[24,2560]{1,0:T(8,128)(2,1)S(1)}, bf16[24,2560]{1,0:T(8,128)(2,1)S(1)}, u32[]{:S(2)}, u32[]{:S(2)}) %collective-permute-start.1) | collective-permute-done | bytes 122912 | tf_op jit(solution)/shard_map/ppermute | solution.py:43
  14.8 3.2 collective-permute-done.2
  18.1 1.3 collective-permute-start.4
  19.4 1.2 collective-permute-start.5
  22.3 2.9 collective-permute-start.3
  25.2 4.5 %collective-permute-done.4 = bf16[96,2560]{1,0:T(8,128)(2,1)S(1)} collective-permute-done((bf16[96,2560]{1,0:T(8,128)(2,1)S(1)}, bf16[96,2560]{1,0:T(8,128)(2,1)S(1)}, u32[]{:S(2)}, u32[]{:S(2)}) %collective-permute-start.4) | collective-permute-done | bytes 491552 | tf_op jit(solution)/shard_map/ppermute | solution.py:34
  29.7 1.3 collective-permute-start.6
  31.1 1.3 collective-permute-start.7
  32.4 3.0 collective-permute-done.6
  36.8 3.3 collective-permute-start.10
  41.9 1.8 collective-permute-done.10.refs_1_.refs_3_
  43.7 2.2 collective-permute-start.16
  47.0 1.5 collective-permute-start.14
  48.6 13.7 %keys.1 = (bf16[1024,768]{1,0:T(8,128)(2,1)}, bf16[1024,768]{1,0:T(8,128)(2,1)}, bf16[1024,768]{1,0:T(8,128)(2,1)}, bf16[1024,1536]{1,0:T(8,128)(2,1)}, bf16[7,1...) custom-call(s32[1]{0:T(128)} %bitcast.me_ref, f32[5]{0:T(128)} %copy-done.22, ...), custom_call_target="tpu_custom_call" | custom-call | flops 11000000512 | bytes 22000000 | tf_op jit(solution)/shard_map/keys/pallas_call | solution.py:706
  65.6 10.2 %local.2 = (bf16[1024,768]{1,0:T(8,128)(2,1)}, bf16[1024,1536]{1,0:T(8,128)(2,1)}, f32[1024,768]{1,0:T(8,128)}, f32[1024,768]{1,0:T(8,128)}, bf16[4,12,128,128]{3,2,1,0:T(8,128)(2,1)}, /*index=5*/f32[12,128,128]{2,1,0:T(8,128)}) custom-call(s32[1]{0:T(128)} %bitcast.me_ref, f32[5]{0:T(128)} %copy-done.22, bf16[1024,768]{1,0:T(8,128)(2,1)} %get-tuple-element.112.h_ref, ...), custom_call_target="tpu_custom_call" | custom-call | flops 7500000256 | bytes 15000000 | tf_op jit(solution)/shard_map/local/pallas_call | solution.py:746
  76.8 2.7 collective-permute-done.13
  80.7 1.5 pad_maximum_fusion.1.refs_0_
  82.2 3.5 %collective-permute-start.22 = (bf16[4,96,3840]{2,1,0:T(8,128)(2,1)S(1)}, bf16[4,96,3840]{2,1,0:T(8,128)(2,1)}, u32[]{:S(2)}, u32[]{:S(2)}) collective-permute-start(bf16[4,96,3840]{2,1,0:T(8,128)(2,1)S(1)} %pad_maximum_fusion.1.refs_0_), channel_id=1, source_target_pairs={{0,4},{4,0},{8,12},{12,8},{16,20},{20,16},{24,28},{28,24},{1,5},{5... | collective-permute-start | bytes 8847368 | tf_op jit(solution)/shard_map/ppermute | solution.py:34
  85.7 16.2 %collective-permute-done.20 = bf16[7,128,128]{2,1,0:T(8,128)(2,1)S(1)} collective-permute-done((bf16[7,128,128]{2,1,0:T(8,128)(2,1)}, bf16[7,128,128]{2,1,0:T(8,128)(2,1)S(1)}, u32[]{:S(2)}, u32[]{:S(2)}) %collective-permute-start.20) | collective-permute-done | bytes 229408 | tf_op jit(solution)/shard_map/ppermute | solution.py:34
  103.9 10.7 %local.3 = (bf16[1024,768]{1,0:T(8,128)(2,1)}, bf16[1024,1536]{1,0:T(8,128)(2,1)}, f32[1024,768]{1,0:T(8,128)}, f32[1024,768]{1,0:T(8,128)}, bf16[4,12,128,128]{3,2,1,0:T(8,128)(2,1)}, /*index=5*/f32[12,128,128]{2,1,0:T(8,128)}) custom-call(s32[1]{0:T(128)} %bitcast.me_ref, ...), custom_call_target="tpu_custom_call", output_to_operand_aliasing={{0}: (11, {}), {1}: (12, {}), {2}: (13, {}), {3}: (14, {}),... | custom-call | flops 7500000256 | bytes 15000000 | tf_op jit(solution)/shard_map/local/pallas_call | solution.py:746
  115.8 1.7 pad_maximum_fusion.2.refs_2_
  117.5 2.6 collective-permute-start.24
  120.2 2.1 pad_maximum_fusion.5.refs_4_
  123.7 2.2 collective-permute-done.25.refs_5_
  126.0 43.1 %middle.1 = (bf16[1024,768]{1,0:T(8,128)(2,1)}, bf16[1024,768]{1,0:T(8,128)(2,1)}, bf16[1024,768]{1,0:T(8,128)(2,1)}, bf16[1024,3072]{1,0:T(8,128)(2,1)}, bf16[1...) custom-call(s32[1]{0:T(128)} %bitcast.me_ref, ...), custom_call_target="tpu_custom_call" | custom-call | flops 21500000256 | bytes 43000000 | tf_op jit(solution)/shard_map/middle/pallas_call | solution.py:781
  169.1 1.3 collective-permute-start.26
  171.8 8.3 %convolution_convert_fusion.1 = bf16[768,3072]{1,0:T(8,128)(2,1)S(1)} fusion(bf16[1024,768]{1,0:T(8,128)(2,1)} %get-tuple-element.142, bf16[1024,3072]{1,0:T(8,128)(2,1)} %get-tuple-element.143), kind=kOutput, calls=%fused_computation.2 | convolution fusion | flops 4834197504 | bytes 12582912 | tf_op jit(solution)/shard_map/dot_general | solution.py:30
  180.1 1.4 convolution_convert_fusion.4
  181.5 1.8 dynamic-slice_bitcast_fusion
  184.6 3.9 %pad_maximum_fusion = bf16[2,2,96,3968]{3,2,1,0:T(8,128)(2,1)} fusion(bf16[2,2,96,128]{3,2,1,0:T(8,128)(2,1)S(1)} %get-tuple-element.236, bf16[2,2,96,768]{3,2,1,0:T(8,128)(2,1)} %get-tuple-element.219, bf16[2,2,96,3072]{3,2,1,0:T(8,128)(2,1)} %get-tuple-element.213), kind=kLoop, calls=%fused_computation.8 | loop fusion | flops 9142272 | bytes 6094848 | tf_op jit(solution)/shard_map/concatenate | solution.py:102
  189.7 2.2 pad_maximum_fusion.6.refs_0_
  192.0 8.5 %convolution_convert_fusion = bf16[3072,768]{1,0:T(8,128)(2,1)S(1)} fusion(bf16[1024,3072]{1,0:T(8,128)(2,1)} %get-tuple-element.152, bf16[1,1024,768]{2,1,0:T(8,128)(2,1)S(1)} %copy-done.24), kind=kOutput, calls=%fused_computation.1 | convolution fusion | flops 4834197504 | bytes 12582912 | tf_op jit(solution)/shard_map/dot_general | solution.py:30
  200.5 1.8 dynamic-slice_bitcast_fusion.1
  202.2 1.2 copy-done
  206.3 2.4 add_convert_fusion
  208.7 1.2 dynamic-slice_bitcast_fusion.3
  209.9 2.2 fusion
  214.7 15.0 %back.2 = (bf16[1024,1152]{1,0:T(8,128)(2,1)}, bf16[384,128]{1,0:T(8,128)(2,1)}) custom-call(s32[1]{0:T(128)} %bitcast.me_ref, f32[8]{0:T(128)} %bitcast.237, f32[5]{0:T(128)} %copy-done.22, bf16[1024,768]{1,0:T(8,128)(2,1)} %get-tuple-element.156.q_ref, bf16[1024,768]{1,0:T(8,128)(2,1)} %get-tuple-element.157.k_ref, ...), custom_call_target="tpu_custom_call" | custom-call | flops 9500000256 | bytes 19000000 | tf_op jit(solution)/shard_map/back/pallas_call | solution.py:848
  229.7 4.4 %convolution_convert_fusion.3 = bf16[768,1152]{1,0:T(8,128)(2,1)S(1)} fusion(bf16[1024,768]{1,0:T(8,128)(2,1)} %get-tuple-element.112.h_ref, bf16[1024,1152]{1,0:T(8,128)(2,1)} %get-tuple-element.161.refs_0_), kind=kOutput, calls=%fused_computation.7 | convolution fusion | flops 1812824064 | bytes 5701632 | tf_op jit(solution)/shard_map/dot_general | solution.py:30
  234.1 1.4 dynamic-slice_bitcast_fusion.6
  235.5 5.6 %collective-permute-done.31 = bf16[2,384,768]{2,1,0:T(8,128)(2,1)} collective-permute-done((bf16[2,384,768]{2,1,0:T(8,128)(2,1)}, bf16[2,384,768]{2,1,0:T(8,128)(2,1)}, u32[]{:S(2)}, u32[]{:S(2)}) %collective-permute-start.31) | collective-permute-done | bytes 1179680 | tf_op jit(solution)/shard_map/ppermute | solution.py:34
  241.1 1.5 fusion.2
  244.7 14.9 %back.3 = (bf16[1024,1152]{1,0:T(8,128)(2,1)}, bf16[384,128]{1,0:T(8,128)(2,1)}) custom-call(s32[1]{0:T(128)} %bitcast.me_ref, f32[8]{0:T(128)} %bitcast.238, f32[5]{0:T(128)} %copy-done.22, bf16[1024,768]{1,0:T(8,128)(2,1)} %get-tuple-element.156.q_ref, bf16[1024,768]{1,0:T(8,128)(2,1)} %get-tuple-element.157.k_ref, ...), custom_call_target="tpu_custom_call" | custom-call | flops 9500000256 | bytes 19000000 | tf_op jit(solution)/shard_map/back/pallas_call | solution.py:848
  260.6 4.4 %convolution_convert_fusion.2 = bf16[768,1152]{1,0:T(8,128)(2,1)S(1)} fusion(bf16[1024,768]{1,0:T(8,128)(2,1)} %get-tuple-element.112.h_ref, bf16[1024,1152]{1,0:T(8,128)(2,1)} %get-tuple-element.164.refs_1_), kind=kOutput, calls=%fused_computation.6 | convolution fusion | flops 1812824064 | bytes 5701632 | tf_op jit(solution)/shard_map/dot_general | solution.py:30
  266.4 1.5 pad_maximum_fusion.4
  269.0 1.7 fusion.1
  273.4 11.9 %enter.1 = (f32[1024,768]{1,0:T(8,128)}, f32[8,768]{1,0:T(8,128)}) custom-call(s32[1]{0:T(128)} %bitcast.me_ref, bf16[1024,768]{1,0:T(8,128)(2,1)} %bitcast.242, f32[1024,768]{1,0:T(8,128)} %get-tuple-element.170.dr_ref, f32[8,768]{1,0:T(8,128)} %get-tuple-element.102.gb_ref, bf16[1024,1152]{1,0:T(8,128)(2,1)} %get-tuple-element.161.refs_0_, ...), custom_call_target="tpu_custom_call" | custom-call | flops 5500000256 | bytes 11000000 | tf_op jit(solution)/shard_map/enter/pallas_call | solution.py:888
  287.0 2.8 collective-permute-start.49
  290.1 2.2 add_convert_fusion.1
  294.2 1.3 fusion.3
  295.5 4.1 %collective-permute-done.49 = bf16[96,768]{1,0:T(8,128)(2,1)S(1)} collective-permute-done((bf16[96,768]{1,0:T(8,128)(2,1)S(1)}, bf16[96,768]{1,0:T(8,128)(2,1)S(1)}, u32[]{:S(2)}, u32[]{:S(2)}) %collective-permute-start.49) | collective-permute-done | bytes 147488 | tf_op jit(solution)/shard_map/ppermute | solution.py:155
  299.6 3.7 %collective-permute-done.50 = bf16[96,768]{1,0:T(8,128)(2,1)S(1)} collective-permute-done((bf16[96,768]{1,0:T(8,128)(2,1)S(1)}, bf16[96,768]{1,0:T(8,128)(2,1)S(1)}, u32[]{:S(2)}, u32[]{:S(2)}) %collective-permute-start.50) | collective-permute-done | bytes 147488 | tf_op jit(solution)/shard_map/ppermute | solution.py:155
  303.5 1.3 collective-permute-start.47
  305.8 1.3 collective-permute-start.37
  307.6 4.6 %collective-permute-done.37 = bf16[96,1280]{1,0:T(8,128)(2,1)S(1)} collective-permute-done((bf16[96,1280]{1,0:T(8,128)(2,1)S(1)}, bf16[96,1280]{1,0:T(8,128)(2,1)S(1)}, u32[]{:S(2)}, u32[]{:S(2)}) %collective-permute-start.37) | collective-permute-done | bytes 245792 | tf_op jit(solution)/shard_map/ppermute | solution.py:34
  313.4 5.9 %collective-permute-done.46 = bf16[24,3968]{1,0:T(8,128)(2,1)S(1)} collective-permute-done((bf16[24,3968]{1,0:T(8,128)(2,1)S(1)}, bf16[24,3968]{1,0:T(8,128)(2,1)S(1)}, u32[]{:S(2)}, u32[]{:S(2)}) %collective-permute-start.46) | collective-permute-done | bytes 190496 | tf_op jit(solution)/shard_map/ppermute | solution.py:155
  319.4 1.6 collective-permute-done.47
  322.5 1.5 collective-permute-start.42
  324.1 1.4 collective-permute-start.43
  326.9 5.8 %collective-permute-done.42 = bf16[24,2560]{1,0:T(8,128)(2,1)S(1)} collective-permute-done((bf16[24,2560]{1,0:T(8,128)(2,1)S(1)}, bf16[24,2560]{1,0:T(8,128)(2,1)S(1)}, u32[]{:S(2)}, u32[]{:S(2)}) %collective-permute-start.42) | collective-permute-done | bytes 122912 | tf_op jit(solution)/shard_map/ppermute | solution.py:155
  332.8 2.9 collective-permute-done.43
  (231 shorter events, 48.5 us)
Async XLA Ops:
  4.2 17.6 %copy-start.16 = (bf16[24,3072]{1,0:T(8,128)(2,1)S(1)}, bf16[24,3072]{1,0:T(8,128)(2,1)}, u32[]{:S(2)}) copy-start(bf16[24,3072]{1,0:T(8,128)(2,1)} %param.17) | copy-start | bytes 442372
  4.2 17.6 %copy-start.18 = (bf16[24,768]{1,0:T(8,128)(2,1)S(1)}, bf16[24,768]{1,0:T(8,128)(2,1)}, u32[]{:S(2)}) copy-start(bf16[24,768]{1,0:T(8,128)(2,1)} %param.16) | copy-start | bytes 110596
  5.2 6.0 %collective-permute-start = (bf16[24,2560]{1,0:T(8,128)(2,1)S(1)}, bf16[24,2560]{1,0:T(8,128)(2,1)S(1)}, u32[]{:S(2)}, u32[]{:S(2)}) collective-permute-start(bf16[24,2560]{1,0:T(8,128)(2,1)S(1)} %concatenate.58), channel_id=1, source_target_pairs={{0,3},{1,0},{2,1},{3,2},{4,7},{5,4},{6,5},{7,6},{8,11},{9,8},{10,9... | collective-permute-start | bytes 368648 | tf_op jit(solution)/shard_map/ppermute | solution.py:43
  5.3 9.5 %collective-permute-start.1 = (bf16[24,2560]{1,0:T(8,128)(2,1)S(1)}, bf16[24,2560]{1,0:T(8,128)(2,1)S(1)}, u32[]{:S(2)}, u32[]{:S(2)}) collective-permute-start(bf16[24,2560]{1,0:T(8,128)(2,1)S(1)} %concatenate.58), channel_id=1, source_target_pairs={{0,2},{1,3},{2,0},{3,1},{4,6},{5,7},{6,4},{7,5},{8,10},{9,11},{10,... | collective-permute-start | bytes 368648 | tf_op jit(solution)/shard_map/ppermute | solution.py:43
  7.7 10.2 %collective-permute-start.2 = (bf16[24,2560]{1,0:T(8,128)(2,1)S(1)}, bf16[24,2560]{1,0:T(8,128)(2,1)S(1)}, u32[]{:S(2)}, u32[]{:S(2)}) collective-permute-start(bf16[24,2560]{1,0:T(8,128)(2,1)S(1)} %concatenate.58), channel_id=1, source_target_pairs={{0,1},{1,2},{2,3},{3,0},{4,5},{5,6},{6,7},{7,4},{8,9},{9,10},{10,1... | collective-permute-start | bytes 368648 | tf_op jit(solution)/shard_map/ppermute | solution.py:43
  11.2 18.6 %copy-start.22 = (f32[5]{0:T(128)}, f32[5]{0:T(128)S(1)}, u32[]{:S(2)}) copy-start(f32[5]{0:T(128)S(1)} %pad_maximum_fusion.14.cend_ref) | copy-start | bytes 64
  18.1 11.6 %collective-permute-start.4 = (bf16[96,2560]{1,0:T(8,128)(2,1)S(1)}, bf16[96,2560]{1,0:T(8,128)(2,1)S(1)}, u32[]{:S(2)}, u32[]{:S(2)}) collective-permute-start(bf16[96,2560]{1,0:T(8,128)(2,1)S(1)} %constant_dynamic-slice_fusion.3), channel_id=1, source_target_pairs={{0,8},{4,12},{8,0},{12,4},{16,24},{20,28},{24,16},{28,20},{1,9},{5... | collective-permute-start | bytes 1474568 | tf_op jit(solution)/shard_map/ppermute | solution.py:34
  19.4 11.7 %collective-permute-start.5 = (bf16[96,2560]{1,0:T(8,128)(2,1)S(1)}, bf16[96,2560]{1,0:T(8,128)(2,1)S(1)}, u32[]{:S(2)}, u32[]{:S(2)}) collective-permute-start(bf16[96,2560]{1,0:T(8,128)(2,1)S(1)} %constant_dynamic-slice_fusion.3), channel_id=1, source_target_pairs={{0,16},{4,20},{8,24},{12,28},{16,0},{20,4},{24,8},{28,12},{1,17},{... | collective-permute-start | bytes 1474568 | tf_op jit(solution)/shard_map/ppermute | solution.py:34
  20.7 16.1 %copy-start.20 = (f32[1,1,4,256]{3,1,2,0:T(1,128)}, f32[1,1,4,256]{3,1,2,0:T(1,128)S(1)}, u32[]{:S(2)}) copy-start(f32[1,1,4,256]{3,1,2,0:T(1,128)S(1)} %copy.96) | copy-start | bytes 12292
  21.8 19.3 %collective-permute-start.8 = (bf16[24,3840]{1,0:T(8,128)(2,1)S(1)}, bf16[24,3840]{1,0:T(8,128)(2,1)S(1)}, u32[]{:S(2)}, u32[]{:S(2)}) collective-permute-start(bf16[24,3840]{1,0:T(8,128)(2,1)S(1)} %pad_maximum_fusion.9), channel_id=1, source_target_pairs={{0,2},{1,3},{2,0},{3,1},{4,6},{5,7},{6,4},{7,5},{8,10},{9,11},{10,... | collective-permute-start | bytes 552968 | tf_op jit(solution)/shard_map/ppermute | solution.py:43
  22.3 18.7 %collective-permute-start.3 = (bf16[24,3840]{1,0:T(8,128)(2,1)S(1)}, bf16[24,3840]{1,0:T(8,128)(2,1)S(1)}, u32[]{:S(2)}, u32[]{:S(2)}) collective-permute-start(bf16[24,3840]{1,0:T(8,128)(2,1)S(1)} %pad_maximum_fusion.9), channel_id=1, source_target_pairs={{0,3},{1,0},{2,1},{3,2},{4,7},{5,4},{6,5},{7,6},{8,11},{9,8},{10,9... | collective-permute-start | bytes 552968 | tf_op jit(solution)/shard_map/ppermute | solution.py:43
  25.2 15.8 %collective-permute-start.9 = (bf16[24,3840]{1,0:T(8,128)(2,1)S(1)}, bf16[24,3840]{1,0:T(8,128)(2,1)S(1)}, u32[]{:S(2)}, u32[]{:S(2)}) collective-permute-start(bf16[24,3840]{1,0:T(8,128)(2,1)S(1)} %pad_maximum_fusion.9), channel_id=1, source_target_pairs={{0,1},{1,2},{2,3},{3,0},{4,5},{5,6},{6,7},{7,4},{8,9},{9,10},{10,1... | collective-permute-start | bytes 552968 | tf_op jit(solution)/shard_map/ppermute | solution.py:43
  29.7 5.7 %collective-permute-start.6 = (bf16[96,1280]{1,0:T(8,128)(2,1)S(1)}, bf16[96,1280]{1,0:T(8,128)(2,1)S(1)}, u32[]{:S(2)}, u32[]{:S(2)}) collective-permute-start(bf16[96,1280]{1,0:T(8,128)(2,1)S(1)} %slice.127), channel_id=1, source_target_pairs={{0,16},{4,20},{8,24},{12,28},{16,0},{20,4},{24,8},{28,12},{1,17},{... | collective-permute-start | bytes 737288 | tf_op jit(solution)/shard_map/ppermute | solution.py:34
  31.1 5.4 %collective-permute-start.7 = (bf16[96,1280]{1,0:T(8,128)(2,1)S(1)}, bf16[96,1280]{1,0:T(8,128)(2,1)S(1)}, u32[]{:S(2)}, u32[]{:S(2)}) collective-permute-start(bf16[96,1280]{1,0:T(8,128)(2,1)S(1)} %slice.128), channel_id=1, source_target_pairs={{0,8},{4,12},{8,0},{12,4},{16,24},{20,28},{24,16},{28,20},{1,9},{5... | collective-permute-start | bytes 737288 | tf_op jit(solution)/shard_map/ppermute | solution.py:34
  36.8 6.9 %collective-permute-start.10 = (bf16[4,96,2560]{2,1,0:T(8,128)(2,1)S(1)}, bf16[4,96,2560]{2,1,0:T(8,128)(2,1)S(1)}, u32[]{:S(2)}, u32[]{:S(2)}) collective-permute-start(bf16[4,96,2560]{2,1,0:T(8,128)(2,1)S(1)} %pad_maximum_fusion.3.refs_0_.refs_2_), channel_id=1, source_target_pairs={{0,4},{4,0},{8,12},{12,8},{16,20},{20,16},{24,28},{28,24},{1,5},{5... | collective-permute-start | bytes 5898248 | tf_op jit(solution)/shard_map/ppermute | solution.py:34
  41.3 21.0 %collective-permute-start.11 = (bf16[96,3840]{1,0:T(8,128)(2,1)S(1)}, bf16[96,3840]{1,0:T(8,128)(2,1)S(1)}, u32[]{:S(2)}, u32[]{:S(2)}) collective-permute-start(bf16[96,3840]{1,0:T(8,128)(2,1)S(1)} %constant_dynamic-slice_fusion.2), channel_id=1, source_target_pairs={{0,8},{4,12},{8,0},{12,4},{16,24},{20,28},{24,16},{28,20},{1,9},{5... | collective-permute-start | bytes 2211848 | tf_op jit(solution)/shard_map/ppermute | solution.py:34
  41.6 34.2 %collective-permute-start.12 = (bf16[96,3840]{1,0:T(8,128)(2,1)S(1)}, bf16[96,3840]{1,0:T(8,128)(2,1)S(1)}, u32[]{:S(2)}, u32[]{:S(2)}) collective-permute-start(bf16[96,3840]{1,0:T(8,128)(2,1)S(1)} %constant_dynamic-slice_fusion.2), channel_id=1, source_target_pairs={{0,16},{4,20},{8,24},{12,28},{16,0},{20,4},{24,8},{28,12},{1,17},{... | collective-permute-start | bytes 2211848 | tf_op jit(solution)/shard_map/ppermute | solution.py:34
  43.7 19.6 %collective-permute-start.16 = (bf16[96,768]{1,0:T(8,128)(2,1)S(1)}, bf16[96,768]{1,0:T(8,128)(2,1)S(1)}, u32[]{:S(2)}, u32[]{:S(2)}) collective-permute-start(bf16[96,768]{1,0:T(8,128)(2,1)S(1)} %copy-done.10), channel_id=1, source_target_pairs={{0,1},{1,2},{2,3},{3,0},{4,5},{5,6},{6,7},{7,4},{8,9},{9,10},{10,1... | collective-permute-start | bytes 442376 | tf_op jit(solution)/shard_map/ppermute | solution.py:43
  45.9 18.0 %collective-permute-start.15 = (bf16[96,768]{1,0:T(8,128)(2,1)S(1)}, bf16[96,768]{1,0:T(8,128)(2,1)S(1)}, u32[]{:S(2)}, u32[]{:S(2)}) collective-permute-start(bf16[96,768]{1,0:T(8,128)(2,1)S(1)} %copy-done.10), channel_id=1, source_target_pairs={{0,2},{1,3},{2,0},{3,1},{4,6},{5,7},{6,4},{7,5},{8,10},{9,11},{10,... | collective-permute-start | bytes 442376 | tf_op jit(solution)/shard_map/ppermute | solution.py:43
  47.0 16.8 %collective-permute-start.14 = (bf16[96,768]{1,0:T(8,128)(2,1)S(1)}, bf16[96,768]{1,0:T(8,128)(2,1)S(1)}, u32[]{:S(2)}, u32[]{:S(2)}) collective-permute-start(bf16[96,768]{1,0:T(8,128)(2,1)S(1)} %copy-done.10), channel_id=1, source_target_pairs={{0,3},{1,0},{2,1},{3,2},{4,7},{5,4},{6,5},{7,6},{8,11},{9,8},{10,9... | collective-permute-start | bytes 442376 | tf_op jit(solution)/shard_map/ppermute | solution.py:43
  62.3 13.5 %copy-start.8 = (bf16[96,3840]{1,0:T(8,128)(2,1)}, bf16[96,3840]{1,0:T(8,128)(2,1)S(1)}, u32[]{:S(2)}) copy-start(bf16[96,3840]{1,0:T(8,128)(2,1)S(1)} %collective-permute-done.11) | copy-start | bytes 2211844
  62.3 17.2 %collective-permute-start.13 = (bf16[96,3840]{1,0:T(8,128)(2,1)S(1)}, bf16[96,3840]{1,0:T(8,128)(2,1)S(1)}, u32[]{:S(2)}, u32[]{:S(2)}) collective-permute-start(bf16[96,3840]{1,0:T(8,128)(2,1)S(1)} %collective-permute-done.11), channel_id=1, source_target_pairs={{0,16},{4,20},{8,24},{12,28},{16,0},{20,4},{24,8},{28,12},{1,17},{... | collective-permute-start | bytes 2211848 | tf_op jit(solution)/shard_map/ppermute | solution.py:34
  63.3 18.9 %collective-permute-start.19 = (bf16[7,128,128]{2,1,0:T(8,128)(2,1)}, bf16[7,128,128]{2,1,0:T(8,128)(2,1)}, u32[]{:S(2)}, u32[]{:S(2)}) collective-permute-start(bf16[7,128,128]{2,1,0:T(8,128)(2,1)} %get-tuple-element.136), channel_id=1, source_target_pairs={{0,8},{4,12},{8,0},{12,4},{16,24},{20,28},{24,16},{28,20},{1,9},{5... | collective-permute-start | bytes 688136 | tf_op jit(solution)/shard_map/ppermute | solution.py:34
  64.0 37.9 %collective-permute-start.17 = (bf16[384,768]{1,0:T(8,128)(2,1)S(1)}, bf16[384,768]{1,0:T(8,128)(2,1)S(1)}, u32[]{:S(2)}, u32[]{:S(2)}) collective-permute-start(bf16[384,768]{1,0:T(8,128)(2,1)S(1)} %constant_dynamic-slice_fusion), channel_id=1, source_target_pairs={{0,8},{4,12},{8,0},{12,4},{16,24},{20,28},{24,16},{28,20},{1,9},{5... | collective-permute-start | bytes 1769480 | tf_op jit(solution)/shard_map/ppermute | solution.py:34
  65.1 36.9 %collective-permute-start.18 = (bf16[384,768]{1,0:T(8,128)(2,1)S(1)}, bf16[384,768]{1,0:T(8,128)(2,1)S(1)}, u32[]{:S(2)}, u32[]{:S(2)}) collective-permute-start(bf16[384,768]{1,0:T(8,128)(2,1)S(1)} %constant_dynamic-slice_fusion), channel_id=1, source_target_pairs={{0,16},{4,20},{8,24},{12,28},{16,0},{20,4},{24,8},{28,12},{1,17},{... | collective-permute-start | bytes 1769480 | tf_op jit(solution)/shard_map/ppermute | solution.py:34
  75.8 4.8 %copy-start.9 = (bf16[96,3840]{1,0:T(8,128)(2,1)}, bf16[96,3840]{1,0:T(8,128)(2,1)S(1)}, u32[]{:S(2)}) copy-start(bf16[96,3840]{1,0:T(8,128)(2,1)S(1)} %collective-permute-done.12) | copy-start | bytes 2211844
  75.9 26.1 %collective-permute-start.20 = (bf16[7,128,128]{2,1,0:T(8,128)(2,1)}, bf16[7,128,128]{2,1,0:T(8,128)(2,1)S(1)}, u32[]{:S(2)}, u32[]{:S(2)}) collective-permute-start(bf16[7,128,128]{2,1,0:T(8,128)(2,1)} %get-tuple-element.136), channel_id=1, source_target_pairs={{0,16},{4,20},{8,24},{12,28},{16,0},{20,4},{24,8},{28,12},{1,17},{... | collective-permute-start | bytes 688136 | tf_op jit(solution)/shard_map/ppermute | solution.py:34
  79.5 22.5 %collective-permute-start.21 = (bf16[7,128,128]{2,1,0:T(8,128)(2,1)}, bf16[7,128,128]{2,1,0:T(8,128)(2,1)S(1)}, u32[]{:S(2)}, u32[]{:S(2)}) collective-permute-start(bf16[7,128,128]{2,1,0:T(8,128)(2,1)} %get-tuple-element.136), channel_id=1, source_target_pairs={{0,24},{4,28},{8,16},{12,20},{16,8},{20,12},{24,0},{28,4},{1,25},{... | collective-permute-start | bytes 688136 | tf_op jit(solution)/shard_map/ppermute | solution.py:34
  82.2 32.4 %copy-start.6 = (bf16[4,96,3840]{2,1,0:T(8,128)(2,1)}, bf16[4,96,3840]{2,1,0:T(8,128)(2,1)S(1)}, u32[]{:S(2)}) copy-start(bf16[4,96,3840]{2,1,0:T(8,128)(2,1)S(1)} %pad_maximum_fusion.1.refs_0_) | copy-start | bytes 8847364
  82.2 43.8 %collective-permute-start.22 = (bf16[4,96,3840]{2,1,0:T(8,128)(2,1)S(1)}, bf16[4,96,3840]{2,1,0:T(8,128)(2,1)}, u32[]{:S(2)}, u32[]{:S(2)}) collective-permute-start(bf16[4,96,3840]{2,1,0:T(8,128)(2,1)S(1)} %pad_maximum_fusion.1.refs_0_), channel_id=1, source_target_pairs={{0,4},{4,0},{8,12},{12,8},{16,20},{20,16},{24,28},{28,24},{1,5},{5... | collective-permute-start | bytes 8847368 | tf_op jit(solution)/shard_map/ppermute | solution.py:34
  102.7 13.1 %collective-permute-start.23 = (bf16[384,768]{1,0:T(8,128)(2,1)S(1)}, bf16[384,768]{1,0:T(8,128)(2,1)S(1)}, u32[]{:S(2)}, u32[]{:S(2)}) collective-permute-start(bf16[384,768]{1,0:T(8,128)(2,1)S(1)} %collective-permute-done.18), channel_id=1, source_target_pairs={{0,8},{4,12},{8,0},{12,4},{16,24},{20,28},{24,16},{28,20},{1,9},{5... | collective-permute-start | bytes 1769480 | tf_op jit(solution)/shard_map/ppermute | solution.py:34
  117.5 8.5 %collective-permute-start.24 = (bf16[4,384,768]{2,1,0:T(8,128)(2,1)}, bf16[4,384,768]{2,1,0:T(8,128)(2,1)}, u32[]{:S(2)}, u32[]{:S(2)}) collective-permute-start(bf16[4,384,768]{2,1,0:T(8,128)(2,1)} %pad_maximum_fusion.2.refs_2_), channel_id=1, source_target_pairs={{0,4},{4,0},{8,12},{12,8},{16,20},{20,16},{24,28},{28,24},{1,5},{5... | collective-permute-start | bytes 7077896 | tf_op jit(solution)/shard_map/ppermute | solution.py:34
  122.3 3.7 %collective-permute-start.25 = (bf16[4,7,128,128]{3,2,1,0:T(8,128)(2,1)}, bf16[4,7,128,128]{3,2,1,0:T(8,128)(2,1)}, u32[]{:S(2)}, u32[]{:S(2)}) collective-permute-start(bf16[4,7,128,128]{3,2,1,0:T(8,128)(2,1)} %pad_maximum_fusion.5.refs_4_), channel_id=1, source_target_pairs={{0,4},{4,0},{8,12},{12,8},{16,20},{20,16},{24,28},{28,24},{1,5},{5... | collective-permute-start | bytes 2752520 | tf_op jit(solution)/shard_map/ppermute | solution.py:34
  169.1 20.7 %collective-permute-start.26 = (bf16[7,128,128]{2,1,0:T(8,128)(2,1)}, bf16[7,128,128]{2,1,0:T(8,128)(2,1)}, u32[]{:S(2)}, u32[]{:S(2)}) collective-permute-start(bf16[7,128,128]{2,1,0:T(8,128)(2,1)} %get-tuple-element.148), channel_id=1, source_target_pairs={{0,8},{4,12},{8,0},{12,4},{16,24},{20,28},{24,16},{28,20},{1,9},{5... | collective-permute-start | bytes 688136 | tf_op jit(solution)/shard_map/ppermute | solution.py:34
  170.3 19.4 %collective-permute-start.27 = (bf16[7,128,128]{2,1,0:T(8,128)(2,1)}, bf16[7,128,128]{2,1,0:T(8,128)(2,1)}, u32[]{:S(2)}, u32[]{:S(2)}) collective-permute-start(bf16[7,128,128]{2,1,0:T(8,128)(2,1)} %get-tuple-element.148), channel_id=1, source_target_pairs={{0,16},{4,20},{8,24},{12,28},{16,0},{20,4},{24,8},{28,12},{1,17},{... | collective-permute-start | bytes 688136 | tf_op jit(solution)/shard_map/ppermute | solution.py:34
  170.6 19.1 %collective-permute-start.28 = (bf16[7,128,128]{2,1,0:T(8,128)(2,1)}, bf16[7,128,128]{2,1,0:T(8,128)(2,1)}, u32[]{:S(2)}, u32[]{:S(2)}) collective-permute-start(bf16[7,128,128]{2,1,0:T(8,128)(2,1)} %get-tuple-element.148), channel_id=1, source_target_pairs={{0,24},{4,28},{8,16},{12,20},{16,8},{20,12},{24,0},{28,4},{1,25},{... | collective-permute-start | bytes 688136 | tf_op jit(solution)/shard_map/ppermute | solution.py:34
  171.8 8.3 %copy-start.25 = (bf16[1024,768]{1,0:T(8,128)(2,1)S(1)}, bf16[1024,768]{1,0:T(8,128)(2,1)}, u32[]{:S(2)}) copy-start(bf16[1024,768]{1,0:T(8,128)(2,1)} %get-tuple-element.144) | copy-start | bytes 4718596
  171.8 8.3 %copy-start.26 = (bf16[1024,768]{1,0:T(8,128)(2,1)S(1)}, bf16[1024,768]{1,0:T(8,128)(2,1)}, u32[]{:S(2)}) copy-start(bf16[1024,768]{1,0:T(8,128)(2,1)} %get-tuple-element.145) | copy-start | bytes 4718596
  184.6 5.1 %copy-start.11 = (bf16[7,128,128]{2,1,0:T(8,128)(2,1)S(1)}, bf16[7,128,128]{2,1,0:T(8,128)(2,1)}, u32[]{:S(2)}) copy-start(bf16[7,128,128]{2,1,0:T(8,128)(2,1)} %get-tuple-element.148) | copy-start | bytes 688132
  184.6 7.4 %copy-start.24 = (bf16[1,1024,768]{2,1,0:T(8,128)(2,1)S(1)}, bf16[1,1024,768]{2,1,0:T(8,128)(2,1)}, u32[]{:S(2)}) copy-start(bf16[1,1024,768]{2,1,0:T(8,128)(2,1)} %param.19) | copy-start | bytes 4718596
  188.5 17.8 %collective-permute-start.30 = (bf16[2,2,96,3968]{3,2,1,0:T(8,128)(2,1)}, bf16[2,2,96,3968]{3,2,1,0:T(8,128)(2,1)}, u32[]{:S(2)}, u32[]{:S(2)}) collective-permute-start(bf16[2,2,96,3968]{3,2,1,0:T(8,128)(2,1)} %pad_maximum_fusion), channel_id=1, source_target_pairs={{0,4},{4,0},{8,12},{12,8},{16,20},{20,16},{24,28},{28,24},{1,5},{5... | collective-permute-start | bytes 9142280 | tf_op jit(solution)/shard_map/ppermute | solution.py:34
  191.9 12.9 %collective-permute-start.32 = (bf16[4,7,128,128]{3,2,1,0:T(8,128)(2,1)}, bf16[4,7,128,128]{3,2,1,0:T(8,128)(2,1)}, u32[]{:S(2)}, u32[]{:S(2)}) collective-permute-start(bf16[4,7,128,128]{3,2,1,0:T(8,128)(2,1)} %pad_maximum_fusion.6.refs_0_), channel_id=1, source_target_pairs={{0,4},{4,0},{8,12},{12,8},{16,20},{20,16},{24,28},{28,24},{1,5},{5... | collective-permute-start | bytes 2752520 | tf_op jit(solution)/shard_map/ppermute | solution.py:34
  203.5 6.4 %collective-permute-start.29 = (bf16[2,2,384,768]{3,2,1,0:T(8,128)(2,1)}, bf16[2,2,384,768]{3,2,1,0:T(8,128)(2,1)}, u32[]{:S(2)}, u32[]{:S(2)}) collective-permute-start(bf16[2,2,384,768]{3,2,1,0:T(8,128)(2,1)} %dynamic-slice_bitcast_fusion.1), channel_id=1, source_target_pairs={{0,4},{4,0},{8,12},{12,8},{16,20},{20,16},{24,28},{28,24},{1,5},{5... | collective-permute-start | bytes 7077896 | tf_op jit(solution)/shard_map/ppermute | solution.py:34
  213.3 27.8 %collective-permute-start.31 = (bf16[2,384,768]{2,1,0:T(8,128)(2,1)}, bf16[2,384,768]{2,1,0:T(8,128)(2,1)}, u32[]{:S(2)}, u32[]{:S(2)}) collective-permute-start(bf16[2,384,768]{2,1,0:T(8,128)(2,1)} %dynamic-slice_bitcast_fusion.4), channel_id=1, source_target_pairs={{0,8},{4,12},{8,0},{12,4},{16,24},{20,28},{24,16},{28,20},{1,9},{5... | collective-permute-start | bytes 3538952 | tf_op jit(solution)/shard_map/ppermute | solution.py:34
  214.5 54.5 %collective-permute-start.34 = (bf16[2,96,3968]{2,1,0:T(8,128)(2,1)}, bf16[2,96,3968]{2,1,0:T(8,128)(2,1)}, u32[]{:S(2)}, u32[]{:S(2)}) collective-permute-start(bf16[2,96,3968]{2,1,0:T(8,128)(2,1)} %dynamic-slice_bitcast_fusion.3), channel_id=1, source_target_pairs={{0,16},{4,20},{8,24},{12,28},{16,0},{20,4},{24,8},{28,12},{1,17},{... | collective-permute-start | bytes 4571144 | tf_op jit(solution)/shard_map/ppermute | solution.py:34
  243.7 15.9 %copy-start.17 = (bf16[384,128]{1,0:T(8,128)(2,1)S(1)}, bf16[384,128]{1,0:T(8,128)(2,1)}, u32[]{:S(2)}) copy-start(bf16[384,128]{1,0:T(8,128)(2,1)} %get-tuple-element.165) | copy-start | bytes 294916
  243.7 28.4 %collective-permute-start.33 = (bf16[384,768]{1,0:T(8,128)(2,1)S(1)}, bf16[384,768]{1,0:T(8,128)(2,1)}, u32[]{:S(2)}, u32[]{:S(2)}) collective-permute-start(bf16[384,768]{1,0:T(8,128)(2,1)S(1)} %dynamic-slice_bitcast_fusion.10), channel_id=1, source_target_pairs={{0,16},{4,20},{8,24},{12,28},{16,0},{20,4},{24,8},{28,12},{1,17},{... | collective-permute-start | bytes 1769480 | tf_op jit(solution)/shard_map/ppermute | solution.py:34
  267.8 22.0 %collective-permute-start.35 = (bf16[2,2,96,2432]{3,2,1,0:T(8,128)(2,1)}, bf16[2,2,96,2432]{3,2,1,0:T(8,128)(2,1)}, u32[]{:S(2)}, u32[]{:S(2)}) collective-permute-start(bf16[2,2,96,2432]{3,2,1,0:T(8,128)(2,1)} %pad_maximum_fusion.4), channel_id=1, source_target_pairs={{0,4},{4,0},{8,12},{12,8},{16,20},{20,16},{24,28},{28,24},{1,5},{5... | collective-permute-start | bytes 5603336 | tf_op jit(solution)/shard_map/ppermute | solution.py:34
  271.6 21.9 %collective-permute-start.44 = (bf16[96,3968]{1,0:T(8,128)(2,1)}, bf16[96,3968]{1,0:T(8,128)(2,1)}, u32[]{:S(2)}, u32[]{:S(2)}) collective-permute-start(bf16[96,3968]{1,0:T(8,128)(2,1)} %dynamic-slice_bitcast_fusion.9), channel_id=1, source_target_pairs={{0,8},{4,12},{8,0},{12,4},{16,24},{20,28},{24,16},{28,20},{1,9},{5... | collective-permute-start | bytes 2285576 | tf_op jit(solution)/shard_map/ppermute | solution.py:34
  285.3 4.7 %copy-start.5 = (bf16[2,2,96,1152]{3,2,1,0:T(8,128)(2,1)S(1)}, bf16[2,2,96,1152]{3,2,1,0:T(8,128)(2,1)}, u32[]{:S(2)}) copy-start(bf16[2,2,96,1152]{3,2,1,0:T(8,128)(2,1)} %get-tuple-element.214) | copy-start | bytes 2654212
  286.5 6.0 %collective-permute-start.38 = (bf16[2,2,96,128]{3,2,1,0:T(8,128)(2,1)S(1)}, bf16[2,2,96,128]{3,2,1,0:T(8,128)(2,1)S(1)}, u32[]{:S(2)}, u32[]{:S(2)}) collective-permute-start(bf16[2,2,96,128]{3,2,1,0:T(8,128)(2,1)S(1)} %dynamic-slice_bitcast_fusion.25), channel_id=1, source_target_pairs={{0,4},{4,0},{8,12},{12,8},{16,20},{20,16},{24,28},{28,24},{1,5},{5... | collective-permute-start | bytes 294920 | tf_op jit(solution)/shard_map/ppermute | solution.py:34
  286.9 8.5 %collective-permute-start.48 = (bf16[96,768]{1,0:T(8,128)(2,1)S(1)}, bf16[96,768]{1,0:T(8,128)(2,1)S(1)}, u32[]{:S(2)}, u32[]{:S(2)}) collective-permute-start(bf16[96,768]{1,0:T(8,128)(2,1)S(1)} %get-tuple-element.223), channel_id=1, source_target_pairs={{0,1},{1,2},{2,3},{3,0},{4,5},{5,6},{6,7},{7,4},{8,9},{9,10},{10,1... | collective-permute-start | bytes 442376 | tf_op jit(solution)/shard_map/ppermute | solution.py:155
  287.0 12.6 %collective-permute-start.49 = (bf16[96,768]{1,0:T(8,128)(2,1)S(1)}, bf16[96,768]{1,0:T(8,128)(2,1)S(1)}, u32[]{:S(2)}, u32[]{:S(2)}) collective-permute-start(bf16[96,768]{1,0:T(8,128)(2,1)S(1)} %get-tuple-element.225), channel_id=1, source_target_pairs={{0,2},{1,3},{2,0},{3,1},{4,6},{5,7},{6,4},{7,5},{8,10},{9,11},{10,... | collective-permute-start | bytes 442376 | tf_op jit(solution)/shard_map/ppermute | solution.py:155
  289.8 13.4 %collective-permute-start.50 = (bf16[96,768]{1,0:T(8,128)(2,1)S(1)}, bf16[96,768]{1,0:T(8,128)(2,1)S(1)}, u32[]{:S(2)}, u32[]{:S(2)}) collective-permute-start(bf16[96,768]{1,0:T(8,128)(2,1)S(1)} %get-tuple-element.224), channel_id=1, source_target_pairs={{0,3},{1,0},{2,1},{3,2},{4,7},{5,4},{6,5},{7,6},{8,11},{9,8},{10,9... | collective-permute-start | bytes 442376 | tf_op jit(solution)/shard_map/ppermute | solution.py:155
  292.4 13.2 %collective-permute-start.36 = (bf16[2,96,1280]{2,1,0:T(8,128)(2,1)S(1)}, bf16[2,96,1280]{2,1,0:T(8,128)(2,1)S(1)}, u32[]{:S(2)}, u32[]{:S(2)}) collective-permute-start(bf16[2,96,1280]{2,1,0:T(8,128)(2,1)S(1)} %dynamic-slice_bitcast_fusion.13), channel_id=1, source_target_pairs={{0,8},{4,12},{8,0},{12,4},{16,24},{20,28},{24,16},{28,20},{1,9},{5... | collective-permute-start | bytes 1474568 | tf_op jit(solution)/shard_map/ppermute | solution.py:34
  293.5 13.5 %collective-permute-start.39 = (bf16[2,96,1280]{2,1,0:T(8,128)(2,1)S(1)}, bf16[2,96,1280]{2,1,0:T(8,128)(2,1)S(1)}, u32[]{:S(2)}, u32[]{:S(2)}) collective-permute-start(bf16[2,96,1280]{2,1,0:T(8,128)(2,1)S(1)} %fusion.8), channel_id=1, source_target_pairs={{0,16},{4,20},{8,24},{12,28},{16,0},{20,4},{24,8},{28,12},{1,17},{... | collective-permute-start | bytes 1474568 | tf_op jit(solution)/shard_map/ppermute | solution.py:34
  303.3 10.1 %collective-permute-start.45 = (bf16[24,3968]{1,0:T(8,128)(2,1)S(1)}, bf16[24,3968]{1,0:T(8,128)(2,1)S(1)}, u32[]{:S(2)}, u32[]{:S(2)}) collective-permute-start(bf16[24,3968]{1,0:T(8,128)(2,1)S(1)} %get-tuple-element.220), channel_id=1, source_target_pairs={{0,1},{1,2},{2,3},{3,0},{4,5},{5,6},{6,7},{7,4},{8,9},{9,10},{10,1... | collective-permute-start | bytes 571400 | tf_op jit(solution)/shard_map/ppermute | solution.py:155
  303.4 16.0 %collective-permute-start.46 = (bf16[24,3968]{1,0:T(8,128)(2,1)S(1)}, bf16[24,3968]{1,0:T(8,128)(2,1)S(1)}, u32[]{:S(2)}, u32[]{:S(2)}) collective-permute-start(bf16[24,3968]{1,0:T(8,128)(2,1)S(1)} %get-tuple-element.222), channel_id=1, source_target_pairs={{0,2},{1,3},{2,0},{3,1},{4,6},{5,7},{6,4},{7,5},{8,10},{9,11},{10,... | collective-permute-start | bytes 571400 | tf_op jit(solution)/shard_map/ppermute | solution.py:155
  303.5 17.5 %collective-permute-start.47 = (bf16[24,3968]{1,0:T(8,128)(2,1)S(1)}, bf16[24,3968]{1,0:T(8,128)(2,1)S(1)}, u32[]{:S(2)}, u32[]{:S(2)}) collective-permute-start(bf16[24,3968]{1,0:T(8,128)(2,1)S(1)} %get-tuple-element.221), channel_id=1, source_target_pairs={{0,3},{1,0},{2,1},{3,2},{4,7},{5,4},{6,5},{7,6},{8,11},{9,8},{10,9... | collective-permute-start | bytes 571400 | tf_op jit(solution)/shard_map/ppermute | solution.py:155
  305.8 6.3 %collective-permute-start.37 = (bf16[96,1280]{1,0:T(8,128)(2,1)S(1)}, bf16[96,1280]{1,0:T(8,128)(2,1)S(1)}, u32[]{:S(2)}, u32[]{:S(2)}) collective-permute-start(bf16[96,1280]{1,0:T(8,128)(2,1)S(1)} %dynamic-slice_bitcast_fusion.15), channel_id=1, source_target_pairs={{0,16},{4,20},{8,24},{12,28},{16,0},{20,4},{24,8},{28,12},{1,17},{... | collective-permute-start | bytes 737288 | tf_op jit(solution)/shard_map/ppermute | solution.py:34
  307.3 6.0 %collective-permute-start.40 = (bf16[96,1280]{1,0:T(8,128)(2,1)S(1)}, bf16[96,1280]{1,0:T(8,128)(2,1)S(1)}, u32[]{:S(2)}, u32[]{:S(2)}) collective-permute-start(bf16[96,1280]{1,0:T(8,128)(2,1)S(1)} %dynamic-slice_bitcast_fusion.14), channel_id=1, source_target_pairs={{0,8},{4,12},{8,0},{12,4},{16,24},{20,28},{24,16},{28,20},{1,9},{5... | collective-permute-start | bytes 737288 | tf_op jit(solution)/shard_map/ppermute | solution.py:34
  322.5 4.4 %collective-permute-start.41 = (bf16[24,2560]{1,0:T(8,128)(2,1)S(1)}, bf16[24,2560]{1,0:T(8,128)(2,1)S(1)}, u32[]{:S(2)}, u32[]{:S(2)}) collective-permute-start(bf16[24,2560]{1,0:T(8,128)(2,1)S(1)} %get-tuple-element.226), channel_id=1, source_target_pairs={{0,1},{1,2},{2,3},{3,0},{4,5},{5,6},{6,7},{7,4},{8,9},{9,10},{10,1... | collective-permute-start | bytes 368648 | tf_op jit(solution)/shard_map/ppermute | solution.py:155
  322.5 10.2 %collective-permute-start.42 = (bf16[24,2560]{1,0:T(8,128)(2,1)S(1)}, bf16[24,2560]{1,0:T(8,128)(2,1)S(1)}, u32[]{:S(2)}, u32[]{:S(2)}) collective-permute-start(bf16[24,2560]{1,0:T(8,128)(2,1)S(1)} %get-tuple-element.228), channel_id=1, source_target_pairs={{0,2},{1,3},{2,0},{3,1},{4,6},{5,7},{6,4},{7,5},{8,10},{9,11},{10,... | collective-permute-start | bytes 368648 | tf_op jit(solution)/shard_map/ppermute | solution.py:155
  324.1 11.6 %collective-permute-start.43 = (bf16[24,2560]{1,0:T(8,128)(2,1)S(1)}, bf16[24,2560]{1,0:T(8,128)(2,1)S(1)}, u32[]{:S(2)}, u32[]{:S(2)}) collective-permute-start(bf16[24,2560]{1,0:T(8,128)(2,1)S(1)} %get-tuple-element.227), channel_id=1, source_target_pairs={{0,3},{1,0},{2,1},{3,2},{4,7},{5,4},{6,5},{7,6},{8,11},{9,8},{10,9... | collective-permute-start | bytes 368648 | tf_op jit(solution)/shard_map/ppermute | solution.py:155
  (14 other events, 35.9 us)
where the time goes:
time: 341 us; the launch traced here: 337 us
  Pallas kernels  120 us (35%)
  waiting for transfers between devices  77 us (23%)
  starting transfers between devices  54.4 us (16%)
  other arithmetic  34.2 us (10%)
  matrix products  27.2 us (8%)
  local copies, waits for them, and re-layouts  22.6 us (7%)
    ppermute x33, waiting for transfers between devices, xor_send(): return lax.ppermute(arr, 'seq', [(i, i ^ mask) for i in range(size)])  43.9 us
    pallas_call x1, Pallas kernels, shards(): pl.pallas_call(functools.partial(middle_body, n_seq, pairs), name='middle...  43.1 us
    ppermute x33, starting transfers between devices, xor_send(): return lax.ppermute(arr, 'seq', [(i, i ^ mask) for i in range(size)])  33.8 us
    pallas_call x2, Pallas kernels, shards(): pl.pallas_call(functools.partial(back_body, g * some, some, pairs), name=...  29.9 us
    dot_general x5, matrix products, mm_f(): lax.dot_general(a, b, (((0,), (0,)), ((), ())), preferred_element_type=f32)  27 us
    ppermute x9, waiting for transfers between devices, send_stream(): lax.ppermute(piece, 'stream', [(i, (i + d) % depth) for i in range(depth)])  25.4 us
    pallas_call x2, Pallas kernels, shards(): pl.pallas_call(functools.partial(local_body, base, pairs), name='local',...  20.9 us
    pallas_call x1, Pallas kernels, shards(): pl.pallas_call(functools.partial(keys_body, n_seq, pairs), name='keys', c...  13.7 us
  transfers between devices with their start and end apart: 51, of which 21 were waited for; matrix products, arithmetic and copies ran while one was open for 21% of the time, Pallas kernels for 23%

commit v1 on v0

--- a/solution.py
+++ b/solution.py
@@ -81,14 +81,17 @@
                     self.found[r ^ bit] = xor_send(after(src, *deps) if deps else src, self.size, bit)
         return self
 
-    def far_halves(self):
+    def far_halves(self, *deps):
         one, two = self.bits[:2]
-        half = self.block.shape[1] // 2
-        self.cuts = [self.found[one][:, :half], self.found[two][:, half:]]
+        half = self.block.shape[1] // 256 * 128
+        srcs = (self.found[one], self.found[two])
+        if deps:
+            srcs = lax.optimization_barrier(srcs + deps)[:2]
+        self.cuts = [srcs[0][:, :half], srcs[1][:, half:]]
         left = xor_send(self.cuts[0], self.size, two)
         right = xor_send(self.cuts[1], self.size, one)
         self.found[one ^ two] = jnp.concatenate([left, right], axis=1)
-        return self.far()
+        return self.far(*deps)
 
     def cores(self, *deps):
         parts = [self.found[2 * r] for r in range(self.size // 2)]
@@ -725,7 +728,7 @@
     flags = gb[4].reshape(n_seq, depth, rows)[:, :, 0]
     keeps = lax.dynamic_index_in_dim(flags, level, 1, False)
     spread = Spread(state, n_seq, False).near_all()
-    up.far(gb)
+    up.far_halves(gb)
     proj = Spread(stream_rows([after(a, gb) for a in proj_pieces], depth), n_seq, False).near()
     part_blk = nblk // 2
     local = []

time: 341 us -> 335 us (0.982)
  waiting for transfers between devices: 77 us -> 71.5 us
    ppermute x33 -> x34, waiting for transfers between devices: 43.9 us -> 37.8 us  [xor_send(): return lax.ppermute(arr, 'seq', [(i, i ^ mask) for i in range(size)])]
    unnamed x87 -> x85, local copies, waits for them, and re-layouts: 7.19 us -> 6.52 us
    ppermute x33 -> x34, starting transfers between devices: 33.8 us -> 33.1 us  [xor_send(): return lax.ppermute(arr, 'seq', [(i, i ^ mask) for i in range(size)])]
  transfers between devices with their start and end apart: 51 -> 52, of which waited for: 21 -> 22; matrix products, arithmetic and copies ran while one was open for 21% -> 21% of each run, Pallas kernels for 23% -> 23%
where the time goes in v1:
time: 335 us; the launch traced here: 331 us
  Pallas kernels  120 us (36%)
  waiting for transfers between devices  71.5 us (21%)
  starting transfers between devices  53.7 us (16%)
  other arithmetic  34.3 us (10%)
  matrix products  27.2 us (8%)
  local copies, waits for them, and re-layouts  22 us (7%)
    pallas_call x1, Pallas kernels, shards(): pl.pallas_call(functools.partial(middle_body, n_seq, pairs), name='middle...  43.1 us
    ppermute x34, waiting for transfers between devices, xor_send(): return lax.ppermute(arr, 'seq', [(i, i ^ mask) for i in range(size)])  37.8 us
    ppermute x34, starting transfers between devices, xor_send(): return lax.ppermute(arr, 'seq', [(i, i ^ mask) for i in range(size)])  33.1 us
    pallas_call x2, Pallas kernels, shards(): pl.pallas_call(functools.partial(back_body, g * some, some, pairs), name=...  29.9 us
    dot_general x5, matrix products, mm_f(): lax.dot_general(a, b, (((0,), (0,)), ((), ())), preferred_element_type=f32)  27 us
    ppermute x9, waiting for transfers between devices, send_stream(): lax.ppermute(piece, 'stream', [(i, (i + d) % depth) for i in range(depth)])  26 us
    pallas_call x2, Pallas kernels, shards(): pl.pallas_call(functools.partial(local_body, base, pairs), name='local',...  21 us
    pallas_call x1, Pallas kernels, shards(): pl.pallas_call(functools.partial(keys_body, n_seq, pairs), name='keys', c...  13.7 us
  transfers between devices with their start and end apart: 52, of which 22 were waited for; matrix products, arithmetic and copies ran while one was open for 21% of the time, Pallas kernels for 23%

profile of v1, /device:TPU:9, one launch (start us, length us, event | category | flops | bytes accessed | tf_op | source)
XLA Modules:
  0.0 330.8 jit_solution(627314670792324302)
XLA Ops:
  2.1 1.3 reduce_max.9
  5.3 2.5 collective-permute-start.1
  7.7 2.2 collective-permute-start.2
  11.2 3.5 %collective-permute-done.1 = bf16[24,2560]{1,0:T(8,128)(2,1)S(1)} collective-permute-done((bf16[24,2560]{1,0:T(8,128)(2,1)S(1)}, bf16[24,2560]{1,0:T(8,128)(2,1)S(1)}, u32[]{:S(2)}, u32[]{:S(2)}) %collective-permute-start.1) | collective-permute-done | bytes 122912 | tf_op jit(solution)/shard_map/ppermute | solution.py:43
  14.8 3.2 collective-permute-done.2
  18.1 1.3 collective-permute-start.4
  22.3 2.9 collective-permute-start.3
  25.2 4.5 %collective-permute-done.4 = bf16[96,2560]{1,0:T(8,128)(2,1)S(1)} collective-permute-done((bf16[96,2560]{1,0:T(8,128)(2,1)S(1)}, bf16[96,2560]{1,0:T(8,128)(2,1)S(1)}, u32[]{:S(2)}, u32[]{:S(2)}) %collective-permute-start.4) | collective-permute-done | bytes 491552 | tf_op jit(solution)/shard_map/ppermute | solution.py:34
  29.7 1.3 collective-permute-start.6
  31.1 1.3 collective-permute-start.7
  32.4 3.0 collective-permute-done.6
  36.8 3.3 collective-permute-start.10
  41.9 1.8 collective-permute-done.10.refs_1_.refs_3_
  43.7 2.2 collective-permute-start.17
  47.0 1.5 collective-permute-start.15
  48.6 13.7 %keys.1 = (bf16[1024,768]{1,0:T(8,128)(2,1)}, bf16[1024,768]{1,0:T(8,128)(2,1)}, bf16[1024,768]{1,0:T(8,128)(2,1)}, bf16[1024,1536]{1,0:T(8,128)(2,1)}, bf16[7,1...) custom-call(s32[1]{0:T(128)} %bitcast.me_ref, f32[5]{0:T(128)} %copy-done.21, ...), custom_call_target="tpu_custom_call" | custom-call | flops 11000000512 | bytes 22000000 | tf_op jit(solution)/shard_map/keys/pallas_call | solution.py:709
  62.3 1.3 collective-permute-start.20
  63.9 1.3 collective-permute-start.22
  66.9 10.2 %local.2 = (bf16[1024,768]{1,0:T(8,128)(2,1)}, bf16[1024,1536]{1,0:T(8,128)(2,1)}, f32[1024,768]{1,0:T(8,128)}, f32[1024,768]{1,0:T(8,128)}, bf16[4,12,128,128]{3,2,1,0:T(8,128)(2,1)}, /*index=5*/f32[12,128,128]{2,1,0:T(8,128)}) custom-call(s32[1]{0:T(128)} %bitcast.me_ref, f32[5]{0:T(128)} %copy-done.21, bf16[1024,768]{1,0:T(8,128)(2,1)} %get-tuple-element.114.h_ref, ...), custom_call_target="tpu_custom_call" | custom-call | flops 7500000256 | bytes 15000000 | tf_op jit(solution)/shard_map/local/pallas_call | solution.py:749
  77.1 4.7 %collective-permute-done.13 = bf16[96,1920]{1,0:T(8,128)(2,1)S(1)} collective-permute-done((bf16[96,1920]{1,0:T(8,128)(2,1)S(1)}, bf16[96,1920]{1,0:T(8,128)(2,1)S(1)}, u32[]{:S(2)}, u32[]{:S(2)}) %collective-permute-start.13) | collective-permute-done | bytes 368672 | tf_op jit(solution)/shard_map/ppermute | solution.py:34
  84.8 2.3 collective-permute-start.23
  87.1 7.9 %collective-permute-done.18 = bf16[384,768]{1,0:T(8,128)(2,1)S(1)} collective-permute-done((bf16[384,768]{1,0:T(8,128)(2,1)S(1)}, bf16[384,768]{1,0:T(8,128)(2,1)S(1)}, u32[]{:S(2)}, u32[]{:S(2)}) %collective-permute-start.18) | collective-permute-done | bytes 589856 | tf_op jit(solution)/shard_map/ppermute | solution.py:34
  96.2 10.7 %local.3 = (bf16[1024,768]{1,0:T(8,128)(2,1)}, bf16[1024,1536]{1,0:T(8,128)(2,1)}, f32[1024,768]{1,0:T(8,128)}, f32[1024,768]{1,0:T(8,128)}, bf16[4,12,128,128]{3,2,1,0:T(8,128)(2,1)}, /*index=5*/f32[12,128,128]{2,1,0:T(8,128)}) custom-call(s32[1]{0:T(128)} %bitcast.me_ref, ...), custom_call_target="tpu_custom_call", output_to_operand_aliasing={{0}: (11, {}), {1}: (12, {}), {2}: (13, {}), {3}: (14, {}),... | custom-call | flops 7500000256 | bytes 15000000 | tf_op jit(solution)/shard_map/local/pallas_call | solution.py:749
  108.0 1.7 pad_maximum_fusion.2.refs_2_
  109.7 3.7 %collective-permute-start.25 = (bf16[4,384,768]{2,1,0:T(8,128)(2,1)}, bf16[4,384,768]{2,1,0:T(8,128)(2,1)}, u32[]{:S(2)}, u32[]{:S(2)}) collective-permute-start(bf16[4,384,768]{2,1,0:T(8,128)(2,1)} %pad_maximum_fusion.2.refs_2_), channel_id=1, source_target_pairs={{0,4},{4,0},{8,12},{12,8},{16,20},{20,16},{24,28},{28,24},{1,5},{5... | collective-permute-start | bytes 7077896 | tf_op jit(solution)/shard_map/ppermute | solution.py:34
  113.4 2.2 pad_maximum_fusion.5.refs_4_
  117.1 2.1 collective-permute-done.26.refs_5_
  119.2 43.1 %middle.1 = (bf16[1024,768]{1,0:T(8,128)(2,1)}, bf16[1024,768]{1,0:T(8,128)(2,1)}, bf16[1024,768]{1,0:T(8,128)(2,1)}, bf16[1024,3072]{1,0:T(8,128)(2,1)}, bf16[1...) custom-call(s32[1]{0:T(128)} %bitcast.me_ref, ...), custom_call_target="tpu_custom_call" | custom-call | flops 21500000256 | bytes 43000000 | tf_op jit(solution)/shard_map/middle/pallas_call | solution.py:784
  163.6 1.4 collective-permute-start.29
  165.0 8.3 %convolution_convert_fusion.1 = bf16[768,3072]{1,0:T(8,128)(2,1)S(1)} fusion(bf16[1024,768]{1,0:T(8,128)(2,1)} %get-tuple-element.144, bf16[1024,3072]{1,0:T(8,128)(2,1)} %get-tuple-element.145), kind=kOutput, calls=%fused_computation.2 | convolution fusion | flops 4834197504 | bytes 12582912 | tf_op jit(solution)/shard_map/dot_general | solution.py:30
  173.4 1.4 convolution_convert_fusion.4
  174.8 1.8 dynamic-slice_bitcast_fusion
  177.9 3.9 %pad_maximum_fusion = bf16[2,2,96,3968]{3,2,1,0:T(8,128)(2,1)} fusion(bf16[2,2,96,128]{3,2,1,0:T(8,128)(2,1)S(1)} %get-tuple-element.238, bf16[2,2,96,768]{3,2,1,0:T(8,128)(2,1)} %get-tuple-element.221, bf16[2,2,96,3072]{3,2,1,0:T(8,128)(2,1)} %get-tuple-element.215), kind=kLoop, calls=%fused_computation.8 | loop fusion | flops 9142272 | bytes 6094848 | tf_op jit(solution)/shard_map/concatenate | solution.py:105
  183.0 2.2 pad_maximum_fusion.6.refs_0_
  185.2 8.5 %convolution_convert_fusion = bf16[3072,768]{1,0:T(8,128)(2,1)S(1)} fusion(bf16[1024,3072]{1,0:T(8,128)(2,1)} %get-tuple-element.154, bf16[1,1024,768]{2,1,0:T(8,128)(2,1)S(1)} %copy-done.23), kind=kOutput, calls=%fused_computation.1 | convolution fusion | flops 4834197504 | bytes 12582912 | tf_op jit(solution)/shard_map/dot_general | solution.py:30
  193.7 1.8 dynamic-slice_bitcast_fusion.1
  199.5 2.4 add_convert_fusion
  201.9 1.2 dynamic-slice_bitcast_fusion.3
  203.2 2.2 fusion
  207.7 15.0 %back.2 = (bf16[1024,1152]{1,0:T(8,128)(2,1)}, bf16[384,128]{1,0:T(8,128)(2,1)}) custom-call(s32[1]{0:T(128)} %bitcast.me_ref, f32[8]{0:T(128)} %bitcast.236, f32[5]{0:T(128)} %copy-done.21, bf16[1024,768]{1,0:T(8,128)(2,1)} %get-tuple-element.158.q_ref, bf16[1024,768]{1,0:T(8,128)(2,1)} %get-tuple-element.159.k_ref, ...), custom_call_target="tpu_custom_call" | custom-call | flops 9500000256 | bytes 19000000 | tf_op jit(solution)/shard_map/back/pallas_call | solution.py:851
  222.7 4.4 %convolution_convert_fusion.3 = bf16[768,1152]{1,0:T(8,128)(2,1)S(1)} fusion(bf16[1024,768]{1,0:T(8,128)(2,1)} %get-tuple-element.114.h_ref, bf16[1024,1152]{1,0:T(8,128)(2,1)} %get-tuple-element.163.refs_0_), kind=kOutput, calls=%fused_computation.7 | convolution fusion | flops 1812824064 | bytes 5701632 | tf_op jit(solution)/shard_map/dot_general | solution.py:30
  227.1 1.4 dynamic-slice_bitcast_fusion.6
  228.5 5.8 %collective-permute-done.32 = bf16[2,384,768]{2,1,0:T(8,128)(2,1)} collective-permute-done((bf16[2,384,768]{2,1,0:T(8,128)(2,1)}, bf16[2,384,768]{2,1,0:T(8,128)(2,1)}, u32[]{:S(2)}, u32[]{:S(2)}) %collective-permute-start.32) | collective-permute-done | bytes 1179680 | tf_op jit(solution)/shard_map/ppermute | solution.py:34
  234.4 1.5 fusion.2
  237.3 14.9 %back.3 = (bf16[1024,1152]{1,0:T(8,128)(2,1)}, bf16[384,128]{1,0:T(8,128)(2,1)}) custom-call(s32[1]{0:T(128)} %bitcast.me_ref, f32[8]{0:T(128)} %bitcast.237, f32[5]{0:T(128)} %copy-done.21, bf16[1024,768]{1,0:T(8,128)(2,1)} %get-tuple-element.158.q_ref, bf16[1024,768]{1,0:T(8,128)(2,1)} %get-tuple-element.159.k_ref, ...), custom_call_target="tpu_custom_call" | custom-call | flops 9500000256 | bytes 19000000 | tf_op jit(solution)/shard_map/back/pallas_call | solution.py:851
  253.2 4.4 %convolution_convert_fusion.2 = bf16[768,1152]{1,0:T(8,128)(2,1)S(1)} fusion(bf16[1024,768]{1,0:T(8,128)(2,1)} %get-tuple-element.114.h_ref, bf16[1024,1152]{1,0:T(8,128)(2,1)} %get-tuple-element.166.refs_1_), kind=kOutput, calls=%fused_computation.6 | convolution fusion | flops 1812824064 | bytes 5701632 | tf_op jit(solution)/shard_map/dot_general | solution.py:30
  258.9 1.5 pad_maximum_fusion.4
  261.6 1.7 fusion.1
  266.4 11.9 %enter.1 = (f32[1024,768]{1,0:T(8,128)}, f32[8,768]{1,0:T(8,128)}) custom-call(s32[1]{0:T(128)} %bitcast.me_ref, bf16[1024,768]{1,0:T(8,128)(2,1)} %bitcast.241, f32[1024,768]{1,0:T(8,128)} %get-tuple-element.172.dr_ref, f32[8,768]{1,0:T(8,128)} %get-tuple-element.103.gb_ref, bf16[1024,1152]{1,0:T(8,128)(2,1)} %get-tuple-element.163.refs_0_, ...), custom_call_target="tpu_custom_call" | custom-call | flops 5500000256 | bytes 11000000 | tf_op jit(solution)/shard_map/enter/pallas_call | solution.py:891
  280.0 2.5 collective-permute-start.50
  282.8 2.2 add_convert_fusion.1
  285.8 1.3 collective-permute-start.40
  287.1 1.3 fusion.3
  288.4 4.4 %collective-permute-done.50 = bf16[96,768]{1,0:T(8,128)(2,1)S(1)} collective-permute-done((bf16[96,768]{1,0:T(8,128)(2,1)S(1)}, bf16[96,768]{1,0:T(8,128)(2,1)S(1)}, u32[]{:S(2)}, u32[]{:S(2)}) %collective-permute-start.50) | collective-permute-done | bytes 147488 | tf_op jit(solution)/shard_map/ppermute | solution.py:158
  292.8 3.5 %collective-permute-done.51 = bf16[96,768]{1,0:T(8,128)(2,1)S(1)} collective-permute-done((bf16[96,768]{1,0:T(8,128)(2,1)S(1)}, bf16[96,768]{1,0:T(8,128)(2,1)S(1)}, u32[]{:S(2)}, u32[]{:S(2)}) %collective-permute-start.51) | collective-permute-done | bytes 147488 | tf_op jit(solution)/shard_map/ppermute | solution.py:158
  296.6 1.3 collective-permute-start.48
  299.7 1.2 collective-permute-start.41
  301.0 4.4 %collective-permute-done.38 = bf16[96,1280]{1,0:T(8,128)(2,1)S(1)} collective-permute-done((bf16[96,1280]{1,0:T(8,128)(2,1)S(1)}, bf16[96,1280]{1,0:T(8,128)(2,1)S(1)}, u32[]{:S(2)}, u32[]{:S(2)}) %collective-permute-start.38) | collective-permute-done | bytes 245792 | tf_op jit(solution)/shard_map/ppermute | solution.py:34
  306.0 6.6 %collective-permute-done.47 = bf16[24,3968]{1,0:T(8,128)(2,1)S(1)} collective-permute-done((bf16[24,3968]{1,0:T(8,128)(2,1)S(1)}, bf16[24,3968]{1,0:T(8,128)(2,1)S(1)}, u32[]{:S(2)}, u32[]{:S(2)}) %collective-permute-start.47) | collective-permute-done | bytes 190496 | tf_op jit(solution)/shard_map/ppermute | solution.py:158
  312.7 1.4 collective-permute-done.48
  315.7 1.8 collective-permute-start.43
  317.4 1.4 collective-permute-start.44
  320.0 5.8 %collective-permute-done.43 = bf16[24,2560]{1,0:T(8,128)(2,1)S(1)} collective-permute-done((bf16[24,2560]{1,0:T(8,128)(2,1)S(1)}, bf16[24,2560]{1,0:T(8,128)(2,1)S(1)}, u32[]{:S(2)}, u32[]{:S(2)}) %collective-permute-start.43) | collective-permute-done | bytes 122912 | tf_op jit(solution)/shard_map/ppermute | solution.py:158
  325.9 3.1 collective-permute-done.44
  (234 shorter events, 47.3 us)
Async XLA Ops:
  4.2 17.6 %copy-start.15 = (bf16[24,3072]{1,0:T(8,128)(2,1)S(1)}, bf16[24,3072]{1,0:T(8,128)(2,1)}, u32[]{:S(2)}) copy-start(bf16[24,3072]{1,0:T(8,128)(2,1)} %param.17) | copy-start | bytes 442372
  4.2 17.6 %copy-start.17 = (bf16[24,768]{1,0:T(8,128)(2,1)S(1)}, bf16[24,768]{1,0:T(8,128)(2,1)}, u32[]{:S(2)}) copy-start(bf16[24,768]{1,0:T(8,128)(2,1)} %param.16) | copy-start | bytes 110596
  5.2 6.0 %collective-permute-start = (bf16[24,2560]{1,0:T(8,128)(2,1)S(1)}, bf16[24,2560]{1,0:T(8,128)(2,1)S(1)}, u32[]{:S(2)}, u32[]{:S(2)}) collective-permute-start(bf16[24,2560]{1,0:T(8,128)(2,1)S(1)} %concatenate.61), channel_id=1, source_target_pairs={{0,3},{1,0},{2,1},{3,2},{4,7},{5,4},{6,5},{7,6},{8,11},{9,8},{10,9... | collective-permute-start | bytes 368648 | tf_op jit(solution)/shard_map/ppermute | solution.py:43
  5.3 9.5 %collective-permute-start.1 = (bf16[24,2560]{1,0:T(8,128)(2,1)S(1)}, bf16[24,2560]{1,0:T(8,128)(2,1)S(1)}, u32[]{:S(2)}, u32[]{:S(2)}) collective-permute-start(bf16[24,2560]{1,0:T(8,128)(2,1)S(1)} %concatenate.61), channel_id=1, source_target_pairs={{0,2},{1,3},{2,0},{3,1},{4,6},{5,7},{6,4},{7,5},{8,10},{9,11},{10,... | collective-permute-start | bytes 368648 | tf_op jit(solution)/shard_map/ppermute | solution.py:43
  7.7 10.2 %collective-permute-start.2 = (bf16[24,2560]{1,0:T(8,128)(2,1)S(1)}, bf16[24,2560]{1,0:T(8,128)(2,1)S(1)}, u32[]{:S(2)}, u32[]{:S(2)}) collective-permute-start(bf16[24,2560]{1,0:T(8,128)(2,1)S(1)} %concatenate.61), channel_id=1, source_target_pairs={{0,1},{1,2},{2,3},{3,0},{4,5},{5,6},{6,7},{7,4},{8,9},{9,10},{10,1... | collective-permute-start | bytes 368648 | tf_op jit(solution)/shard_map/ppermute | solution.py:43
  11.2 18.6 %copy-start.21 = (f32[5]{0:T(128)}, f32[5]{0:T(128)S(1)}, u32[]{:S(2)}) copy-start(f32[5]{0:T(128)S(1)} %pad_maximum_fusion.15.cend_ref) | copy-start | bytes 64
  18.1 11.6 %collective-permute-start.4 = (bf16[96,2560]{1,0:T(8,128)(2,1)S(1)}, bf16[96,2560]{1,0:T(8,128)(2,1)S(1)}, u32[]{:S(2)}, u32[]{:S(2)}) collective-permute-start(bf16[96,2560]{1,0:T(8,128)(2,1)S(1)} %constant_dynamic-slice_fusion.3), channel_id=1, source_target_pairs={{0,8},{4,12},{8,0},{12,4},{16,24},{20,28},{24,16},{28,20},{1,9},{5... | collective-permute-start | bytes 1474568 | tf_op jit(solution)/shard_map/ppermute | solution.py:34
  19.4 11.7 %collective-permute-start.5 = (bf16[96,2560]{1,0:T(8,128)(2,1)S(1)}, bf16[96,2560]{1,0:T(8,128)(2,1)S(1)}, u32[]{:S(2)}, u32[]{:S(2)}) collective-permute-start(bf16[96,2560]{1,0:T(8,128)(2,1)S(1)} %constant_dynamic-slice_fusion.3), channel_id=1, source_target_pairs={{0,16},{4,20},{8,24},{12,28},{16,0},{20,4},{24,8},{28,12},{1,17},{... | collective-permute-start | bytes 1474568 | tf_op jit(solution)/shard_map/ppermute | solution.py:34
  20.7 16.1 %copy-start.19 = (f32[1,1,4,256]{3,1,2,0:T(1,128)}, f32[1,1,4,256]{3,1,2,0:T(1,128)S(1)}, u32[]{:S(2)}) copy-start(f32[1,1,4,256]{3,1,2,0:T(1,128)S(1)} %copy.96) | copy-start | bytes 12292
  21.8 19.3 %collective-permute-start.8 = (bf16[24,3840]{1,0:T(8,128)(2,1)S(1)}, bf16[24,3840]{1,0:T(8,128)(2,1)S(1)}, u32[]{:S(2)}, u32[]{:S(2)}) collective-permute-start(bf16[24,3840]{1,0:T(8,128)(2,1)S(1)} %pad_maximum_fusion.10), channel_id=1, source_target_pairs={{0,2},{1,3},{2,0},{3,1},{4,6},{5,7},{6,4},{7,5},{8,10},{9,11},{10,... | collective-permute-start | bytes 552968 | tf_op jit(solution)/shard_map/ppermute | solution.py:43
  22.3 18.7 %collective-permute-start.3 = (bf16[24,3840]{1,0:T(8,128)(2,1)S(1)}, bf16[24,3840]{1,0:T(8,128)(2,1)S(1)}, u32[]{:S(2)}, u32[]{:S(2)}) collective-permute-start(bf16[24,3840]{1,0:T(8,128)(2,1)S(1)} %pad_maximum_fusion.10), channel_id=1, source_target_pairs={{0,3},{1,0},{2,1},{3,2},{4,7},{5,4},{6,5},{7,6},{8,11},{9,8},{10,9... | collective-permute-start | bytes 552968 | tf_op jit(solution)/shard_map/ppermute | solution.py:43
  25.2 15.8 %collective-permute-start.9 = (bf16[24,3840]{1,0:T(8,128)(2,1)S(1)}, bf16[24,3840]{1,0:T(8,128)(2,1)S(1)}, u32[]{:S(2)}, u32[]{:S(2)}) collective-permute-start(bf16[24,3840]{1,0:T(8,128)(2,1)S(1)} %pad_maximum_fusion.10), channel_id=1, source_target_pairs={{0,1},{1,2},{2,3},{3,0},{4,5},{5,6},{6,7},{7,4},{8,9},{9,10},{10,1... | collective-permute-start | bytes 552968 | tf_op jit(solution)/shard_map/ppermute | solution.py:43
  29.7 5.7 %collective-permute-start.6 = (bf16[96,1280]{1,0:T(8,128)(2,1)S(1)}, bf16[96,1280]{1,0:T(8,128)(2,1)S(1)}, u32[]{:S(2)}, u32[]{:S(2)}) collective-permute-start(bf16[96,1280]{1,0:T(8,128)(2,1)S(1)} %slice.135), channel_id=1, source_target_pairs={{0,16},{4,20},{8,24},{12,28},{16,0},{20,4},{24,8},{28,12},{1,17},{... | collective-permute-start | bytes 737288 | tf_op jit(solution)/shard_map/ppermute | solution.py:34
  31.1 5.4 %collective-permute-start.7 = (bf16[96,1280]{1,0:T(8,128)(2,1)S(1)}, bf16[96,1280]{1,0:T(8,128)(2,1)S(1)}, u32[]{:S(2)}, u32[]{:S(2)}) collective-permute-start(bf16[96,1280]{1,0:T(8,128)(2,1)S(1)} %slice.136), channel_id=1, source_target_pairs={{0,8},{4,12},{8,0},{12,4},{16,24},{20,28},{24,16},{28,20},{1,9},{5... | collective-permute-start | bytes 737288 | tf_op jit(solution)/shard_map/ppermute | solution.py:34
  36.8 6.9 %collective-permute-start.10 = (bf16[4,96,2560]{2,1,0:T(8,128)(2,1)S(1)}, bf16[4,96,2560]{2,1,0:T(8,128)(2,1)S(1)}, u32[]{:S(2)}, u32[]{:S(2)}) collective-permute-start(bf16[4,96,2560]{2,1,0:T(8,128)(2,1)S(1)} %pad_maximum_fusion.3.refs_0_.refs_2_), channel_id=1, source_target_pairs={{0,4},{4,0},{8,12},{12,8},{16,20},{20,16},{24,28},{28,24},{1,5},{5... | collective-permute-start | bytes 5898248 | tf_op jit(solution)/shard_map/ppermute | solution.py:34
  41.3 21.0 %collective-permute-start.11 = (bf16[96,3840]{1,0:T(8,128)(2,1)S(1)}, bf16[96,3840]{1,0:T(8,128)(2,1)S(1)}, u32[]{:S(2)}, u32[]{:S(2)}) collective-permute-start(bf16[96,3840]{1,0:T(8,128)(2,1)S(1)} %constant_dynamic-slice_fusion.2), channel_id=1, source_target_pairs={{0,8},{4,12},{8,0},{12,4},{16,24},{20,28},{24,16},{28,20},{1,9},{5... | collective-permute-start | bytes 2211848 | tf_op jit(solution)/shard_map/ppermute | solution.py:34
  41.6 22.0 %collective-permute-start.12 = (bf16[96,3840]{1,0:T(8,128)(2,1)S(1)}, bf16[96,3840]{1,0:T(8,128)(2,1)S(1)}, u32[]{:S(2)}, u32[]{:S(2)}) collective-permute-start(bf16[96,3840]{1,0:T(8,128)(2,1)S(1)} %constant_dynamic-slice_fusion.2), channel_id=1, source_target_pairs={{0,16},{4,20},{8,24},{12,28},{16,0},{20,4},{24,8},{28,12},{1,17},{... | collective-permute-start | bytes 2211848 | tf_op jit(solution)/shard_map/ppermute | solution.py:34
  43.7 20.2 %collective-permute-start.17 = (bf16[96,768]{1,0:T(8,128)(2,1)S(1)}, bf16[96,768]{1,0:T(8,128)(2,1)S(1)}, u32[]{:S(2)}, u32[]{:S(2)}) collective-permute-start(bf16[96,768]{1,0:T(8,128)(2,1)S(1)} %copy-done.12), channel_id=1, source_target_pairs={{0,1},{1,2},{2,3},{3,0},{4,5},{5,6},{6,7},{7,4},{8,9},{9,10},{10,1... | collective-permute-start | bytes 442376 | tf_op jit(solution)/shard_map/ppermute | solution.py:43
  45.9 19.3 %collective-permute-start.16 = (bf16[96,768]{1,0:T(8,128)(2,1)S(1)}, bf16[96,768]{1,0:T(8,128)(2,1)S(1)}, u32[]{:S(2)}, u32[]{:S(2)}) collective-permute-start(bf16[96,768]{1,0:T(8,128)(2,1)S(1)} %copy-done.12), channel_id=1, source_target_pairs={{0,2},{1,3},{2,0},{3,1},{4,6},{5,7},{6,4},{7,5},{8,10},{9,11},{10,... | collective-permute-start | bytes 442376 | tf_op jit(solution)/shard_map/ppermute | solution.py:43
  47.0 19.4 %collective-permute-start.15 = (bf16[96,768]{1,0:T(8,128)(2,1)S(1)}, bf16[96,768]{1,0:T(8,128)(2,1)S(1)}, u32[]{:S(2)}, u32[]{:S(2)}) collective-permute-start(bf16[96,768]{1,0:T(8,128)(2,1)S(1)} %copy-done.12), channel_id=1, source_target_pairs={{0,3},{1,0},{2,1},{3,2},{4,7},{5,4},{6,5},{7,6},{8,11},{9,8},{10,9... | collective-permute-start | bytes 442376 | tf_op jit(solution)/shard_map/ppermute | solution.py:43
  62.3 22.4 %collective-permute-start.20 = (bf16[7,128,128]{2,1,0:T(8,128)(2,1)}, bf16[7,128,128]{2,1,0:T(8,128)(2,1)}, u32[]{:S(2)}, u32[]{:S(2)}) collective-permute-start(bf16[7,128,128]{2,1,0:T(8,128)(2,1)} %get-tuple-element.138), channel_id=1, source_target_pairs={{0,8},{4,12},{8,0},{12,4},{16,24},{20,28},{24,16},{28,20},{1,9},{5... | collective-permute-start | bytes 688136 | tf_op jit(solution)/shard_map/ppermute | solution.py:34
  63.6 23.5 %collective-permute-start.21 = (bf16[7,128,128]{2,1,0:T(8,128)(2,1)}, bf16[7,128,128]{2,1,0:T(8,128)(2,1)}, u32[]{:S(2)}, u32[]{:S(2)}) collective-permute-start(bf16[7,128,128]{2,1,0:T(8,128)(2,1)} %get-tuple-element.138), channel_id=1, source_target_pairs={{0,16},{4,20},{8,24},{12,28},{16,0},{20,4},{24,8},{28,12},{1,17},{... | collective-permute-start | bytes 688136 | tf_op jit(solution)/shard_map/ppermute | solution.py:34
  63.9 23.2 %collective-permute-start.22 = (bf16[7,128,128]{2,1,0:T(8,128)(2,1)}, bf16[7,128,128]{2,1,0:T(8,128)(2,1)}, u32[]{:S(2)}, u32[]{:S(2)}) collective-permute-start(bf16[7,128,128]{2,1,0:T(8,128)(2,1)} %get-tuple-element.138), channel_id=1, source_target_pairs={{0,24},{4,28},{8,16},{12,20},{16,8},{20,12},{24,0},{28,4},{1,25},{... | collective-permute-start | bytes 688136 | tf_op jit(solution)/shard_map/ppermute | solution.py:34
  65.2 16.6 %collective-permute-start.13 = (bf16[96,1920]{1,0:T(8,128)(2,1)S(1)}, bf16[96,1920]{1,0:T(8,128)(2,1)S(1)}, u32[]{:S(2)}, u32[]{:S(2)}) collective-permute-start(bf16[96,1920]{1,0:T(8,128)(2,1)S(1)} %slice.112), channel_id=1, source_target_pairs={{0,8},{4,12},{8,0},{12,4},{16,24},{20,28},{24,16},{28,20},{1,9},{5... | collective-permute-start | bytes 1105928 | tf_op jit(solution)/shard_map/ppermute | solution.py:34
  66.4 16.6 %collective-permute-start.14 = (bf16[96,1920]{1,0:T(8,128)(2,1)S(1)}, bf16[96,1920]{1,0:T(8,128)(2,1)}, u32[]{:S(2)}, u32[]{:S(2)}) collective-permute-start(bf16[96,1920]{1,0:T(8,128)(2,1)S(1)} %slice.113), channel_id=1, source_target_pairs={{0,16},{4,20},{8,24},{12,28},{16,0},{20,4},{24,8},{28,12},{1,17},{... | collective-permute-start | bytes 1105928 | tf_op jit(solution)/shard_map/ppermute | solution.py:34
  77.1 7.2 %copy-start.9 = (bf16[96,3840]{1,0:T(8,128)(2,1)S(1)}, bf16[96,3840]{1,0:T(8,128)(2,1)}, u32[]{:S(2)}) copy-start(bf16[96,3840]{1,0:T(8,128)(2,1)} %copy-done.8) | copy-start | bytes 2211844
  77.1 7.2 %copy-start.11 = (bf16[96,3840]{1,0:T(8,128)(2,1)S(1)}, bf16[96,3840]{1,0:T(8,128)(2,1)}, u32[]{:S(2)}) copy-start(bf16[96,3840]{1,0:T(8,128)(2,1)} %copy-done.10) | copy-start | bytes 2211844
  81.8 13.2 %collective-permute-start.18 = (bf16[384,768]{1,0:T(8,128)(2,1)S(1)}, bf16[384,768]{1,0:T(8,128)(2,1)S(1)}, u32[]{:S(2)}, u32[]{:S(2)}) collective-permute-start(bf16[384,768]{1,0:T(8,128)(2,1)S(1)} %constant_dynamic-slice_fusion), channel_id=1, source_target_pairs={{0,8},{4,12},{8,0},{12,4},{16,24},{20,28},{24,16},{28,20},{1,9},{5... | collective-permute-start | bytes 1769480 | tf_op jit(solution)/shard_map/ppermute | solution.py:34
  83.0 12.9 %collective-permute-start.19 = (bf16[384,768]{1,0:T(8,128)(2,1)S(1)}, bf16[384,768]{1,0:T(8,128)(2,1)S(1)}, u32[]{:S(2)}, u32[]{:S(2)}) collective-permute-start(bf16[384,768]{1,0:T(8,128)(2,1)S(1)} %constant_dynamic-slice_fusion), channel_id=1, source_target_pairs={{0,16},{4,20},{8,24},{12,28},{16,0},{20,4},{24,8},{28,12},{1,17},{... | collective-permute-start | bytes 1769480 | tf_op jit(solution)/shard_map/ppermute | solution.py:34
  84.7 22.2 %copy-start.6 = (bf16[4,96,3840]{2,1,0:T(8,128)(2,1)}, bf16[4,96,3840]{2,1,0:T(8,128)(2,1)S(1)}, u32[]{:S(2)}) copy-start(bf16[4,96,3840]{2,1,0:T(8,128)(2,1)S(1)} %pad_maximum_fusion.1.refs_0_) | copy-start | bytes 8847364
  84.8 34.5 %collective-permute-start.23 = (bf16[4,96,3840]{2,1,0:T(8,128)(2,1)S(1)}, bf16[4,96,3840]{2,1,0:T(8,128)(2,1)}, u32[]{:S(2)}, u32[]{:S(2)}) collective-permute-start(bf16[4,96,3840]{2,1,0:T(8,128)(2,1)S(1)} %pad_maximum_fusion.1.refs_0_), channel_id=1, source_target_pairs={{0,4},{4,0},{8,12},{12,8},{16,20},{20,16},{24,28},{28,24},{1,5},{5... | collective-permute-start | bytes 8847368 | tf_op jit(solution)/shard_map/ppermute | solution.py:34
  95.9 12.1 %collective-permute-start.24 = (bf16[384,768]{1,0:T(8,128)(2,1)S(1)}, bf16[384,768]{1,0:T(8,128)(2,1)S(1)}, u32[]{:S(2)}, u32[]{:S(2)}) collective-permute-start(bf16[384,768]{1,0:T(8,128)(2,1)S(1)} %collective-permute-done.19), channel_id=1, source_target_pairs={{0,8},{4,12},{8,0},{12,4},{16,24},{20,28},{24,16},{28,20},{1,9},{5... | collective-permute-start | bytes 1769480 | tf_op jit(solution)/shard_map/ppermute | solution.py:34
  108.0 5.4 %copy-start.13 = (bf16[7,128,128]{2,1,0:T(8,128)(2,1)S(1)}, bf16[7,128,128]{2,1,0:T(8,128)(2,1)}, u32[]{:S(2)}) copy-start(bf16[7,128,128]{2,1,0:T(8,128)(2,1)} %get-tuple-element.138) | copy-start | bytes 688132
  109.7 9.5 %collective-permute-start.25 = (bf16[4,384,768]{2,1,0:T(8,128)(2,1)}, bf16[4,384,768]{2,1,0:T(8,128)(2,1)}, u32[]{:S(2)}, u32[]{:S(2)}) collective-permute-start(bf16[4,384,768]{2,1,0:T(8,128)(2,1)} %pad_maximum_fusion.2.refs_2_), channel_id=1, source_target_pairs={{0,4},{4,0},{8,12},{12,8},{16,20},{20,16},{24,28},{28,24},{1,5},{5... | collective-permute-start | bytes 7077896 | tf_op jit(solution)/shard_map/ppermute | solution.py:34
  115.7 3.6 %collective-permute-start.26 = (bf16[4,7,128,128]{3,2,1,0:T(8,128)(2,1)}, bf16[4,7,128,128]{3,2,1,0:T(8,128)(2,1)}, u32[]{:S(2)}, u32[]{:S(2)}) collective-permute-start(bf16[4,7,128,128]{3,2,1,0:T(8,128)(2,1)} %pad_maximum_fusion.5.refs_4_), channel_id=1, source_target_pairs={{0,4},{4,0},{8,12},{12,8},{16,20},{20,16},{24,28},{28,24},{1,5},{5... | collective-permute-start | bytes 2752520 | tf_op jit(solution)/shard_map/ppermute | solution.py:34
  162.3 20.6 %collective-permute-start.27 = (bf16[7,128,128]{2,1,0:T(8,128)(2,1)}, bf16[7,128,128]{2,1,0:T(8,128)(2,1)}, u32[]{:S(2)}, u32[]{:S(2)}) collective-permute-start(bf16[7,128,128]{2,1,0:T(8,128)(2,1)} %get-tuple-element.150), channel_id=1, source_target_pairs={{0,8},{4,12},{8,0},{12,4},{16,24},{20,28},{24,16},{28,20},{1,9},{5... | collective-permute-start | bytes 688136 | tf_op jit(solution)/shard_map/ppermute | solution.py:34
  162.7 20.3 %collective-permute-start.28 = (bf16[7,128,128]{2,1,0:T(8,128)(2,1)}, bf16[7,128,128]{2,1,0:T(8,128)(2,1)}, u32[]{:S(2)}, u32[]{:S(2)}) collective-permute-start(bf16[7,128,128]{2,1,0:T(8,128)(2,1)} %get-tuple-element.150), channel_id=1, source_target_pairs={{0,16},{4,20},{8,24},{12,28},{16,0},{20,4},{24,8},{28,12},{1,17},{... | collective-permute-start | bytes 688136 | tf_op jit(solution)/shard_map/ppermute | solution.py:34
  163.6 19.4 %collective-permute-start.29 = (bf16[7,128,128]{2,1,0:T(8,128)(2,1)}, bf16[7,128,128]{2,1,0:T(8,128)(2,1)}, u32[]{:S(2)}, u32[]{:S(2)}) collective-permute-start(bf16[7,128,128]{2,1,0:T(8,128)(2,1)} %get-tuple-element.150), channel_id=1, source_target_pairs={{0,24},{4,28},{8,16},{12,20},{16,8},{20,12},{24,0},{28,4},{1,25},{... | collective-permute-start | bytes 688136 | tf_op jit(solution)/shard_map/ppermute | solution.py:34
  165.0 8.3 %copy-start.24 = (bf16[1024,768]{1,0:T(8,128)(2,1)S(1)}, bf16[1024,768]{1,0:T(8,128)(2,1)}, u32[]{:S(2)}) copy-start(bf16[1024,768]{1,0:T(8,128)(2,1)} %get-tuple-element.146) | copy-start | bytes 4718596
  165.0 8.3 %copy-start.25 = (bf16[1024,768]{1,0:T(8,128)(2,1)S(1)}, bf16[1024,768]{1,0:T(8,128)(2,1)}, u32[]{:S(2)}) copy-start(bf16[1024,768]{1,0:T(8,128)(2,1)} %get-tuple-element.147) | copy-start | bytes 4718596
  177.9 7.3 %copy-start.23 = (bf16[1,1024,768]{2,1,0:T(8,128)(2,1)S(1)}, bf16[1,1024,768]{2,1,0:T(8,128)(2,1)}, u32[]{:S(2)}) copy-start(bf16[1,1024,768]{2,1,0:T(8,128)(2,1)} %param.19) | copy-start | bytes 4718596
  181.8 17.8 %collective-permute-start.31 = (bf16[2,2,96,3968]{3,2,1,0:T(8,128)(2,1)}, bf16[2,2,96,3968]{3,2,1,0:T(8,128)(2,1)}, u32[]{:S(2)}, u32[]{:S(2)}) collective-permute-start(bf16[2,2,96,3968]{3,2,1,0:T(8,128)(2,1)} %pad_maximum_fusion), channel_id=1, source_target_pairs={{0,4},{4,0},{8,12},{12,8},{16,20},{20,16},{24,28},{28,24},{1,5},{5... | collective-permute-start | bytes 9142280 | tf_op jit(solution)/shard_map/ppermute | solution.py:34
  185.2 12.9 %collective-permute-start.33 = (bf16[4,7,128,128]{3,2,1,0:T(8,128)(2,1)}, bf16[4,7,128,128]{3,2,1,0:T(8,128)(2,1)}, u32[]{:S(2)}, u32[]{:S(2)}) collective-permute-start(bf16[4,7,128,128]{3,2,1,0:T(8,128)(2,1)} %pad_maximum_fusion.6.refs_0_), channel_id=1, source_target_pairs={{0,4},{4,0},{8,12},{12,8},{16,20},{20,16},{24,28},{28,24},{1,5},{5... | collective-permute-start | bytes 2752520 | tf_op jit(solution)/shard_map/ppermute | solution.py:34
  196.7 6.4 %collective-permute-start.30 = (bf16[2,2,384,768]{3,2,1,0:T(8,128)(2,1)}, bf16[2,2,384,768]{3,2,1,0:T(8,128)(2,1)}, u32[]{:S(2)}, u32[]{:S(2)}) collective-permute-start(bf16[2,2,384,768]{3,2,1,0:T(8,128)(2,1)} %dynamic-slice_bitcast_fusion.1), channel_id=1, source_target_pairs={{0,4},{4,0},{8,12},{12,8},{16,20},{20,16},{24,28},{28,24},{1,5},{5... | collective-permute-start | bytes 7077896 | tf_op jit(solution)/shard_map/ppermute | solution.py:34
  206.5 27.8 %collective-permute-start.32 = (bf16[2,384,768]{2,1,0:T(8,128)(2,1)}, bf16[2,384,768]{2,1,0:T(8,128)(2,1)}, u32[]{:S(2)}, u32[]{:S(2)}) collective-permute-start(bf16[2,384,768]{2,1,0:T(8,128)(2,1)} %dynamic-slice_bitcast_fusion.4), channel_id=1, source_target_pairs={{0,8},{4,12},{8,0},{12,4},{16,24},{20,28},{24,16},{28,20},{1,9},{5... | collective-permute-start | bytes 3538952 | tf_op jit(solution)/shard_map/ppermute | solution.py:34
  206.8 54.8 %collective-permute-start.35 = (bf16[2,96,3968]{2,1,0:T(8,128)(2,1)}, bf16[2,96,3968]{2,1,0:T(8,128)(2,1)}, u32[]{:S(2)}, u32[]{:S(2)}) collective-permute-start(bf16[2,96,3968]{2,1,0:T(8,128)(2,1)} %dynamic-slice_bitcast_fusion.3), channel_id=1, source_target_pairs={{0,16},{4,20},{8,24},{12,28},{16,0},{20,4},{24,8},{28,12},{1,17},{... | collective-permute-start | bytes 4571144 | tf_op jit(solution)/shard_map/ppermute | solution.py:34
  237.0 15.2 %copy-start.16 = (bf16[384,128]{1,0:T(8,128)(2,1)S(1)}, bf16[384,128]{1,0:T(8,128)(2,1)}, u32[]{:S(2)}) copy-start(bf16[384,128]{1,0:T(8,128)(2,1)} %get-tuple-element.167) | copy-start | bytes 294916
  237.0 28.2 %collective-permute-start.34 = (bf16[384,768]{1,0:T(8,128)(2,1)S(1)}, bf16[384,768]{1,0:T(8,128)(2,1)}, u32[]{:S(2)}, u32[]{:S(2)}) collective-permute-start(bf16[384,768]{1,0:T(8,128)(2,1)S(1)} %dynamic-slice_bitcast_fusion.10), channel_id=1, source_target_pairs={{0,16},{4,20},{8,24},{12,28},{16,0},{20,4},{24,8},{28,12},{1,17},{... | collective-permute-start | bytes 1769480 | tf_op jit(solution)/shard_map/ppermute | solution.py:34
  260.4 22.2 %collective-permute-start.36 = (bf16[2,2,96,2432]{3,2,1,0:T(8,128)(2,1)}, bf16[2,2,96,2432]{3,2,1,0:T(8,128)(2,1)}, u32[]{:S(2)}, u32[]{:S(2)}) collective-permute-start(bf16[2,2,96,2432]{3,2,1,0:T(8,128)(2,1)} %pad_maximum_fusion.4), channel_id=1, source_target_pairs={{0,4},{4,0},{8,12},{12,8},{16,20},{20,16},{24,28},{28,24},{1,5},{5... | collective-permute-start | bytes 5603336 | tf_op jit(solution)/shard_map/ppermute | solution.py:34
  264.2 21.6 %collective-permute-start.45 = (bf16[96,3968]{1,0:T(8,128)(2,1)}, bf16[96,3968]{1,0:T(8,128)(2,1)}, u32[]{:S(2)}, u32[]{:S(2)}) collective-permute-start(bf16[96,3968]{1,0:T(8,128)(2,1)} %dynamic-slice_bitcast_fusion.9), channel_id=1, source_target_pairs={{0,8},{4,12},{8,0},{12,4},{16,24},{20,28},{24,16},{28,20},{1,9},{5... | collective-permute-start | bytes 2285576 | tf_op jit(solution)/shard_map/ppermute | solution.py:34
  279.5 5.7 %collective-permute-start.39 = (bf16[2,2,96,128]{3,2,1,0:T(8,128)(2,1)S(1)}, bf16[2,2,96,128]{3,2,1,0:T(8,128)(2,1)S(1)}, u32[]{:S(2)}, u32[]{:S(2)}) collective-permute-start(bf16[2,2,96,128]{3,2,1,0:T(8,128)(2,1)S(1)} %dynamic-slice_bitcast_fusion.25), channel_id=1, source_target_pairs={{0,4},{4,0},{8,12},{12,8},{16,20},{20,16},{24,28},{28,24},{1,5},{5... | collective-permute-start | bytes 294920 | tf_op jit(solution)/shard_map/ppermute | solution.py:34
  279.9 8.5 %collective-permute-start.49 = (bf16[96,768]{1,0:T(8,128)(2,1)S(1)}, bf16[96,768]{1,0:T(8,128)(2,1)S(1)}, u32[]{:S(2)}, u32[]{:S(2)}) collective-permute-start(bf16[96,768]{1,0:T(8,128)(2,1)S(1)} %get-tuple-element.225), channel_id=1, source_target_pairs={{0,1},{1,2},{2,3},{3,0},{4,5},{5,6},{6,7},{7,4},{8,9},{9,10},{10,1... | collective-permute-start | bytes 442376 | tf_op jit(solution)/shard_map/ppermute | solution.py:158
  280.0 12.8 %collective-permute-start.50 = (bf16[96,768]{1,0:T(8,128)(2,1)S(1)}, bf16[96,768]{1,0:T(8,128)(2,1)S(1)}, u32[]{:S(2)}, u32[]{:S(2)}) collective-permute-start(bf16[96,768]{1,0:T(8,128)(2,1)S(1)} %get-tuple-element.227), channel_id=1, source_target_pairs={{0,2},{1,3},{2,0},{3,1},{4,6},{5,7},{6,4},{7,5},{8,10},{9,11},{10,... | collective-permute-start | bytes 442376 | tf_op jit(solution)/shard_map/ppermute | solution.py:158
  282.6 13.8 %collective-permute-start.51 = (bf16[96,768]{1,0:T(8,128)(2,1)S(1)}, bf16[96,768]{1,0:T(8,128)(2,1)S(1)}, u32[]{:S(2)}, u32[]{:S(2)}) collective-permute-start(bf16[96,768]{1,0:T(8,128)(2,1)S(1)} %get-tuple-element.226), channel_id=1, source_target_pairs={{0,3},{1,0},{2,1},{3,2},{4,7},{5,4},{6,5},{7,6},{8,11},{9,8},{10,9... | collective-permute-start | bytes 442376 | tf_op jit(solution)/shard_map/ppermute | solution.py:158
  285.1 13.6 %collective-permute-start.37 = (bf16[2,96,1280]{2,1,0:T(8,128)(2,1)S(1)}, bf16[2,96,1280]{2,1,0:T(8,128)(2,1)S(1)}, u32[]{:S(2)}, u32[]{:S(2)}) collective-permute-start(bf16[2,96,1280]{2,1,0:T(8,128)(2,1)S(1)} %dynamic-slice_bitcast_fusion.13), channel_id=1, source_target_pairs={{0,8},{4,12},{8,0},{12,4},{16,24},{20,28},{24,16},{28,20},{1,9},{5... | collective-permute-start | bytes 1474568 | tf_op jit(solution)/shard_map/ppermute | solution.py:34
  285.8 13.7 %collective-permute-start.40 = (bf16[2,96,1280]{2,1,0:T(8,128)(2,1)S(1)}, bf16[2,96,1280]{2,1,0:T(8,128)(2,1)S(1)}, u32[]{:S(2)}, u32[]{:S(2)}) collective-permute-start(bf16[2,96,1280]{2,1,0:T(8,128)(2,1)S(1)} %fusion.8), channel_id=1, source_target_pairs={{0,16},{4,20},{8,24},{12,28},{16,0},{20,4},{24,8},{28,12},{1,17},{... | collective-permute-start | bytes 1474568 | tf_op jit(solution)/shard_map/ppermute | solution.py:34
  296.4 9.6 %collective-permute-start.46 = (bf16[24,3968]{1,0:T(8,128)(2,1)S(1)}, bf16[24,3968]{1,0:T(8,128)(2,1)S(1)}, u32[]{:S(2)}, u32[]{:S(2)}) collective-permute-start(bf16[24,3968]{1,0:T(8,128)(2,1)S(1)} %get-tuple-element.222), channel_id=1, source_target_pairs={{0,1},{1,2},{2,3},{3,0},{4,5},{5,6},{6,7},{7,4},{8,9},{9,10},{10,1... | collective-permute-start | bytes 571400 | tf_op jit(solution)/shard_map/ppermute | solution.py:158
  296.5 16.2 %collective-permute-start.47 = (bf16[24,3968]{1,0:T(8,128)(2,1)S(1)}, bf16[24,3968]{1,0:T(8,128)(2,1)S(1)}, u32[]{:S(2)}, u32[]{:S(2)}) collective-permute-start(bf16[24,3968]{1,0:T(8,128)(2,1)S(1)} %get-tuple-element.224), channel_id=1, source_target_pairs={{0,2},{1,3},{2,0},{3,1},{4,6},{5,7},{6,4},{7,5},{8,10},{9,11},{10,... | collective-permute-start | bytes 571400 | tf_op jit(solution)/shard_map/ppermute | solution.py:158
  296.6 17.5 %collective-permute-start.48 = (bf16[24,3968]{1,0:T(8,128)(2,1)S(1)}, bf16[24,3968]{1,0:T(8,128)(2,1)S(1)}, u32[]{:S(2)}, u32[]{:S(2)}) collective-permute-start(bf16[24,3968]{1,0:T(8,128)(2,1)S(1)} %get-tuple-element.223), channel_id=1, source_target_pairs={{0,3},{1,0},{2,1},{3,2},{4,7},{5,4},{6,5},{7,6},{8,11},{9,8},{10,9... | collective-permute-start | bytes 571400 | tf_op jit(solution)/shard_map/ppermute | solution.py:158
  298.9 6.5 %collective-permute-start.38 = (bf16[96,1280]{1,0:T(8,128)(2,1)S(1)}, bf16[96,1280]{1,0:T(8,128)(2,1)S(1)}, u32[]{:S(2)}, u32[]{:S(2)}) collective-permute-start(bf16[96,1280]{1,0:T(8,128)(2,1)S(1)} %dynamic-slice_bitcast_fusion.15), channel_id=1, source_target_pairs={{0,16},{4,20},{8,24},{12,28},{16,0},{20,4},{24,8},{28,12},{1,17},{... | collective-permute-start | bytes 737288 | tf_op jit(solution)/shard_map/ppermute | solution.py:34
  299.7 6.2 %collective-permute-start.41 = (bf16[96,1280]{1,0:T(8,128)(2,1)S(1)}, bf16[96,1280]{1,0:T(8,128)(2,1)S(1)}, u32[]{:S(2)}, u32[]{:S(2)}) collective-permute-start(bf16[96,1280]{1,0:T(8,128)(2,1)S(1)} %dynamic-slice_bitcast_fusion.14), channel_id=1, source_target_pairs={{0,8},{4,12},{8,0},{12,4},{16,24},{20,28},{24,16},{28,20},{1,9},{5... | collective-permute-start | bytes 737288 | tf_op jit(solution)/shard_map/ppermute | solution.py:34
  315.6 4.4 %collective-permute-start.42 = (bf16[24,2560]{1,0:T(8,128)(2,1)S(1)}, bf16[24,2560]{1,0:T(8,128)(2,1)S(1)}, u32[]{:S(2)}, u32[]{:S(2)}) collective-permute-start(bf16[24,2560]{1,0:T(8,128)(2,1)S(1)} %get-tuple-element.228), channel_id=1, source_target_pairs={{0,1},{1,2},{2,3},{3,0},{4,5},{5,6},{6,7},{7,4},{8,9},{9,10},{10,1... | collective-permute-start | bytes 368648 | tf_op jit(solution)/shard_map/ppermute | solution.py:158
  315.7 10.2 %collective-permute-start.43 = (bf16[24,2560]{1,0:T(8,128)(2,1)S(1)}, bf16[24,2560]{1,0:T(8,128)(2,1)S(1)}, u32[]{:S(2)}, u32[]{:S(2)}) collective-permute-start(bf16[24,2560]{1,0:T(8,128)(2,1)S(1)} %get-tuple-element.230), channel_id=1, source_target_pairs={{0,2},{1,3},{2,0},{3,1},{4,6},{5,7},{6,4},{7,5},{8,10},{9,11},{10,... | collective-permute-start | bytes 368648 | tf_op jit(solution)/shard_map/ppermute | solution.py:158
  317.4 11.6 %collective-permute-start.44 = (bf16[24,2560]{1,0:T(8,128)(2,1)S(1)}, bf16[24,2560]{1,0:T(8,128)(2,1)S(1)}, u32[]{:S(2)}, u32[]{:S(2)}) collective-permute-start(bf16[24,2560]{1,0:T(8,128)(2,1)S(1)} %get-tuple-element.229), channel_id=1, source_target_pairs={{0,3},{1,0},{2,1},{3,2},{4,7},{5,4},{6,5},{7,6},{8,11},{9,8},{10,9... | collective-permute-start | bytes 368648 | tf_op jit(solution)/shard_map/ppermute | solution.py:158
  (14 other events, 42.3 us)

commit v2 on v1

--- a/solution.py
+++ b/solution.py
@@ -830,11 +830,6 @@
     red_fc.add(red_proj.out).send()
     red_proj.add(red_fc.out).send()
     me_back = after(me_arr, red_proj.out, red_fc.out)
-    squares = sum(
-        jnp.sum(stack[:, pairs, :3, 126:].astype(f32), axis=(0, 2)) for stack in g_states
-    )
-    branch_rms = jnp.sqrt(squares / (tokens * n_seq * width)).reshape(1, 3)
-
     groups = 2
     some = pairs // groups
     part = some * 128
@@ -904,18 +899,23 @@
     norm_one = jnp.stack([sums_one[0], sums_one[1]], axis=1).astype(bf16)
     norm_one = jnp.concatenate([norm_one, jnp.zeros((width, 126), bf16)], axis=1)
     red_norm = Reduce([norm_one], n_seq, depth).send()
-    red_a, red_b = red_two.add(dx).cut((groups * 3 * part + 256) // 2)
+    grad_proj = red_proj.done(dx)
+    red_a, red_b = red_two.add(grad_proj).cut((groups * 3 * part + 256) // 2)
     red_a.send()
     red_norm.add(red_a.out)
     red_b.cur = [beside(red_b.cur + red_norm.cur)]
     red_b.send()
     red_fc.add(red_a.out, red_b.out).send_stream()
-    grad_proj = red_proj.done(red_fc.out)
     while red_a.order:
         red_a.add().send()
         red_b.add().send()
     tail = Reduce(red_a.add().cur + red_b.add().cur, n_seq, depth, [], []).send_stream()
     grad_up = red_fc.done(tail.out)
+    squares = sum(
+        jnp.sum(after(stack[:, pairs, :3, 126:], tail.out).astype(f32), axis=(0, 2))
+        for stack in g_states
+    )
+    branch_rms = jnp.sqrt(squares / (tokens * n_seq * width)).reshape(1, 3)
     tail = tail.done()
     grads = [tail[:, g * 3 * part : (g + 1) * 3 * part] for g in range(groups)]
     grad_feat = tail[:, groups * 3 * part : groups * 3 * part + 128]

time: 335 us -> 331 us (0.988)
  waiting for transfers between devices: 71.5 us -> 64.1 us
    ppermute x9, waiting for transfers between devices: 26 us -> 12.8 us  [send_stream(): lax.ppermute(piece, 'stream', [(i, (i + d) % depth) for i in range(depth)])]
    ppermute x34, waiting for transfers between devices: 37.8 us -> 43.7 us  [xor_send(): return lax.ppermute(arr, 'seq', [(i, i ^ mask) for i in range(size)])]
  transfers between devices with their start and end apart: 52 -> 52, of which waited for: 22 -> 21; matrix products, arithmetic and copies ran while one was open for 21% -> 22% of each run, Pallas kernels for 23% -> 23%
where the time goes in v2:
time: 331 us; the launch traced here: 327 us
  Pallas kernels  120 us (36%)
  waiting for transfers between devices  64.1 us (19%)
  starting transfers between devices  55.1 us (17%)
  other arithmetic  33.6 us (10%)
  matrix products  27.2 us (8%)
  local copies, waits for them, and re-layouts  24.5 us (7%)
    ppermute x34, waiting for transfers between devices, xor_send(): return lax.ppermute(arr, 'seq', [(i, i ^ mask) for i in range(size)])  43.7 us
    pallas_call x1, Pallas kernels, shards(): pl.pallas_call(functools.partial(middle_body, n_seq, pairs), name='middle...  43.1 us
    ppermute x34, starting transfers between devices, xor_send(): return lax.ppermute(arr, 'seq', [(i, i ^ mask) for i in range(size)])  33.6 us
    pallas_call x2, Pallas kernels, shards(): pl.pallas_call(functools.partial(back_body, g * some, some, pairs), name=...  29.9 us
    dot_general x5, matrix products, mm_f(): lax.dot_general(a, b, (((0,), (0,)), ((), ())), preferred_element_type=f32)  27 us
    pallas_call x2, Pallas kernels, shards(): pl.pallas_call(functools.partial(local_body, base, pairs), name='local',...  20.9 us
    pallas_call x1, Pallas kernels, shards(): pl.pallas_call(functools.partial(keys_body, n_seq, pairs), name='keys', c...  13.7 us
    ppermute x9, starting transfers between devices, stream_send(): lax.ppermute(shard, 'stream', [(i, (i + d) % depth) for i in range(depth)])  13 us
  transfers between devices with their start and end apart: 52, of which 21 were waited for; matrix products, arithmetic and copies ran while one was open for 22% of the time, Pallas kernels for 23%

profile of v2, /device:TPU:9, one launch (start us, length us, event | category | flops | bytes accessed | tf_op | source)
XLA Modules:
  0.0 326.8 jit_solution(8882586346929924425)
XLA Ops:
  2.1 1.3 reduce_max.9
  5.3 2.5 collective-permute-start.1
  7.7 2.2 collective-permute-start.2
  11.2 3.5 %collective-permute-done.1 = bf16[24,2560]{1,0:T(8,128)(2,1)S(1)} collective-permute-done((bf16[24,2560]{1,0:T(8,128)(2,1)S(1)}, bf16[24,2560]{1,0:T(8,128)(2,1)S(1)}, u32[]{:S(2)}, u32[]{:S(2)}) %collective-permute-start.1) | collective-permute-done | bytes 122912 | tf_op jit(solution)/shard_map/ppermute | solution.py:43
  14.8 3.2 collective-permute-done.2
  18.1 1.3 collective-permute-start.4
  19.4 1.2 collective-permute-start.5
  22.3 2.9 collective-permute-start.3
  25.2 4.5 %collective-permute-done.4 = bf16[96,2560]{1,0:T(8,128)(2,1)S(1)} collective-permute-done((bf16[96,2560]{1,0:T(8,128)(2,1)S(1)}, bf16[96,2560]{1,0:T(8,128)(2,1)S(1)}, u32[]{:S(2)}, u32[]{:S(2)}) %collective-permute-start.4) | collective-permute-done | bytes 491552 | tf_op jit(solution)/shard_map/ppermute | solution.py:34
  29.7 1.3 collective-permute-start.6
  31.1 1.3 collective-permute-start.7
  32.4 3.0 collective-permute-done.6
  36.8 3.3 %collective-permute-start.10 = (bf16[4,96,2560]{2,1,0:T(8,128)(2,1)S(1)}, bf16[4,96,2560]{2,1,0:T(8,128)(2,1)S(1)}, u32[]{:S(2)}, u32[]{:S(2)}) collective-permute-start(bf16[4,96,2560]{2,1,0:T(8,128)(2,1)S(1)} %pad_maximum_fusion.3.refs_0_.refs_2_), channel_id=1, source_target_pairs={{0,4},{4,0},{8,12},{12,8},{16,20},{20,16},{24,28},{28,24},{1,5},{5... | collective-permute-start | bytes 5898248 | tf_op jit(solution)/shard_map/ppermute | solution.py:34
  41.9 1.8 collective-permute-done.10.refs_1_.refs_3_
  43.7 2.2 collective-permute-start.17
  47.0 1.5 collective-permute-start.15
  48.6 13.7 %keys.1 = (bf16[1024,768]{1,0:T(8,128)(2,1)}, bf16[1024,768]{1,0:T(8,128)(2,1)}, bf16[1024,768]{1,0:T(8,128)(2,1)}, bf16[1024,1536]{1,0:T(8,128)(2,1)}, bf16[7,1...) custom-call(s32[1]{0:T(128)} %bitcast.me_ref, f32[5]{0:T(128)} %copy-done.21, ...), custom_call_target="tpu_custom_call" | custom-call | flops 11000000512 | bytes 22000000 | tf_op jit(solution)/shard_map/keys/pallas_call | solution.py:709
  62.3 1.3 collective-permute-start.20
  63.9 1.3 collective-permute-start.22
  66.8 10.2 %local.2 = (bf16[1024,768]{1,0:T(8,128)(2,1)}, bf16[1024,1536]{1,0:T(8,128)(2,1)}, f32[1024,768]{1,0:T(8,128)}, f32[1024,768]{1,0:T(8,128)}, bf16[4,12,128,128]{3,2,1,0:T(8,128)(2,1)}, /*index=5*/f32[12,128,128]{2,1,0:T(8,128)}) custom-call(s32[1]{0:T(128)} %bitcast.me_ref, f32[5]{0:T(128)} %copy-done.21, bf16[1024,768]{1,0:T(8,128)(2,1)} %get-tuple-element.116.h_ref, ...), custom_call_target="tpu_custom_call" | custom-call | flops 7500000256 | bytes 15000000 | tf_op jit(solution)/shard_map/local/pallas_call | solution.py:749
  77.1 4.7 %collective-permute-done.13 = bf16[96,1920]{1,0:T(8,128)(2,1)S(1)} collective-permute-done((bf16[96,1920]{1,0:T(8,128)(2,1)S(1)}, bf16[96,1920]{1,0:T(8,128)(2,1)S(1)}, u32[]{:S(2)}, u32[]{:S(2)}) %collective-permute-start.13) | collective-permute-done | bytes 368672 | tf_op jit(solution)/shard_map/ppermute | solution.py:34
  84.7 2.3 collective-permute-start.23
  87.0 7.9 %collective-permute-done.18 = bf16[384,768]{1,0:T(8,128)(2,1)S(1)} collective-permute-done((bf16[384,768]{1,0:T(8,128)(2,1)S(1)}, bf16[384,768]{1,0:T(8,128)(2,1)S(1)}, u32[]{:S(2)}, u32[]{:S(2)}) %collective-permute-start.18) | collective-permute-done | bytes 589856 | tf_op jit(solution)/shard_map/ppermute | solution.py:34
  96.2 10.7 %local.3 = (bf16[1024,768]{1,0:T(8,128)(2,1)}, bf16[1024,1536]{1,0:T(8,128)(2,1)}, f32[1024,768]{1,0:T(8,128)}, f32[1024,768]{1,0:T(8,128)}, bf16[4,12,128,128]{3,2,1,0:T(8,128)(2,1)}, /*index=5*/f32[12,128,128]{2,1,0:T(8,128)}) custom-call(s32[1]{0:T(128)} %bitcast.me_ref, ...), custom_call_target="tpu_custom_call", output_to_operand_aliasing={{0}: (11, {}), {1}: (12, {}), {2}: (13, {}), {3}: (14, {}),... | custom-call | flops 7500000256 | bytes 15000000 | tf_op jit(solution)/shard_map/local/pallas_call | solution.py:749
  108.0 1.8 pad_maximum_fusion.2.refs_2_
  109.7 3.7 %collective-permute-start.25 = (bf16[4,384,768]{2,1,0:T(8,128)(2,1)}, bf16[4,384,768]{2,1,0:T(8,128)(2,1)}, u32[]{:S(2)}, u32[]{:S(2)}) collective-permute-start(bf16[4,384,768]{2,1,0:T(8,128)(2,1)} %pad_maximum_fusion.2.refs_2_), channel_id=1, source_target_pairs={{0,4},{4,0},{8,12},{12,8},{16,20},{20,16},{24,28},{28,24},{1,5},{5... | collective-permute-start | bytes 7077896 | tf_op jit(solution)/shard_map/ppermute | solution.py:34
  113.4 2.2 pad_maximum_fusion.5.refs_4_
  117.1 2.1 collective-permute-done.26.refs_5_
  119.2 43.1 %middle.1 = (bf16[1024,768]{1,0:T(8,128)(2,1)}, bf16[1024,768]{1,0:T(8,128)(2,1)}, bf16[1024,768]{1,0:T(8,128)(2,1)}, bf16[1024,3072]{1,0:T(8,128)(2,1)}, bf16[1...) custom-call(s32[1]{0:T(128)} %bitcast.me_ref, ...), custom_call_target="tpu_custom_call" | custom-call | flops 21500000256 | bytes 43000000 | tf_op jit(solution)/shard_map/middle/pallas_call | solution.py:784
  163.6 1.5 collective-permute-start.29
  165.0 8.3 %convolution_convert_fusion.1 = bf16[768,3072]{1,0:T(8,128)(2,1)S(1)} fusion(bf16[1024,768]{1,0:T(8,128)(2,1)} %get-tuple-element.146, bf16[1024,3072]{1,0:T(8,128)(2,1)} %get-tuple-element.147), kind=kOutput, calls=%fused_computation.2 | convolution fusion | flops 4834197504 | bytes 12582912 | tf_op jit(solution)/shard_map/dot_general | solution.py:30
  173.4 1.4 convolution_convert_fusion.4
  174.8 1.8 dynamic-slice_bitcast_fusion
  177.9 3.9 %pad_maximum_fusion = bf16[2,2,96,3968]{3,2,1,0:T(8,128)(2,1)} fusion(bf16[2,2,96,128]{3,2,1,0:T(8,128)(2,1)S(1)} %get-tuple-element.242, bf16[2,2,96,768]{3,2,1,0:T(8,128)(2,1)} %get-tuple-element.225, bf16[2,2,96,3072]{3,2,1,0:T(8,128)(2,1)} %get-tuple-element.219), kind=kLoop, calls=%fused_computation.8 | loop fusion | flops 9142272 | bytes 6094848 | tf_op jit(solution)/shard_map/concatenate | solution.py:105
  183.0 2.2 pad_maximum_fusion.6.refs_0_
  185.2 8.5 %convolution_convert_fusion = bf16[3072,768]{1,0:T(8,128)(2,1)S(1)} fusion(bf16[1024,3072]{1,0:T(8,128)(2,1)} %get-tuple-element.156, bf16[1,1024,768]{2,1,0:T(8,128)(2,1)S(1)} %copy-done.23), kind=kOutput, calls=%fused_computation.1 | convolution fusion | flops 4834197504 | bytes 12582912 | tf_op jit(solution)/shard_map/dot_general | solution.py:30
  193.7 1.7 dynamic-slice_bitcast_fusion.1
  195.4 1.3 copy-done
  199.0 2.4 add_convert_fusion
  201.4 1.2 dynamic-slice_bitcast_fusion.3
  202.6 2.2 fusion
  207.1 15.0 %back.2 = (bf16[1024,1152]{1,0:T(8,128)(2,1)}, bf16[384,128]{1,0:T(8,128)(2,1)}) custom-call(s32[1]{0:T(128)} %bitcast.me_ref, f32[8]{0:T(128)} %bitcast.240, f32[5]{0:T(128)} %copy-done.21, bf16[1024,768]{1,0:T(8,128)(2,1)} %get-tuple-element.160.q_ref, bf16[1024,768]{1,0:T(8,128)(2,1)} %get-tuple-element.161.k_ref, ...), custom_call_target="tpu_custom_call" | custom-call | flops 9500000256 | bytes 19000000 | tf_op jit(solution)/shard_map/back/pallas_call | solution.py:846
  222.2 4.4 %convolution_convert_fusion.3 = bf16[768,1152]{1,0:T(8,128)(2,1)S(1)} fusion(bf16[1024,768]{1,0:T(8,128)(2,1)} %get-tuple-element.116.h_ref, bf16[1024,1152]{1,0:T(8,128)(2,1)} %get-tuple-element.165.refs_0_), kind=kOutput, calls=%fused_computation.7 | convolution fusion | flops 1812824064 | bytes 5701632 | tf_op jit(solution)/shard_map/dot_general | solution.py:30
  226.5 1.4 dynamic-slice_bitcast_fusion.6
  228.0 5.9 %collective-permute-done.32 = bf16[2,384,768]{2,1,0:T(8,128)(2,1)} collective-permute-done((bf16[2,384,768]{2,1,0:T(8,128)(2,1)}, bf16[2,384,768]{2,1,0:T(8,128)(2,1)}, u32[]{:S(2)}, u32[]{:S(2)}) %collective-permute-start.32) | collective-permute-done | bytes 1179680 | tf_op jit(solution)/shard_map/ppermute | solution.py:34
  233.8 1.5 fusion.2
  236.7 14.9 %back.3 = (bf16[1024,1152]{1,0:T(8,128)(2,1)}, bf16[384,128]{1,0:T(8,128)(2,1)}) custom-call(s32[1]{0:T(128)} %bitcast.me_ref, f32[8]{0:T(128)} %bitcast.241, f32[5]{0:T(128)} %copy-done.21, bf16[1024,768]{1,0:T(8,128)(2,1)} %get-tuple-element.160.q_ref, bf16[1024,768]{1,0:T(8,128)(2,1)} %get-tuple-element.161.k_ref, ...), custom_call_target="tpu_custom_call" | custom-call | flops 9500000256 | bytes 19000000 | tf_op jit(solution)/shard_map/back/pallas_call | solution.py:846
  252.6 4.4 %convolution_convert_fusion.2 = bf16[768,1152]{1,0:T(8,128)(2,1)S(1)} fusion(bf16[1024,768]{1,0:T(8,128)(2,1)} %get-tuple-element.116.h_ref, bf16[1024,1152]{1,0:T(8,128)(2,1)} %get-tuple-element.168.refs_1_), kind=kOutput, calls=%fused_computation.6 | convolution fusion | flops 1812824064 | bytes 5701632 | tf_op jit(solution)/shard_map/dot_general | solution.py:30
  258.4 1.5 pad_maximum_fusion.4
  261.0 1.7 fusion.1
  266.6 2.6 collective-permute-start.38
  269.2 12.1 %enter.1 = (f32[1024,768]{1,0:T(8,128)}, f32[8,768]{1,0:T(8,128)}) custom-call(s32[1]{0:T(128)} %bitcast.me_ref, bf16[1024,768]{1,0:T(8,128)(2,1)} %bitcast.245, f32[1024,768]{1,0:T(8,128)} %get-tuple-element.174.dr_ref, f32[8,768]{1,0:T(8,128)} %get-tuple-element.105.gb_ref, bf16[1024,1152]{1,0:T(8,128)(2,1)} %get-tuple-element.165.refs_0_, ...), custom_call_target="tpu_custom_call" | custom-call | flops 5500000256 | bytes 11000000 | tf_op jit(solution)/shard_map/enter/pallas_call | solution.py:886
  283.5 1.8 fusion.16
  285.3 2.2 add_convert_fusion.1
  288.3 1.3 collective-permute-start.43
  289.6 1.3 fusion.3
  290.9 1.8 collective-permute-start.49
  292.7 1.5 collective-permute-start.50
  294.2 5.9 %collective-permute-done.40 = bf16[2,96,1280]{2,1,0:T(8,128)(2,1)S(1)} collective-permute-done((bf16[2,96,1280]{2,1,0:T(8,128)(2,1)S(1)}, bf16[2,96,1280]{2,1,0:T(8,128)(2,1)S(1)}, u32[]{:S(2)}, u32[]{:S(2)}) %collective-permute-start.40) | collective-permute-done | bytes 491552 | tf_op jit(solution)/shard_map/ppermute | solution.py:34
  302.3 4.3 %collective-permute-done.41 = bf16[96,1280]{1,0:T(8,128)(2,1)S(1)} collective-permute-done((bf16[96,1280]{1,0:T(8,128)(2,1)S(1)}, bf16[96,1280]{1,0:T(8,128)(2,1)S(1)}, u32[]{:S(2)}, u32[]{:S(2)}) %collective-permute-start.41) | collective-permute-done | bytes 245792 | tf_op jit(solution)/shard_map/ppermute | solution.py:34
  308.5 2.0 collective-permute-done.51
  313.3 1.4 collective-permute-start.47
  315.9 1.7 collective-permute-done.46
  317.6 7.4 %collective-permute-done.47 = bf16[24,2560]{1,0:T(8,128)(2,1)S(1)} collective-permute-done((bf16[24,2560]{1,0:T(8,128)(2,1)S(1)}, bf16[24,2560]{1,0:T(8,128)(2,1)S(1)}, u32[]{:S(2)}, u32[]{:S(2)}) %collective-permute-start.47) | collective-permute-done | bytes 122912 | tf_op jit(solution)/shard_map/ppermute | solution.py:158
  (237 shorter events, 48.0 us)
Async XLA Ops:
  4.2 17.6 %copy-start.15 = (bf16[24,3072]{1,0:T(8,128)(2,1)S(1)}, bf16[24,3072]{1,0:T(8,128)(2,1)}, u32[]{:S(2)}) copy-start(bf16[24,3072]{1,0:T(8,128)(2,1)} %param.17) | copy-start | bytes 442372
  4.2 17.6 %copy-start.17 = (bf16[24,768]{1,0:T(8,128)(2,1)S(1)}, bf16[24,768]{1,0:T(8,128)(2,1)}, u32[]{:S(2)}) copy-start(bf16[24,768]{1,0:T(8,128)(2,1)} %param.16) | copy-start | bytes 110596
  5.2 6.0 %collective-permute-start = (bf16[24,2560]{1,0:T(8,128)(2,1)S(1)}, bf16[24,2560]{1,0:T(8,128)(2,1)S(1)}, u32[]{:S(2)}, u32[]{:S(2)}) collective-permute-start(bf16[24,2560]{1,0:T(8,128)(2,1)S(1)} %concatenate.61), channel_id=1, source_target_pairs={{0,3},{1,0},{2,1},{3,2},{4,7},{5,4},{6,5},{7,6},{8,11},{9,8},{10,9... | collective-permute-start | bytes 368648 | tf_op jit(solution)/shard_map/ppermute | solution.py:43
  5.3 9.5 %collective-permute-start.1 = (bf16[24,2560]{1,0:T(8,128)(2,1)S(1)}, bf16[24,2560]{1,0:T(8,128)(2,1)S(1)}, u32[]{:S(2)}, u32[]{:S(2)}) collective-permute-start(bf16[24,2560]{1,0:T(8,128)(2,1)S(1)} %concatenate.61), channel_id=1, source_target_pairs={{0,2},{1,3},{2,0},{3,1},{4,6},{5,7},{6,4},{7,5},{8,10},{9,11},{10,... | collective-permute-start | bytes 368648 | tf_op jit(solution)/shard_map/ppermute | solution.py:43
  7.7 10.2 %collective-permute-start.2 = (bf16[24,2560]{1,0:T(8,128)(2,1)S(1)}, bf16[24,2560]{1,0:T(8,128)(2,1)S(1)}, u32[]{:S(2)}, u32[]{:S(2)}) collective-permute-start(bf16[24,2560]{1,0:T(8,128)(2,1)S(1)} %concatenate.61), channel_id=1, source_target_pairs={{0,1},{1,2},{2,3},{3,0},{4,5},{5,6},{6,7},{7,4},{8,9},{9,10},{10,1... | collective-permute-start | bytes 368648 | tf_op jit(solution)/shard_map/ppermute | solution.py:43
  11.2 18.6 %copy-start.21 = (f32[5]{0:T(128)}, f32[5]{0:T(128)S(1)}, u32[]{:S(2)}) copy-start(f32[5]{0:T(128)S(1)} %pad_maximum_fusion.15.cend_ref) | copy-start | bytes 64
  18.1 11.6 %collective-permute-start.4 = (bf16[96,2560]{1,0:T(8,128)(2,1)S(1)}, bf16[96,2560]{1,0:T(8,128)(2,1)S(1)}, u32[]{:S(2)}, u32[]{:S(2)}) collective-permute-start(bf16[96,2560]{1,0:T(8,128)(2,1)S(1)} %constant_dynamic-slice_fusion.3), channel_id=1, source_target_pairs={{0,8},{4,12},{8,0},{12,4},{16,24},{20,28},{24,16},{28,20},{1,9},{5... | collective-permute-start | bytes 1474568 | tf_op jit(solution)/shard_map/ppermute | solution.py:34
  19.4 11.7 %collective-permute-start.5 = (bf16[96,2560]{1,0:T(8,128)(2,1)S(1)}, bf16[96,2560]{1,0:T(8,128)(2,1)S(1)}, u32[]{:S(2)}, u32[]{:S(2)}) collective-permute-start(bf16[96,2560]{1,0:T(8,128)(2,1)S(1)} %constant_dynamic-slice_fusion.3), channel_id=1, source_target_pairs={{0,16},{4,20},{8,24},{12,28},{16,0},{20,4},{24,8},{28,12},{1,17},{... | collective-permute-start | bytes 1474568 | tf_op jit(solution)/shard_map/ppermute | solution.py:34
  20.7 16.1 %copy-start.19 = (f32[1,1,4,256]{3,1,2,0:T(1,128)}, f32[1,1,4,256]{3,1,2,0:T(1,128)S(1)}, u32[]{:S(2)}) copy-start(f32[1,1,4,256]{3,1,2,0:T(1,128)S(1)} %copy.104) | copy-start | bytes 12292
  21.8 19.3 %collective-permute-start.8 = (bf16[24,3840]{1,0:T(8,128)(2,1)S(1)}, bf16[24,3840]{1,0:T(8,128)(2,1)S(1)}, u32[]{:S(2)}, u32[]{:S(2)}) collective-permute-start(bf16[24,3840]{1,0:T(8,128)(2,1)S(1)} %pad_maximum_fusion.10), channel_id=1, source_target_pairs={{0,2},{1,3},{2,0},{3,1},{4,6},{5,7},{6,4},{7,5},{8,10},{9,11},{10,... | collective-permute-start | bytes 552968 | tf_op jit(solution)/shard_map/ppermute | solution.py:43
  22.3 18.7 %collective-permute-start.3 = (bf16[24,3840]{1,0:T(8,128)(2,1)S(1)}, bf16[24,3840]{1,0:T(8,128)(2,1)S(1)}, u32[]{:S(2)}, u32[]{:S(2)}) collective-permute-start(bf16[24,3840]{1,0:T(8,128)(2,1)S(1)} %pad_maximum_fusion.10), channel_id=1, source_target_pairs={{0,3},{1,0},{2,1},{3,2},{4,7},{5,4},{6,5},{7,6},{8,11},{9,8},{10,9... | collective-permute-start | bytes 552968 | tf_op jit(solution)/shard_map/ppermute | solution.py:43
  25.2 15.8 %collective-permute-start.9 = (bf16[24,3840]{1,0:T(8,128)(2,1)S(1)}, bf16[24,3840]{1,0:T(8,128)(2,1)S(1)}, u32[]{:S(2)}, u32[]{:S(2)}) collective-permute-start(bf16[24,3840]{1,0:T(8,128)(2,1)S(1)} %pad_maximum_fusion.10), channel_id=1, source_target_pairs={{0,1},{1,2},{2,3},{3,0},{4,5},{5,6},{6,7},{7,4},{8,9},{9,10},{10,1... | collective-permute-start | bytes 552968 | tf_op jit(solution)/shard_map/ppermute | solution.py:43
  29.7 5.7 %collective-permute-start.6 = (bf16[96,1280]{1,0:T(8,128)(2,1)S(1)}, bf16[96,1280]{1,0:T(8,128)(2,1)S(1)}, u32[]{:S(2)}, u32[]{:S(2)}) collective-permute-start(bf16[96,1280]{1,0:T(8,128)(2,1)S(1)} %slice.135), channel_id=1, source_target_pairs={{0,16},{4,20},{8,24},{12,28},{16,0},{20,4},{24,8},{28,12},{1,17},{... | collective-permute-start | bytes 737288 | tf_op jit(solution)/shard_map/ppermute | solution.py:34
  31.1 5.4 %collective-permute-start.7 = (bf16[96,1280]{1,0:T(8,128)(2,1)S(1)}, bf16[96,1280]{1,0:T(8,128)(2,1)S(1)}, u32[]{:S(2)}, u32[]{:S(2)}) collective-permute-start(bf16[96,1280]{1,0:T(8,128)(2,1)S(1)} %slice.136), channel_id=1, source_target_pairs={{0,8},{4,12},{8,0},{12,4},{16,24},{20,28},{24,16},{28,20},{1,9},{5... | collective-permute-start | bytes 737288 | tf_op jit(solution)/shard_map/ppermute | solution.py:34
  36.8 6.9 %collective-permute-start.10 = (bf16[4,96,2560]{2,1,0:T(8,128)(2,1)S(1)}, bf16[4,96,2560]{2,1,0:T(8,128)(2,1)S(1)}, u32[]{:S(2)}, u32[]{:S(2)}) collective-permute-start(bf16[4,96,2560]{2,1,0:T(8,128)(2,1)S(1)} %pad_maximum_fusion.3.refs_0_.refs_2_), channel_id=1, source_target_pairs={{0,4},{4,0},{8,12},{12,8},{16,20},{20,16},{24,28},{28,24},{1,5},{5... | collective-permute-start | bytes 5898248 | tf_op jit(solution)/shard_map/ppermute | solution.py:34
  41.3 21.0 %collective-permute-start.11 = (bf16[96,3840]{1,0:T(8,128)(2,1)S(1)}, bf16[96,3840]{1,0:T(8,128)(2,1)S(1)}, u32[]{:S(2)}, u32[]{:S(2)}) collective-permute-start(bf16[96,3840]{1,0:T(8,128)(2,1)S(1)} %constant_dynamic-slice_fusion.2), channel_id=1, source_target_pairs={{0,8},{4,12},{8,0},{12,4},{16,24},{20,28},{24,16},{28,20},{1,9},{5... | collective-permute-start | bytes 2211848 | tf_op jit(solution)/shard_map/ppermute | solution.py:34
  41.6 22.0 %collective-permute-start.12 = (bf16[96,3840]{1,0:T(8,128)(2,1)S(1)}, bf16[96,3840]{1,0:T(8,128)(2,1)S(1)}, u32[]{:S(2)}, u32[]{:S(2)}) collective-permute-start(bf16[96,3840]{1,0:T(8,128)(2,1)S(1)} %constant_dynamic-slice_fusion.2), channel_id=1, source_target_pairs={{0,16},{4,20},{8,24},{12,28},{16,0},{20,4},{24,8},{28,12},{1,17},{... | collective-permute-start | bytes 2211848 | tf_op jit(solution)/shard_map/ppermute | solution.py:34
  43.7 20.2 %collective-permute-start.17 = (bf16[96,768]{1,0:T(8,128)(2,1)S(1)}, bf16[96,768]{1,0:T(8,128)(2,1)S(1)}, u32[]{:S(2)}, u32[]{:S(2)}) collective-permute-start(bf16[96,768]{1,0:T(8,128)(2,1)S(1)} %copy-done.12), channel_id=1, source_target_pairs={{0,1},{1,2},{2,3},{3,0},{4,5},{5,6},{6,7},{7,4},{8,9},{9,10},{10,1... | collective-permute-start | bytes 442376 | tf_op jit(solution)/shard_map/ppermute | solution.py:43
  45.9 19.3 %collective-permute-start.16 = (bf16[96,768]{1,0:T(8,128)(2,1)S(1)}, bf16[96,768]{1,0:T(8,128)(2,1)S(1)}, u32[]{:S(2)}, u32[]{:S(2)}) collective-permute-start(bf16[96,768]{1,0:T(8,128)(2,1)S(1)} %copy-done.12), channel_id=1, source_target_pairs={{0,2},{1,3},{2,0},{3,1},{4,6},{5,7},{6,4},{7,5},{8,10},{9,11},{10,... | collective-permute-start | bytes 442376 | tf_op jit(solution)/shard_map/ppermute | solution.py:43
  47.0 19.3 %collective-permute-start.15 = (bf16[96,768]{1,0:T(8,128)(2,1)S(1)}, bf16[96,768]{1,0:T(8,128)(2,1)S(1)}, u32[]{:S(2)}, u32[]{:S(2)}) collective-permute-start(bf16[96,768]{1,0:T(8,128)(2,1)S(1)} %copy-done.12), channel_id=1, source_target_pairs={{0,3},{1,0},{2,1},{3,2},{4,7},{5,4},{6,5},{7,6},{8,11},{9,8},{10,9... | collective-permute-start | bytes 442376 | tf_op jit(solution)/shard_map/ppermute | solution.py:43
  62.3 22.4 %collective-permute-start.20 = (bf16[7,128,128]{2,1,0:T(8,128)(2,1)}, bf16[7,128,128]{2,1,0:T(8,128)(2,1)}, u32[]{:S(2)}, u32[]{:S(2)}) collective-permute-start(bf16[7,128,128]{2,1,0:T(8,128)(2,1)} %get-tuple-element.140), channel_id=1, source_target_pairs={{0,8},{4,12},{8,0},{12,4},{16,24},{20,28},{24,16},{28,20},{1,9},{5... | collective-permute-start | bytes 688136 | tf_op jit(solution)/shard_map/ppermute | solution.py:34
  63.6 23.5 %collective-permute-start.21 = (bf16[7,128,128]{2,1,0:T(8,128)(2,1)}, bf16[7,128,128]{2,1,0:T(8,128)(2,1)}, u32[]{:S(2)}, u32[]{:S(2)}) collective-permute-start(bf16[7,128,128]{2,1,0:T(8,128)(2,1)} %get-tuple-element.140), channel_id=1, source_target_pairs={{0,16},{4,20},{8,24},{12,28},{16,0},{20,4},{24,8},{28,12},{1,17},{... | collective-permute-start | bytes 688136 | tf_op jit(solution)/shard_map/ppermute | solution.py:34
  63.9 23.2 %collective-permute-start.22 = (bf16[7,128,128]{2,1,0:T(8,128)(2,1)}, bf16[7,128,128]{2,1,0:T(8,128)(2,1)}, u32[]{:S(2)}, u32[]{:S(2)}) collective-permute-start(bf16[7,128,128]{2,1,0:T(8,128)(2,1)} %get-tuple-element.140), channel_id=1, source_target_pairs={{0,24},{4,28},{8,16},{12,20},{16,8},{20,12},{24,0},{28,4},{1,25},{... | collective-permute-start | bytes 688136 | tf_op jit(solution)/shard_map/ppermute | solution.py:34
  65.2 16.6 %collective-permute-start.13 = (bf16[96,1920]{1,0:T(8,128)(2,1)S(1)}, bf16[96,1920]{1,0:T(8,128)(2,1)S(1)}, u32[]{:S(2)}, u32[]{:S(2)}) collective-permute-start(bf16[96,1920]{1,0:T(8,128)(2,1)S(1)} %slice.112), channel_id=1, source_target_pairs={{0,8},{4,12},{8,0},{12,4},{16,24},{20,28},{24,16},{28,20},{1,9},{5... | collective-permute-start | bytes 1105928 | tf_op jit(solution)/shard_map/ppermute | solution.py:34
  66.4 16.6 %collective-permute-start.14 = (bf16[96,1920]{1,0:T(8,128)(2,1)S(1)}, bf16[96,1920]{1,0:T(8,128)(2,1)}, u32[]{:S(2)}, u32[]{:S(2)}) collective-permute-start(bf16[96,1920]{1,0:T(8,128)(2,1)S(1)} %slice.113), channel_id=1, source_target_pairs={{0,16},{4,20},{8,24},{12,28},{16,0},{20,4},{24,8},{28,12},{1,17},{... | collective-permute-start | bytes 1105928 | tf_op jit(solution)/shard_map/ppermute | solution.py:34
  77.1 7.2 %copy-start.9 = (bf16[96,3840]{1,0:T(8,128)(2,1)S(1)}, bf16[96,3840]{1,0:T(8,128)(2,1)}, u32[]{:S(2)}) copy-start(bf16[96,3840]{1,0:T(8,128)(2,1)} %copy-done.8) | copy-start | bytes 2211844
  77.1 7.2 %copy-start.11 = (bf16[96,3840]{1,0:T(8,128)(2,1)S(1)}, bf16[96,3840]{1,0:T(8,128)(2,1)}, u32[]{:S(2)}) copy-start(bf16[96,3840]{1,0:T(8,128)(2,1)} %copy-done.10) | copy-start | bytes 2211844
  81.8 13.2 %collective-permute-start.18 = (bf16[384,768]{1,0:T(8,128)(2,1)S(1)}, bf16[384,768]{1,0:T(8,128)(2,1)S(1)}, u32[]{:S(2)}, u32[]{:S(2)}) collective-permute-start(bf16[384,768]{1,0:T(8,128)(2,1)S(1)} %constant_dynamic-slice_fusion), channel_id=1, source_target_pairs={{0,8},{4,12},{8,0},{12,4},{16,24},{20,28},{24,16},{28,20},{1,9},{5... | collective-permute-start | bytes 1769480 | tf_op jit(solution)/shard_map/ppermute | solution.py:34
  83.0 12.9 %collective-permute-start.19 = (bf16[384,768]{1,0:T(8,128)(2,1)S(1)}, bf16[384,768]{1,0:T(8,128)(2,1)S(1)}, u32[]{:S(2)}, u32[]{:S(2)}) collective-permute-start(bf16[384,768]{1,0:T(8,128)(2,1)S(1)} %constant_dynamic-slice_fusion), channel_id=1, source_target_pairs={{0,16},{4,20},{8,24},{12,28},{16,0},{20,4},{24,8},{28,12},{1,17},{... | collective-permute-start | bytes 1769480 | tf_op jit(solution)/shard_map/ppermute | solution.py:34
  84.7 22.2 %copy-start.6 = (bf16[4,96,3840]{2,1,0:T(8,128)(2,1)}, bf16[4,96,3840]{2,1,0:T(8,128)(2,1)S(1)}, u32[]{:S(2)}) copy-start(bf16[4,96,3840]{2,1,0:T(8,128)(2,1)S(1)} %pad_maximum_fusion.1.refs_0_) | copy-start | bytes 8847364
  84.7 34.5 %collective-permute-start.23 = (bf16[4,96,3840]{2,1,0:T(8,128)(2,1)S(1)}, bf16[4,96,3840]{2,1,0:T(8,128)(2,1)}, u32[]{:S(2)}, u32[]{:S(2)}) collective-permute-start(bf16[4,96,3840]{2,1,0:T(8,128)(2,1)S(1)} %pad_maximum_fusion.1.refs_0_), channel_id=1, source_target_pairs={{0,4},{4,0},{8,12},{12,8},{16,20},{20,16},{24,28},{28,24},{1,5},{5... | collective-permute-start | bytes 8847368 | tf_op jit(solution)/shard_map/ppermute | solution.py:34
  95.9 12.1 %collective-permute-start.24 = (bf16[384,768]{1,0:T(8,128)(2,1)S(1)}, bf16[384,768]{1,0:T(8,128)(2,1)S(1)}, u32[]{:S(2)}, u32[]{:S(2)}) collective-permute-start(bf16[384,768]{1,0:T(8,128)(2,1)S(1)} %collective-permute-done.19), channel_id=1, source_target_pairs={{0,8},{4,12},{8,0},{12,4},{16,24},{20,28},{24,16},{28,20},{1,9},{5... | collective-permute-start | bytes 1769480 | tf_op jit(solution)/shard_map/ppermute | solution.py:34
  108.0 5.4 %copy-start.13 = (bf16[7,128,128]{2,1,0:T(8,128)(2,1)S(1)}, bf16[7,128,128]{2,1,0:T(8,128)(2,1)}, u32[]{:S(2)}) copy-start(bf16[7,128,128]{2,1,0:T(8,128)(2,1)} %get-tuple-element.140) | copy-start | bytes 688132
  109.7 9.5 %collective-permute-start.25 = (bf16[4,384,768]{2,1,0:T(8,128)(2,1)}, bf16[4,384,768]{2,1,0:T(8,128)(2,1)}, u32[]{:S(2)}, u32[]{:S(2)}) collective-permute-start(bf16[4,384,768]{2,1,0:T(8,128)(2,1)} %pad_maximum_fusion.2.refs_2_), channel_id=1, source_target_pairs={{0,4},{4,0},{8,12},{12,8},{16,20},{20,16},{24,28},{28,24},{1,5},{5... | collective-permute-start | bytes 7077896 | tf_op jit(solution)/shard_map/ppermute | solution.py:34
  115.7 3.6 %collective-permute-start.26 = (bf16[4,7,128,128]{3,2,1,0:T(8,128)(2,1)}, bf16[4,7,128,128]{3,2,1,0:T(8,128)(2,1)}, u32[]{:S(2)}, u32[]{:S(2)}) collective-permute-start(bf16[4,7,128,128]{3,2,1,0:T(8,128)(2,1)} %pad_maximum_fusion.5.refs_4_), channel_id=1, source_target_pairs={{0,4},{4,0},{8,12},{12,8},{16,20},{20,16},{24,28},{28,24},{1,5},{5... | collective-permute-start | bytes 2752520 | tf_op jit(solution)/shard_map/ppermute | solution.py:34
  162.3 20.6 %collective-permute-start.27 = (bf16[7,128,128]{2,1,0:T(8,128)(2,1)}, bf16[7,128,128]{2,1,0:T(8,128)(2,1)}, u32[]{:S(2)}, u32[]{:S(2)}) collective-permute-start(bf16[7,128,128]{2,1,0:T(8,128)(2,1)} %get-tuple-element.152), channel_id=1, source_target_pairs={{0,8},{4,12},{8,0},{12,4},{16,24},{20,28},{24,16},{28,20},{1,9},{5... | collective-permute-start | bytes 688136 | tf_op jit(solution)/shard_map/ppermute | solution.py:34
  162.7 20.3 %collective-permute-start.28 = (bf16[7,128,128]{2,1,0:T(8,128)(2,1)}, bf16[7,128,128]{2,1,0:T(8,128)(2,1)}, u32[]{:S(2)}, u32[]{:S(2)}) collective-permute-start(bf16[7,128,128]{2,1,0:T(8,128)(2,1)} %get-tuple-element.152), channel_id=1, source_target_pairs={{0,16},{4,20},{8,24},{12,28},{16,0},{20,4},{24,8},{28,12},{1,17},{... | collective-permute-start | bytes 688136 | tf_op jit(solution)/shard_map/ppermute | solution.py:34
  163.6 19.4 %collective-permute-start.29 = (bf16[7,128,128]{2,1,0:T(8,128)(2,1)}, bf16[7,128,128]{2,1,0:T(8,128)(2,1)}, u32[]{:S(2)}, u32[]{:S(2)}) collective-permute-start(bf16[7,128,128]{2,1,0:T(8,128)(2,1)} %get-tuple-element.152), channel_id=1, source_target_pairs={{0,24},{4,28},{8,16},{12,20},{16,8},{20,12},{24,0},{28,4},{1,25},{... | collective-permute-start | bytes 688136 | tf_op jit(solution)/shard_map/ppermute | solution.py:34
  165.0 8.3 %copy-start.24 = (bf16[1024,768]{1,0:T(8,128)(2,1)S(1)}, bf16[1024,768]{1,0:T(8,128)(2,1)}, u32[]{:S(2)}) copy-start(bf16[1024,768]{1,0:T(8,128)(2,1)} %get-tuple-element.148) | copy-start | bytes 4718596
  165.0 8.3 %copy-start.25 = (bf16[1024,768]{1,0:T(8,128)(2,1)S(1)}, bf16[1024,768]{1,0:T(8,128)(2,1)}, u32[]{:S(2)}) copy-start(bf16[1024,768]{1,0:T(8,128)(2,1)} %get-tuple-element.149) | copy-start | bytes 4718596
  177.9 7.3 %copy-start.23 = (bf16[1,1024,768]{2,1,0:T(8,128)(2,1)S(1)}, bf16[1,1024,768]{2,1,0:T(8,128)(2,1)}, u32[]{:S(2)}) copy-start(bf16[1,1024,768]{2,1,0:T(8,128)(2,1)} %param.19) | copy-start | bytes 4718596
  181.7 17.3 %collective-permute-start.31 = (bf16[2,2,96,3968]{3,2,1,0:T(8,128)(2,1)}, bf16[2,2,96,3968]{3,2,1,0:T(8,128)(2,1)}, u32[]{:S(2)}, u32[]{:S(2)}) collective-permute-start(bf16[2,2,96,3968]{3,2,1,0:T(8,128)(2,1)} %pad_maximum_fusion), channel_id=1, source_target_pairs={{0,4},{4,0},{8,12},{12,8},{16,20},{20,16},{24,28},{28,24},{1,5},{5... | collective-permute-start | bytes 9142280 | tf_op jit(solution)/shard_map/ppermute | solution.py:34
  185.2 12.9 %collective-permute-start.33 = (bf16[4,7,128,128]{3,2,1,0:T(8,128)(2,1)}, bf16[4,7,128,128]{3,2,1,0:T(8,128)(2,1)}, u32[]{:S(2)}, u32[]{:S(2)}) collective-permute-start(bf16[4,7,128,128]{3,2,1,0:T(8,128)(2,1)} %pad_maximum_fusion.6.refs_0_), channel_id=1, source_target_pairs={{0,4},{4,0},{8,12},{12,8},{16,20},{20,16},{24,28},{28,24},{1,5},{5... | collective-permute-start | bytes 2752520 | tf_op jit(solution)/shard_map/ppermute | solution.py:34
  196.7 5.9 %collective-permute-start.30 = (bf16[2,2,384,768]{3,2,1,0:T(8,128)(2,1)}, bf16[2,2,384,768]{3,2,1,0:T(8,128)(2,1)}, u32[]{:S(2)}, u32[]{:S(2)}) collective-permute-start(bf16[2,2,384,768]{3,2,1,0:T(8,128)(2,1)} %dynamic-slice_bitcast_fusion.1), channel_id=1, source_target_pairs={{0,4},{4,0},{8,12},{12,8},{16,20},{20,16},{24,28},{28,24},{1,5},{5... | collective-permute-start | bytes 7077896 | tf_op jit(solution)/shard_map/ppermute | solution.py:34
  206.0 27.8 %collective-permute-start.32 = (bf16[2,384,768]{2,1,0:T(8,128)(2,1)}, bf16[2,384,768]{2,1,0:T(8,128)(2,1)}, u32[]{:S(2)}, u32[]{:S(2)}) collective-permute-start(bf16[2,384,768]{2,1,0:T(8,128)(2,1)} %dynamic-slice_bitcast_fusion.4), channel_id=1, source_target_pairs={{0,8},{4,12},{8,0},{12,4},{16,24},{20,28},{24,16},{28,20},{1,9},{5... | collective-permute-start | bytes 3538952 | tf_op jit(solution)/shard_map/ppermute | solution.py:34
  206.3 54.7 %collective-permute-start.35 = (bf16[2,96,3968]{2,1,0:T(8,128)(2,1)}, bf16[2,96,3968]{2,1,0:T(8,128)(2,1)}, u32[]{:S(2)}, u32[]{:S(2)}) collective-permute-start(bf16[2,96,3968]{2,1,0:T(8,128)(2,1)} %dynamic-slice_bitcast_fusion.3), channel_id=1, source_target_pairs={{0,16},{4,20},{8,24},{12,28},{16,0},{20,4},{24,8},{28,12},{1,17},{... | collective-permute-start | bytes 4571144 | tf_op jit(solution)/shard_map/ppermute | solution.py:34
  236.4 15.2 %copy-start.16 = (bf16[384,128]{1,0:T(8,128)(2,1)S(1)}, bf16[384,128]{1,0:T(8,128)(2,1)}, u32[]{:S(2)}) copy-start(bf16[384,128]{1,0:T(8,128)(2,1)} %get-tuple-element.169) | copy-start | bytes 294916
  236.5 28.2 %collective-permute-start.34 = (bf16[384,768]{1,0:T(8,128)(2,1)S(1)}, bf16[384,768]{1,0:T(8,128)(2,1)}, u32[]{:S(2)}, u32[]{:S(2)}) collective-permute-start(bf16[384,768]{1,0:T(8,128)(2,1)S(1)} %dynamic-slice_bitcast_fusion.10), channel_id=1, source_target_pairs={{0,16},{4,20},{8,24},{12,28},{16,0},{20,4},{24,8},{28,12},{1,17},{... | collective-permute-start | bytes 1769480 | tf_op jit(solution)/shard_map/ppermute | solution.py:34
  259.8 25.4 %collective-permute-start.36 = (bf16[2,2,96,2432]{3,2,1,0:T(8,128)(2,1)}, bf16[2,2,96,2432]{3,2,1,0:T(8,128)(2,1)}, u32[]{:S(2)}, u32[]{:S(2)}) collective-permute-start(bf16[2,2,96,2432]{3,2,1,0:T(8,128)(2,1)} %pad_maximum_fusion.4), channel_id=1, source_target_pairs={{0,4},{4,0},{8,12},{12,8},{16,20},{20,16},{24,28},{28,24},{1,5},{5... | collective-permute-start | bytes 5603336 | tf_op jit(solution)/shard_map/ppermute | solution.py:34
  263.7 25.9 %collective-permute-start.48 = (bf16[96,3968]{1,0:T(8,128)(2,1)}, bf16[96,3968]{1,0:T(8,128)(2,1)}, u32[]{:S(2)}, u32[]{:S(2)}) collective-permute-start(bf16[96,3968]{1,0:T(8,128)(2,1)} %dynamic-slice_bitcast_fusion.9), channel_id=1, source_target_pairs={{0,8},{4,12},{8,0},{12,4},{16,24},{20,28},{24,16},{28,20},{1,9},{5... | collective-permute-start | bytes 2285576 | tf_op jit(solution)/shard_map/ppermute | solution.py:34
  266.6 15.8 %collective-permute-start.37 = (bf16[96,768]{1,0:T(8,128)(2,1)}, bf16[96,768]{1,0:T(8,128)(2,1)S(1)}, u32[]{:S(2)}, u32[]{:S(2)}) collective-permute-start(bf16[96,768]{1,0:T(8,128)(2,1)} %get-tuple-element.229), channel_id=1, source_target_pairs={{0,1},{1,2},{2,3},{3,0},{4,5},{5,6},{6,7},{7,4},{8,9},{9,10},{10,1... | collective-permute-start | bytes 442376 | tf_op jit(solution)/shard_map/ppermute | solution.py:158
  266.6 16.9 %collective-permute-start.38 = (bf16[96,768]{1,0:T(8,128)(2,1)}, bf16[96,768]{1,0:T(8,128)(2,1)}, u32[]{:S(2)}, u32[]{:S(2)}) collective-permute-start(bf16[96,768]{1,0:T(8,128)(2,1)} %get-tuple-element.231), channel_id=1, source_target_pairs={{0,2},{1,3},{2,0},{3,1},{4,6},{5,7},{6,4},{7,5},{8,10},{9,11},{10,... | collective-permute-start | bytes 442376 | tf_op jit(solution)/shard_map/ppermute | solution.py:158
  269.2 14.3 %collective-permute-start.39 = (bf16[96,768]{1,0:T(8,128)(2,1)}, bf16[96,768]{1,0:T(8,128)(2,1)}, u32[]{:S(2)}, u32[]{:S(2)}) collective-permute-start(bf16[96,768]{1,0:T(8,128)(2,1)} %get-tuple-element.230), channel_id=1, source_target_pairs={{0,3},{1,0},{2,1},{3,2},{4,7},{5,4},{6,5},{7,6},{8,11},{9,8},{10,9... | collective-permute-start | bytes 442376 | tf_op jit(solution)/shard_map/ppermute | solution.py:158
  282.5 5.7 %collective-permute-start.42 = (bf16[2,2,96,128]{3,2,1,0:T(8,128)(2,1)S(1)}, bf16[2,2,96,128]{3,2,1,0:T(8,128)(2,1)S(1)}, u32[]{:S(2)}, u32[]{:S(2)}) collective-permute-start(bf16[2,2,96,128]{3,2,1,0:T(8,128)(2,1)S(1)} %dynamic-slice_bitcast_fusion.25), channel_id=1, source_target_pairs={{0,4},{4,0},{8,12},{12,8},{16,20},{20,16},{24,28},{28,24},{1,5},{5... | collective-permute-start | bytes 294920 | tf_op jit(solution)/shard_map/ppermute | solution.py:34
  287.6 12.5 %collective-permute-start.40 = (bf16[2,96,1280]{2,1,0:T(8,128)(2,1)S(1)}, bf16[2,96,1280]{2,1,0:T(8,128)(2,1)S(1)}, u32[]{:S(2)}, u32[]{:S(2)}) collective-permute-start(bf16[2,96,1280]{2,1,0:T(8,128)(2,1)S(1)} %dynamic-slice_bitcast_fusion.13), channel_id=1, source_target_pairs={{0,8},{4,12},{8,0},{12,4},{16,24},{20,28},{24,16},{28,20},{1,9},{5... | collective-permute-start | bytes 1474568 | tf_op jit(solution)/shard_map/ppermute | solution.py:34
  288.3 12.6 %collective-permute-start.43 = (bf16[2,96,1280]{2,1,0:T(8,128)(2,1)S(1)}, bf16[2,96,1280]{2,1,0:T(8,128)(2,1)S(1)}, u32[]{:S(2)}, u32[]{:S(2)}) collective-permute-start(bf16[2,96,1280]{2,1,0:T(8,128)(2,1)S(1)} %fusion.8), channel_id=1, source_target_pairs={{0,16},{4,20},{8,24},{12,28},{16,0},{20,4},{24,8},{28,12},{1,17},{... | collective-permute-start | bytes 1474568 | tf_op jit(solution)/shard_map/ppermute | solution.py:34
  290.9 16.3 %collective-permute-start.49 = (bf16[24,3968]{1,0:T(8,128)(2,1)S(1)}, bf16[24,3968]{1,0:T(8,128)(2,1)S(1)}, u32[]{:S(2)}, u32[]{:S(2)}) collective-permute-start(bf16[24,3968]{1,0:T(8,128)(2,1)S(1)} %get-tuple-element.226), channel_id=1, source_target_pairs={{0,1},{1,2},{2,3},{3,0},{4,5},{5,6},{6,7},{7,4},{8,9},{9,10},{10,1... | collective-permute-start | bytes 571400 | tf_op jit(solution)/shard_map/ppermute | solution.py:158
  292.7 15.8 %collective-permute-start.50 = (bf16[24,3968]{1,0:T(8,128)(2,1)S(1)}, bf16[24,3968]{1,0:T(8,128)(2,1)S(1)}, u32[]{:S(2)}, u32[]{:S(2)}) collective-permute-start(bf16[24,3968]{1,0:T(8,128)(2,1)S(1)} %get-tuple-element.228), channel_id=1, source_target_pairs={{0,2},{1,3},{2,0},{3,1},{4,6},{5,7},{6,4},{7,5},{8,10},{9,11},{10,... | collective-permute-start | bytes 571400 | tf_op jit(solution)/shard_map/ppermute | solution.py:158
  294.2 16.3 %collective-permute-start.51 = (bf16[24,3968]{1,0:T(8,128)(2,1)S(1)}, bf16[24,3968]{1,0:T(8,128)(2,1)S(1)}, u32[]{:S(2)}, u32[]{:S(2)}) collective-permute-start(bf16[24,3968]{1,0:T(8,128)(2,1)S(1)} %get-tuple-element.227), channel_id=1, source_target_pairs={{0,3},{1,0},{2,1},{3,2},{4,7},{5,4},{6,5},{7,6},{8,11},{9,8},{10,9... | collective-permute-start | bytes 571400 | tf_op jit(solution)/shard_map/ppermute | solution.py:158
  300.3 6.4 %collective-permute-start.41 = (bf16[96,1280]{1,0:T(8,128)(2,1)S(1)}, bf16[96,1280]{1,0:T(8,128)(2,1)S(1)}, u32[]{:S(2)}, u32[]{:S(2)}) collective-permute-start(bf16[96,1280]{1,0:T(8,128)(2,1)S(1)} %dynamic-slice_bitcast_fusion.15), channel_id=1, source_target_pairs={{0,16},{4,20},{8,24},{12,28},{16,0},{20,4},{24,8},{28,12},{1,17},{... | collective-permute-start | bytes 737288 | tf_op jit(solution)/shard_map/ppermute | solution.py:34
  301.1 6.1 %collective-permute-start.44 = (bf16[96,1280]{1,0:T(8,128)(2,1)S(1)}, bf16[96,1280]{1,0:T(8,128)(2,1)S(1)}, u32[]{:S(2)}, u32[]{:S(2)}) collective-permute-start(bf16[96,1280]{1,0:T(8,128)(2,1)S(1)} %dynamic-slice_bitcast_fusion.14), channel_id=1, source_target_pairs={{0,8},{4,12},{8,0},{12,4},{16,24},{20,28},{24,16},{28,20},{1,9},{5... | collective-permute-start | bytes 737288 | tf_op jit(solution)/shard_map/ppermute | solution.py:34
  312.1 3.8 %collective-permute-start.45 = (bf16[24,2560]{1,0:T(8,128)(2,1)S(1)}, bf16[24,2560]{1,0:T(8,128)(2,1)S(1)}, u32[]{:S(2)}, u32[]{:S(2)}) collective-permute-start(bf16[24,2560]{1,0:T(8,128)(2,1)S(1)} %get-tuple-element.232), channel_id=1, source_target_pairs={{0,1},{1,2},{2,3},{3,0},{4,5},{5,6},{6,7},{7,4},{8,9},{9,10},{10,1... | collective-permute-start | bytes 368648 | tf_op jit(solution)/shard_map/ppermute | solution.py:158
  312.2 5.4 %collective-permute-start.46 = (bf16[24,2560]{1,0:T(8,128)(2,1)S(1)}, bf16[24,2560]{1,0:T(8,128)(2,1)S(1)}, u32[]{:S(2)}, u32[]{:S(2)}) collective-permute-start(bf16[24,2560]{1,0:T(8,128)(2,1)S(1)} %get-tuple-element.234), channel_id=1, source_target_pairs={{0,2},{1,3},{2,0},{3,1},{4,6},{5,7},{6,4},{7,5},{8,10},{9,11},{10,... | collective-permute-start | bytes 368648 | tf_op jit(solution)/shard_map/ppermute | solution.py:158
  313.3 11.7 %collective-permute-start.47 = (bf16[24,2560]{1,0:T(8,128)(2,1)S(1)}, bf16[24,2560]{1,0:T(8,128)(2,1)S(1)}, u32[]{:S(2)}, u32[]{:S(2)}) collective-permute-start(bf16[24,2560]{1,0:T(8,128)(2,1)S(1)} %get-tuple-element.233), channel_id=1, source_target_pairs={{0,3},{1,0},{2,1},{3,2},{4,7},{5,4},{6,5},{7,6},{8,11},{9,8},{10,9... | collective-permute-start | bytes 368648 | tf_op jit(solution)/shard_map/ppermute | solution.py:158
  (14 other events, 41.8 us)

commit v3 on v2

--- a/solution.py
+++ b/solution.py
@@ -368,7 +368,7 @@
     first, last = cend_ref[base + step], cend_ref[base + step + 1]
     row_id = lax.broadcasted_iota(jnp.int32, (size, size), 0)
     mask = (row_id >= lanes((size, size))) & (cnt == row_ref[...])
-    before = jnp.where(cnt == first, 1.0, 0.0)
+    before = jnp.where(cnt == first, 1.0, 0.0).astype(bf16)
     after = jnp.where(cnt == last, 1.0, 0.0).astype(bf16)
     keep = jnp.where(first == last, 1.0, 0.0)
     low = lanes((size, 128)) < 64
@@ -387,7 +387,7 @@
             st = state[h]
             st_b = st.astype(bf16)
             srel_ref[0, h] = st_b
-            res.append(mm(sc, val) + before * mm(pq, st_b))
+            res.append(mm(sc, val) + mm(pq * before, st_b))
             state[h] = keep * st + mm_f(pk, val * after)
         for i, p in enumerate(group):
             two = pl.ds(p * 128, 128)

time: 331 us -> 331 us (level)
  no operation moved by 1% of the time
where the time goes in v3:
time: 331 us; the launch traced here: 327 us
  Pallas kernels  120 us (36%)
  waiting for transfers between devices  64.2 us (19%)
  starting transfers between devices  55.1 us (17%)
  other arithmetic  33.6 us (10%)
  matrix products  27.2 us (8%)
  local copies, waits for them, and re-layouts  24.5 us (7%)
    ppermute x34, waiting for transfers between devices, xor_send(): return lax.ppermute(arr, 'seq', [(i, i ^ mask) for i in range(size)])  43.8 us
    pallas_call x1, Pallas kernels, shards(): pl.pallas_call(functools.partial(middle_body, n_seq, pairs), name='middle...  43.1 us
    ppermute x34, starting transfers between devices, xor_send(): return lax.ppermute(arr, 'seq', [(i, i ^ mask) for i in range(size)])  33.6 us
    pallas_call x2, Pallas kernels, shards(): pl.pallas_call(functools.partial(back_body, g * some, some, pairs), name=...  29.9 us
    dot_general x5, matrix products, mm_f(): lax.dot_general(a, b, (((0,), (0,)), ((), ())), preferred_element_type=f32)  27 us
    pallas_call x2, Pallas kernels, shards(): pl.pallas_call(functools.partial(local_body, base, pairs), name='local',...  20.8 us
    pallas_call x1, Pallas kernels, shards(): pl.pallas_call(functools.partial(keys_body, n_seq, pairs), name='keys', c...  13.7 us
    ppermute x9, starting transfers between devices, stream_send(): lax.ppermute(shard, 'stream', [(i, (i + d) % depth) for i in range(depth)])  13 us
  transfers between devices with their start and end apart: 52, of which 21 were waited for; matrix products, arithmetic and copies ran while one was open for 22% of the time, Pallas kernels for 23%

profile of v3, /device:TPU:9, one launch (start us, length us, event | category | flops | bytes accessed | tf_op | source)
XLA Modules:
  0.0 326.8 jit_solution(12466531051195807018)
XLA Ops:
  2.1 1.3 reduce_max.9
  5.3 2.5 collective-permute-start.1
  7.7 2.2 collective-permute-start.2
  11.2 3.5 %collective-permute-done.1 = bf16[24,2560]{1,0:T(8,128)(2,1)S(1)} collective-permute-done((bf16[24,2560]{1,0:T(8,128)(2,1)S(1)}, bf16[24,2560]{1,0:T(8,128)(2,1)S(1)}, u32[]{:S(2)}, u32[]{:S(2)}) %collective-permute-start.1) | collective-permute-done | bytes 122912 | tf_op jit(solution)/shard_map/ppermute | solution.py:43
  14.8 3.2 collective-permute-done.2
  18.1 1.3 collective-permute-start.4
  19.4 1.2 collective-permute-start.5
  22.3 2.9 collective-permute-start.3
  25.2 4.5 %collective-permute-done.4 = bf16[96,2560]{1,0:T(8,128)(2,1)S(1)} collective-permute-done((bf16[96,2560]{1,0:T(8,128)(2,1)S(1)}, bf16[96,2560]{1,0:T(8,128)(2,1)S(1)}, u32[]{:S(2)}, u32[]{:S(2)}) %collective-permute-start.4) | collective-permute-done | bytes 491552 | tf_op jit(solution)/shard_map/ppermute | solution.py:34
  29.7 1.3 collective-permute-start.6
  31.1 1.3 collective-permute-start.7
  32.4 3.0 collective-permute-done.6
  36.8 3.3 %collective-permute-start.10 = (bf16[4,96,2560]{2,1,0:T(8,128)(2,1)S(1)}, bf16[4,96,2560]{2,1,0:T(8,128)(2,1)S(1)}, u32[]{:S(2)}, u32[]{:S(2)}) collective-permute-start(bf16[4,96,2560]{2,1,0:T(8,128)(2,1)S(1)} %pad_maximum_fusion.3.refs_0_.refs_2_), channel_id=1, source_target_pairs={{0,4},{4,0},{8,12},{12,8},{16,20},{20,16},{24,28},{28,24},{1,5},{5... | collective-permute-start | bytes 5898248 | tf_op jit(solution)/shard_map/ppermute | solution.py:34
  41.9 1.8 collective-permute-done.10.refs_1_.refs_3_
  43.7 2.2 collective-permute-start.17
  47.0 1.5 collective-permute-start.15
  48.6 13.7 %keys.1 = (bf16[1024,768]{1,0:T(8,128)(2,1)}, bf16[1024,768]{1,0:T(8,128)(2,1)}, bf16[1024,768]{1,0:T(8,128)(2,1)}, bf16[1024,1536]{1,0:T(8,128)(2,1)}, bf16[7,1...) custom-call(s32[1]{0:T(128)} %bitcast.me_ref, f32[5]{0:T(128)} %copy-done.21, ...), custom_call_target="tpu_custom_call" | custom-call | flops 11000000512 | bytes 22000000 | tf_op jit(solution)/shard_map/keys/pallas_call | solution.py:709
  62.3 1.3 collective-permute-start.20
  63.9 1.3 collective-permute-start.22
  66.8 10.2 %local.2 = (bf16[1024,768]{1,0:T(8,128)(2,1)}, bf16[1024,1536]{1,0:T(8,128)(2,1)}, f32[1024,768]{1,0:T(8,128)}, f32[1024,768]{1,0:T(8,128)}, bf16[4,12,128,128]{3,2,1,0:T(8,128)(2,1)}, /*index=5*/f32[12,128,128]{2,1,0:T(8,128)}) custom-call(s32[1]{0:T(128)} %bitcast.me_ref, f32[5]{0:T(128)} %copy-done.21, bf16[1024,768]{1,0:T(8,128)(2,1)} %get-tuple-element.116.h_ref, ...), custom_call_target="tpu_custom_call" | custom-call | flops 7500000256 | bytes 15000000 | tf_op jit(solution)/shard_map/local/pallas_call | solution.py:749
  77.1 4.7 %collective-permute-done.13 = bf16[96,1920]{1,0:T(8,128)(2,1)S(1)} collective-permute-done((bf16[96,1920]{1,0:T(8,128)(2,1)S(1)}, bf16[96,1920]{1,0:T(8,128)(2,1)S(1)}, u32[]{:S(2)}, u32[]{:S(2)}) %collective-permute-start.13) | collective-permute-done | bytes 368672 | tf_op jit(solution)/shard_map/ppermute | solution.py:34
  84.7 2.3 collective-permute-start.23
  87.0 7.9 %collective-permute-done.18 = bf16[384,768]{1,0:T(8,128)(2,1)S(1)} collective-permute-done((bf16[384,768]{1,0:T(8,128)(2,1)S(1)}, bf16[384,768]{1,0:T(8,128)(2,1)S(1)}, u32[]{:S(2)}, u32[]{:S(2)}) %collective-permute-start.18) | collective-permute-done | bytes 589856 | tf_op jit(solution)/shard_map/ppermute | solution.py:34
  96.2 10.6 %local.3 = (bf16[1024,768]{1,0:T(8,128)(2,1)}, bf16[1024,1536]{1,0:T(8,128)(2,1)}, f32[1024,768]{1,0:T(8,128)}, f32[1024,768]{1,0:T(8,128)}, bf16[4,12,128,128]{3,2,1,0:T(8,128)(2,1)}, /*index=5*/f32[12,128,128]{2,1,0:T(8,128)}) custom-call(s32[1]{0:T(128)} %bitcast.me_ref, ...), custom_call_target="tpu_custom_call", output_to_operand_aliasing={{0}: (11, {}), {1}: (12, {}), {2}: (13, {}), {3}: (14, {}),... | custom-call | flops 7500000256 | bytes 15000000 | tf_op jit(solution)/shard_map/local/pallas_call | solution.py:749
  108.0 1.8 pad_maximum_fusion.2.refs_2_
  109.7 3.7 %collective-permute-start.25 = (bf16[4,384,768]{2,1,0:T(8,128)(2,1)}, bf16[4,384,768]{2,1,0:T(8,128)(2,1)}, u32[]{:S(2)}, u32[]{:S(2)}) collective-permute-start(bf16[4,384,768]{2,1,0:T(8,128)(2,1)} %pad_maximum_fusion.2.refs_2_), channel_id=1, source_target_pairs={{0,4},{4,0},{8,12},{12,8},{16,20},{20,16},{24,28},{28,24},{1,5},{5... | collective-permute-start | bytes 7077896 | tf_op jit(solution)/shard_map/ppermute | solution.py:34
  113.4 2.2 pad_maximum_fusion.5.refs_4_
  117.1 2.1 collective-permute-done.26.refs_5_
  119.2 43.1 %middle.1 = (bf16[1024,768]{1,0:T(8,128)(2,1)}, bf16[1024,768]{1,0:T(8,128)(2,1)}, bf16[1024,768]{1,0:T(8,128)(2,1)}, bf16[1024,3072]{1,0:T(8,128)(2,1)}, bf16[1...) custom-call(s32[1]{0:T(128)} %bitcast.me_ref, ...), custom_call_target="tpu_custom_call" | custom-call | flops 21500000256 | bytes 43000000 | tf_op jit(solution)/shard_map/middle/pallas_call | solution.py:784
  163.6 1.5 collective-permute-start.29
  165.0 8.3 %convolution_convert_fusion.1 = bf16[768,3072]{1,0:T(8,128)(2,1)S(1)} fusion(bf16[1024,768]{1,0:T(8,128)(2,1)} %get-tuple-element.146, bf16[1024,3072]{1,0:T(8,128)(2,1)} %get-tuple-element.147), kind=kOutput, calls=%fused_computation.2 | convolution fusion | flops 4834197504 | bytes 12582912 | tf_op jit(solution)/shard_map/dot_general | solution.py:30
  173.4 1.4 convolution_convert_fusion.4
  174.8 1.8 dynamic-slice_bitcast_fusion
  177.9 3.9 %pad_maximum_fusion = bf16[2,2,96,3968]{3,2,1,0:T(8,128)(2,1)} fusion(bf16[2,2,96,128]{3,2,1,0:T(8,128)(2,1)S(1)} %get-tuple-element.242, bf16[2,2,96,768]{3,2,1,0:T(8,128)(2,1)} %get-tuple-element.225, bf16[2,2,96,3072]{3,2,1,0:T(8,128)(2,1)} %get-tuple-element.219), kind=kLoop, calls=%fused_computation.8 | loop fusion | flops 9142272 | bytes 6094848 | tf_op jit(solution)/shard_map/concatenate | solution.py:105
  183.0 2.2 pad_maximum_fusion.6.refs_0_
  185.2 8.5 %convolution_convert_fusion = bf16[3072,768]{1,0:T(8,128)(2,1)S(1)} fusion(bf16[1024,3072]{1,0:T(8,128)(2,1)} %get-tuple-element.156, bf16[1,1024,768]{2,1,0:T(8,128)(2,1)S(1)} %copy-done.23), kind=kOutput, calls=%fused_computation.1 | convolution fusion | flops 4834197504 | bytes 12582912 | tf_op jit(solution)/shard_map/dot_general | solution.py:30
  193.7 1.7 dynamic-slice_bitcast_fusion.1
  195.4 1.3 copy-done
  199.0 2.4 add_convert_fusion
  201.4 1.2 dynamic-slice_bitcast_fusion.3
  202.6 2.2 fusion
  207.1 15.0 %back.2 = (bf16[1024,1152]{1,0:T(8,128)(2,1)}, bf16[384,128]{1,0:T(8,128)(2,1)}) custom-call(s32[1]{0:T(128)} %bitcast.me_ref, f32[8]{0:T(128)} %bitcast.240, f32[5]{0:T(128)} %copy-done.21, bf16[1024,768]{1,0:T(8,128)(2,1)} %get-tuple-element.160.q_ref, bf16[1024,768]{1,0:T(8,128)(2,1)} %get-tuple-element.161.k_ref, ...), custom_call_target="tpu_custom_call" | custom-call | flops 9500000256 | bytes 19000000 | tf_op jit(solution)/shard_map/back/pallas_call | solution.py:846
  222.2 4.4 %convolution_convert_fusion.3 = bf16[768,1152]{1,0:T(8,128)(2,1)S(1)} fusion(bf16[1024,768]{1,0:T(8,128)(2,1)} %get-tuple-element.116.h_ref, bf16[1024,1152]{1,0:T(8,128)(2,1)} %get-tuple-element.165.refs_0_), kind=kOutput, calls=%fused_computation.7 | convolution fusion | flops 1812824064 | bytes 5701632 | tf_op jit(solution)/shard_map/dot_general | solution.py:30
  226.5 1.4 dynamic-slice_bitcast_fusion.6
  228.0 5.9 %collective-permute-done.32 = bf16[2,384,768]{2,1,0:T(8,128)(2,1)} collective-permute-done((bf16[2,384,768]{2,1,0:T(8,128)(2,1)}, bf16[2,384,768]{2,1,0:T(8,128)(2,1)}, u32[]{:S(2)}, u32[]{:S(2)}) %collective-permute-start.32) | collective-permute-done | bytes 1179680 | tf_op jit(solution)/shard_map/ppermute | solution.py:34
  233.8 1.5 fusion.2
  236.7 14.9 %back.3 = (bf16[1024,1152]{1,0:T(8,128)(2,1)}, bf16[384,128]{1,0:T(8,128)(2,1)}) custom-call(s32[1]{0:T(128)} %bitcast.me_ref, f32[8]{0:T(128)} %bitcast.241, f32[5]{0:T(128)} %copy-done.21, bf16[1024,768]{1,0:T(8,128)(2,1)} %get-tuple-element.160.q_ref, bf16[1024,768]{1,0:T(8,128)(2,1)} %get-tuple-element.161.k_ref, ...), custom_call_target="tpu_custom_call" | custom-call | flops 9500000256 | bytes 19000000 | tf_op jit(solution)/shard_map/back/pallas_call | solution.py:846
  252.6 4.4 %convolution_convert_fusion.2 = bf16[768,1152]{1,0:T(8,128)(2,1)S(1)} fusion(bf16[1024,768]{1,0:T(8,128)(2,1)} %get-tuple-element.116.h_ref, bf16[1024,1152]{1,0:T(8,128)(2,1)} %get-tuple-element.168.refs_1_), kind=kOutput, calls=%fused_computation.6 | convolution fusion | flops 1812824064 | bytes 5701632 | tf_op jit(solution)/shard_map/dot_general | solution.py:30
  258.4 1.5 pad_maximum_fusion.4
  261.0 1.7 fusion.1
  266.6 2.6 collective-permute-start.38
  269.2 12.1 %enter.1 = (f32[1024,768]{1,0:T(8,128)}, f32[8,768]{1,0:T(8,128)}) custom-call(s32[1]{0:T(128)} %bitcast.me_ref, bf16[1024,768]{1,0:T(8,128)(2,1)} %bitcast.245, f32[1024,768]{1,0:T(8,128)} %get-tuple-element.174.dr_ref, f32[8,768]{1,0:T(8,128)} %get-tuple-element.105.gb_ref, bf16[1024,1152]{1,0:T(8,128)(2,1)} %get-tuple-element.165.refs_0_, ...), custom_call_target="tpu_custom_call" | custom-call | flops 5500000256 | bytes 11000000 | tf_op jit(solution)/shard_map/enter/pallas_call | solution.py:886
  283.5 1.8 fusion.16
  285.3 2.2 add_convert_fusion.1
  288.3 1.3 collective-permute-start.43
  289.6 1.3 fusion.3
  290.9 1.8 collective-permute-start.49
  292.7 1.5 collective-permute-start.50
  294.2 5.9 %collective-permute-done.40 = bf16[2,96,1280]{2,1,0:T(8,128)(2,1)S(1)} collective-permute-done((bf16[2,96,1280]{2,1,0:T(8,128)(2,1)S(1)}, bf16[2,96,1280]{2,1,0:T(8,128)(2,1)S(1)}, u32[]{:S(2)}, u32[]{:S(2)}) %collective-permute-start.40) | collective-permute-done | bytes 491552 | tf_op jit(solution)/shard_map/ppermute | solution.py:34
  302.3 4.3 %collective-permute-done.41 = bf16[96,1280]{1,0:T(8,128)(2,1)S(1)} collective-permute-done((bf16[96,1280]{1,0:T(8,128)(2,1)S(1)}, bf16[96,1280]{1,0:T(8,128)(2,1)S(1)}, u32[]{:S(2)}, u32[]{:S(2)}) %collective-permute-start.41) | collective-permute-done | bytes 245792 | tf_op jit(solution)/shard_map/ppermute | solution.py:34
  308.5 2.0 collective-permute-done.51
  313.3 1.4 collective-permute-start.47
  315.9 1.7 collective-permute-done.46
  317.6 7.4 %collective-permute-done.47 = bf16[24,2560]{1,0:T(8,128)(2,1)S(1)} collective-permute-done((bf16[24,2560]{1,0:T(8,128)(2,1)S(1)}, bf16[24,2560]{1,0:T(8,128)(2,1)S(1)}, u32[]{:S(2)}, u32[]{:S(2)}) %collective-permute-start.47) | collective-permute-done | bytes 122912 | tf_op jit(solution)/shard_map/ppermute | solution.py:158
  (237 shorter events, 48.1 us)
Async XLA Ops:
  4.2 17.6 %copy-start.15 = (bf16[24,3072]{1,0:T(8,128)(2,1)S(1)}, bf16[24,3072]{1,0:T(8,128)(2,1)}, u32[]{:S(2)}) copy-start(bf16[24,3072]{1,0:T(8,128)(2,1)} %param.17) | copy-start | bytes 442372
  4.2 17.6 %copy-start.17 = (bf16[24,768]{1,0:T(8,128)(2,1)S(1)}, bf16[24,768]{1,0:T(8,128)(2,1)}, u32[]{:S(2)}) copy-start(bf16[24,768]{1,0:T(8,128)(2,1)} %param.16) | copy-start | bytes 110596
  5.2 6.0 %collective-permute-start = (bf16[24,2560]{1,0:T(8,128)(2,1)S(1)}, bf16[24,2560]{1,0:T(8,128)(2,1)S(1)}, u32[]{:S(2)}, u32[]{:S(2)}) collective-permute-start(bf16[24,2560]{1,0:T(8,128)(2,1)S(1)} %concatenate.61), channel_id=1, source_target_pairs={{0,3},{1,0},{2,1},{3,2},{4,7},{5,4},{6,5},{7,6},{8,11},{9,8},{10,9... | collective-permute-start | bytes 368648 | tf_op jit(solution)/shard_map/ppermute | solution.py:43
  5.3 9.5 %collective-permute-start.1 = (bf16[24,2560]{1,0:T(8,128)(2,1)S(1)}, bf16[24,2560]{1,0:T(8,128)(2,1)S(1)}, u32[]{:S(2)}, u32[]{:S(2)}) collective-permute-start(bf16[24,2560]{1,0:T(8,128)(2,1)S(1)} %concatenate.61), channel_id=1, source_target_pairs={{0,2},{1,3},{2,0},{3,1},{4,6},{5,7},{6,4},{7,5},{8,10},{9,11},{10,... | collective-permute-start | bytes 368648 | tf_op jit(solution)/shard_map/ppermute | solution.py:43
  7.7 10.2 %collective-permute-start.2 = (bf16[24,2560]{1,0:T(8,128)(2,1)S(1)}, bf16[24,2560]{1,0:T(8,128)(2,1)S(1)}, u32[]{:S(2)}, u32[]{:S(2)}) collective-permute-start(bf16[24,2560]{1,0:T(8,128)(2,1)S(1)} %concatenate.61), channel_id=1, source_target_pairs={{0,1},{1,2},{2,3},{3,0},{4,5},{5,6},{6,7},{7,4},{8,9},{9,10},{10,1... | collective-permute-start | bytes 368648 | tf_op jit(solution)/shard_map/ppermute | solution.py:43
  11.2 18.6 %copy-start.21 = (f32[5]{0:T(128)}, f32[5]{0:T(128)S(1)}, u32[]{:S(2)}) copy-start(f32[5]{0:T(128)S(1)} %pad_maximum_fusion.15.cend_ref) | copy-start | bytes 64
  18.1 11.6 %collective-permute-start.4 = (bf16[96,2560]{1,0:T(8,128)(2,1)S(1)}, bf16[96,2560]{1,0:T(8,128)(2,1)S(1)}, u32[]{:S(2)}, u32[]{:S(2)}) collective-permute-start(bf16[96,2560]{1,0:T(8,128)(2,1)S(1)} %constant_dynamic-slice_fusion.3), channel_id=1, source_target_pairs={{0,8},{4,12},{8,0},{12,4},{16,24},{20,28},{24,16},{28,20},{1,9},{5... | collective-permute-start | bytes 1474568 | tf_op jit(solution)/shard_map/ppermute | solution.py:34
  19.4 11.7 %collective-permute-start.5 = (bf16[96,2560]{1,0:T(8,128)(2,1)S(1)}, bf16[96,2560]{1,0:T(8,128)(2,1)S(1)}, u32[]{:S(2)}, u32[]{:S(2)}) collective-permute-start(bf16[96,2560]{1,0:T(8,128)(2,1)S(1)} %constant_dynamic-slice_fusion.3), channel_id=1, source_target_pairs={{0,16},{4,20},{8,24},{12,28},{16,0},{20,4},{24,8},{28,12},{1,17},{... | collective-permute-start | bytes 1474568 | tf_op jit(solution)/shard_map/ppermute | solution.py:34
  20.7 16.1 %copy-start.19 = (f32[1,1,4,256]{3,1,2,0:T(1,128)}, f32[1,1,4,256]{3,1,2,0:T(1,128)S(1)}, u32[]{:S(2)}) copy-start(f32[1,1,4,256]{3,1,2,0:T(1,128)S(1)} %copy.104) | copy-start | bytes 12292
  21.8 19.3 %collective-permute-start.8 = (bf16[24,3840]{1,0:T(8,128)(2,1)S(1)}, bf16[24,3840]{1,0:T(8,128)(2,1)S(1)}, u32[]{:S(2)}, u32[]{:S(2)}) collective-permute-start(bf16[24,3840]{1,0:T(8,128)(2,1)S(1)} %pad_maximum_fusion.10), channel_id=1, source_target_pairs={{0,2},{1,3},{2,0},{3,1},{4,6},{5,7},{6,4},{7,5},{8,10},{9,11},{10,... | collective-permute-start | bytes 552968 | tf_op jit(solution)/shard_map/ppermute | solution.py:43
  22.3 18.7 %collective-permute-start.3 = (bf16[24,3840]{1,0:T(8,128)(2,1)S(1)}, bf16[24,3840]{1,0:T(8,128)(2,1)S(1)}, u32[]{:S(2)}, u32[]{:S(2)}) collective-permute-start(bf16[24,3840]{1,0:T(8,128)(2,1)S(1)} %pad_maximum_fusion.10), channel_id=1, source_target_pairs={{0,3},{1,0},{2,1},{3,2},{4,7},{5,4},{6,5},{7,6},{8,11},{9,8},{10,9... | collective-permute-start | bytes 552968 | tf_op jit(solution)/shard_map/ppermute | solution.py:43
  25.2 15.8 %collective-permute-start.9 = (bf16[24,3840]{1,0:T(8,128)(2,1)S(1)}, bf16[24,3840]{1,0:T(8,128)(2,1)S(1)}, u32[]{:S(2)}, u32[]{:S(2)}) collective-permute-start(bf16[24,3840]{1,0:T(8,128)(2,1)S(1)} %pad_maximum_fusion.10), channel_id=1, source_target_pairs={{0,1},{1,2},{2,3},{3,0},{4,5},{5,6},{6,7},{7,4},{8,9},{9,10},{10,1... | collective-permute-start | bytes 552968 | tf_op jit(solution)/shard_map/ppermute | solution.py:43
  29.7 5.7 %collective-permute-start.6 = (bf16[96,1280]{1,0:T(8,128)(2,1)S(1)}, bf16[96,1280]{1,0:T(8,128)(2,1)S(1)}, u32[]{:S(2)}, u32[]{:S(2)}) collective-permute-start(bf16[96,1280]{1,0:T(8,128)(2,1)S(1)} %slice.135), channel_id=1, source_target_pairs={{0,16},{4,20},{8,24},{12,28},{16,0},{20,4},{24,8},{28,12},{1,17},{... | collective-permute-start | bytes 737288 | tf_op jit(solution)/shard_map/ppermute | solution.py:34
  31.1 5.4 %collective-permute-start.7 = (bf16[96,1280]{1,0:T(8,128)(2,1)S(1)}, bf16[96,1280]{1,0:T(8,128)(2,1)S(1)}, u32[]{:S(2)}, u32[]{:S(2)}) collective-permute-start(bf16[96,1280]{1,0:T(8,128)(2,1)S(1)} %slice.136), channel_id=1, source_target_pairs={{0,8},{4,12},{8,0},{12,4},{16,24},{20,28},{24,16},{28,20},{1,9},{5... | collective-permute-start | bytes 737288 | tf_op jit(solution)/shard_map/ppermute | solution.py:34
  36.8 6.9 %collective-permute-start.10 = (bf16[4,96,2560]{2,1,0:T(8,128)(2,1)S(1)}, bf16[4,96,2560]{2,1,0:T(8,128)(2,1)S(1)}, u32[]{:S(2)}, u32[]{:S(2)}) collective-permute-start(bf16[4,96,2560]{2,1,0:T(8,128)(2,1)S(1)} %pad_maximum_fusion.3.refs_0_.refs_2_), channel_id=1, source_target_pairs={{0,4},{4,0},{8,12},{12,8},{16,20},{20,16},{24,28},{28,24},{1,5},{5... | collective-permute-start | bytes 5898248 | tf_op jit(solution)/shard_map/ppermute | solution.py:34
  41.3 21.0 %collective-permute-start.11 = (bf16[96,3840]{1,0:T(8,128)(2,1)S(1)}, bf16[96,3840]{1,0:T(8,128)(2,1)S(1)}, u32[]{:S(2)}, u32[]{:S(2)}) collective-permute-start(bf16[96,3840]{1,0:T(8,128)(2,1)S(1)} %constant_dynamic-slice_fusion.2), channel_id=1, source_target_pairs={{0,8},{4,12},{8,0},{12,4},{16,24},{20,28},{24,16},{28,20},{1,9},{5... | collective-permute-start | bytes 2211848 | tf_op jit(solution)/shard_map/ppermute | solution.py:34
  41.6 22.0 %collective-permute-start.12 = (bf16[96,3840]{1,0:T(8,128)(2,1)S(1)}, bf16[96,3840]{1,0:T(8,128)(2,1)S(1)}, u32[]{:S(2)}, u32[]{:S(2)}) collective-permute-start(bf16[96,3840]{1,0:T(8,128)(2,1)S(1)} %constant_dynamic-slice_fusion.2), channel_id=1, source_target_pairs={{0,16},{4,20},{8,24},{12,28},{16,0},{20,4},{24,8},{28,12},{1,17},{... | collective-permute-start | bytes 2211848 | tf_op jit(solution)/shard_map/ppermute | solution.py:34
  43.7 20.2 %collective-permute-start.17 = (bf16[96,768]{1,0:T(8,128)(2,1)S(1)}, bf16[96,768]{1,0:T(8,128)(2,1)S(1)}, u32[]{:S(2)}, u32[]{:S(2)}) collective-permute-start(bf16[96,768]{1,0:T(8,128)(2,1)S(1)} %copy-done.12), channel_id=1, source_target_pairs={{0,1},{1,2},{2,3},{3,0},{4,5},{5,6},{6,7},{7,4},{8,9},{9,10},{10,1... | collective-permute-start | bytes 442376 | tf_op jit(solution)/shard_map/ppermute | solution.py:43
  45.9 19.3 %collective-permute-start.16 = (bf16[96,768]{1,0:T(8,128)(2,1)S(1)}, bf16[96,768]{1,0:T(8,128)(2,1)S(1)}, u32[]{:S(2)}, u32[]{:S(2)}) collective-permute-start(bf16[96,768]{1,0:T(8,128)(2,1)S(1)} %copy-done.12), channel_id=1, source_target_pairs={{0,2},{1,3},{2,0},{3,1},{4,6},{5,7},{6,4},{7,5},{8,10},{9,11},{10,... | collective-permute-start | bytes 442376 | tf_op jit(solution)/shard_map/ppermute | solution.py:43
  47.0 19.3 %collective-permute-start.15 = (bf16[96,768]{1,0:T(8,128)(2,1)S(1)}, bf16[96,768]{1,0:T(8,128)(2,1)S(1)}, u32[]{:S(2)}, u32[]{:S(2)}) collective-permute-start(bf16[96,768]{1,0:T(8,128)(2,1)S(1)} %copy-done.12), channel_id=1, source_target_pairs={{0,3},{1,0},{2,1},{3,2},{4,7},{5,4},{6,5},{7,6},{8,11},{9,8},{10,9... | collective-permute-start | bytes 442376 | tf_op jit(solution)/shard_map/ppermute | solution.py:43
  62.3 22.4 %collective-permute-start.20 = (bf16[7,128,128]{2,1,0:T(8,128)(2,1)}, bf16[7,128,128]{2,1,0:T(8,128)(2,1)}, u32[]{:S(2)}, u32[]{:S(2)}) collective-permute-start(bf16[7,128,128]{2,1,0:T(8,128)(2,1)} %get-tuple-element.140), channel_id=1, source_target_pairs={{0,8},{4,12},{8,0},{12,4},{16,24},{20,28},{24,16},{28,20},{1,9},{5... | collective-permute-start | bytes 688136 | tf_op jit(solution)/shard_map/ppermute | solution.py:34
  63.6 23.5 %collective-permute-start.21 = (bf16[7,128,128]{2,1,0:T(8,128)(2,1)}, bf16[7,128,128]{2,1,0:T(8,128)(2,1)}, u32[]{:S(2)}, u32[]{:S(2)}) collective-permute-start(bf16[7,128,128]{2,1,0:T(8,128)(2,1)} %get-tuple-element.140), channel_id=1, source_target_pairs={{0,16},{4,20},{8,24},{12,28},{16,0},{20,4},{24,8},{28,12},{1,17},{... | collective-permute-start | bytes 688136 | tf_op jit(solution)/shard_map/ppermute | solution.py:34
  63.9 23.2 %collective-permute-start.22 = (bf16[7,128,128]{2,1,0:T(8,128)(2,1)}, bf16[7,128,128]{2,1,0:T(8,128)(2,1)}, u32[]{:S(2)}, u32[]{:S(2)}) collective-permute-start(bf16[7,128,128]{2,1,0:T(8,128)(2,1)} %get-tuple-element.140), channel_id=1, source_target_pairs={{0,24},{4,28},{8,16},{12,20},{16,8},{20,12},{24,0},{28,4},{1,25},{... | collective-permute-start | bytes 688136 | tf_op jit(solution)/shard_map/ppermute | solution.py:34
  65.2 16.6 %collective-permute-start.13 = (bf16[96,1920]{1,0:T(8,128)(2,1)S(1)}, bf16[96,1920]{1,0:T(8,128)(2,1)S(1)}, u32[]{:S(2)}, u32[]{:S(2)}) collective-permute-start(bf16[96,1920]{1,0:T(8,128)(2,1)S(1)} %slice.112), channel_id=1, source_target_pairs={{0,8},{4,12},{8,0},{12,4},{16,24},{20,28},{24,16},{28,20},{1,9},{5... | collective-permute-start | bytes 1105928 | tf_op jit(solution)/shard_map/ppermute | solution.py:34
  66.4 16.6 %collective-permute-start.14 = (bf16[96,1920]{1,0:T(8,128)(2,1)S(1)}, bf16[96,1920]{1,0:T(8,128)(2,1)}, u32[]{:S(2)}, u32[]{:S(2)}) collective-permute-start(bf16[96,1920]{1,0:T(8,128)(2,1)S(1)} %slice.113), channel_id=1, source_target_pairs={{0,16},{4,20},{8,24},{12,28},{16,0},{20,4},{24,8},{28,12},{1,17},{... | collective-permute-start | bytes 1105928 | tf_op jit(solution)/shard_map/ppermute | solution.py:34
  77.1 7.2 %copy-start.9 = (bf16[96,3840]{1,0:T(8,128)(2,1)S(1)}, bf16[96,3840]{1,0:T(8,128)(2,1)}, u32[]{:S(2)}) copy-start(bf16[96,3840]{1,0:T(8,128)(2,1)} %copy-done.8) | copy-start | bytes 2211844
  77.1 7.2 %copy-start.11 = (bf16[96,3840]{1,0:T(8,128)(2,1)S(1)}, bf16[96,3840]{1,0:T(8,128)(2,1)}, u32[]{:S(2)}) copy-start(bf16[96,3840]{1,0:T(8,128)(2,1)} %copy-done.10) | copy-start | bytes 2211844
  81.8 13.2 %collective-permute-start.18 = (bf16[384,768]{1,0:T(8,128)(2,1)S(1)}, bf16[384,768]{1,0:T(8,128)(2,1)S(1)}, u32[]{:S(2)}, u32[]{:S(2)}) collective-permute-start(bf16[384,768]{1,0:T(8,128)(2,1)S(1)} %constant_dynamic-slice_fusion), channel_id=1, source_target_pairs={{0,8},{4,12},{8,0},{12,4},{16,24},{20,28},{24,16},{28,20},{1,9},{5... | collective-permute-start | bytes 1769480 | tf_op jit(solution)/shard_map/ppermute | solution.py:34
  83.0 12.9 %collective-permute-start.19 = (bf16[384,768]{1,0:T(8,128)(2,1)S(1)}, bf16[384,768]{1,0:T(8,128)(2,1)S(1)}, u32[]{:S(2)}, u32[]{:S(2)}) collective-permute-start(bf16[384,768]{1,0:T(8,128)(2,1)S(1)} %constant_dynamic-slice_fusion), channel_id=1, source_target_pairs={{0,16},{4,20},{8,24},{12,28},{16,0},{20,4},{24,8},{28,12},{1,17},{... | collective-permute-start | bytes 1769480 | tf_op jit(solution)/shard_map/ppermute | solution.py:34
  84.7 22.1 %copy-start.6 = (bf16[4,96,3840]{2,1,0:T(8,128)(2,1)}, bf16[4,96,3840]{2,1,0:T(8,128)(2,1)S(1)}, u32[]{:S(2)}) copy-start(bf16[4,96,3840]{2,1,0:T(8,128)(2,1)S(1)} %pad_maximum_fusion.1.refs_0_) | copy-start | bytes 8847364
  84.7 34.5 %collective-permute-start.23 = (bf16[4,96,3840]{2,1,0:T(8,128)(2,1)S(1)}, bf16[4,96,3840]{2,1,0:T(8,128)(2,1)}, u32[]{:S(2)}, u32[]{:S(2)}) collective-permute-start(bf16[4,96,3840]{2,1,0:T(8,128)(2,1)S(1)} %pad_maximum_fusion.1.refs_0_), channel_id=1, source_target_pairs={{0,4},{4,0},{8,12},{12,8},{16,20},{20,16},{24,28},{28,24},{1,5},{5... | collective-permute-start | bytes 8847368 | tf_op jit(solution)/shard_map/ppermute | solution.py:34
  95.9 12.1 %collective-permute-start.24 = (bf16[384,768]{1,0:T(8,128)(2,1)S(1)}, bf16[384,768]{1,0:T(8,128)(2,1)S(1)}, u32[]{:S(2)}, u32[]{:S(2)}) collective-permute-start(bf16[384,768]{1,0:T(8,128)(2,1)S(1)} %collective-permute-done.19), channel_id=1, source_target_pairs={{0,8},{4,12},{8,0},{12,4},{16,24},{20,28},{24,16},{28,20},{1,9},{5... | collective-permute-start | bytes 1769480 | tf_op jit(solution)/shard_map/ppermute | solution.py:34
  108.0 5.4 %copy-start.13 = (bf16[7,128,128]{2,1,0:T(8,128)(2,1)S(1)}, bf16[7,128,128]{2,1,0:T(8,128)(2,1)}, u32[]{:S(2)}) copy-start(bf16[7,128,128]{2,1,0:T(8,128)(2,1)} %get-tuple-element.140) | copy-start | bytes 688132
  109.7 9.5 %collective-permute-start.25 = (bf16[4,384,768]{2,1,0:T(8,128)(2,1)}, bf16[4,384,768]{2,1,0:T(8,128)(2,1)}, u32[]{:S(2)}, u32[]{:S(2)}) collective-permute-start(bf16[4,384,768]{2,1,0:T(8,128)(2,1)} %pad_maximum_fusion.2.refs_2_), channel_id=1, source_target_pairs={{0,4},{4,0},{8,12},{12,8},{16,20},{20,16},{24,28},{28,24},{1,5},{5... | collective-permute-start | bytes 7077896 | tf_op jit(solution)/shard_map/ppermute | solution.py:34
  115.7 3.6 %collective-permute-start.26 = (bf16[4,7,128,128]{3,2,1,0:T(8,128)(2,1)}, bf16[4,7,128,128]{3,2,1,0:T(8,128)(2,1)}, u32[]{:S(2)}, u32[]{:S(2)}) collective-permute-start(bf16[4,7,128,128]{3,2,1,0:T(8,128)(2,1)} %pad_maximum_fusion.5.refs_4_), channel_id=1, source_target_pairs={{0,4},{4,0},{8,12},{12,8},{16,20},{20,16},{24,28},{28,24},{1,5},{5... | collective-permute-start | bytes 2752520 | tf_op jit(solution)/shard_map/ppermute | solution.py:34
  162.3 20.6 %collective-permute-start.27 = (bf16[7,128,128]{2,1,0:T(8,128)(2,1)}, bf16[7,128,128]{2,1,0:T(8,128)(2,1)}, u32[]{:S(2)}, u32[]{:S(2)}) collective-permute-start(bf16[7,128,128]{2,1,0:T(8,128)(2,1)} %get-tuple-element.152), channel_id=1, source_target_pairs={{0,8},{4,12},{8,0},{12,4},{16,24},{20,28},{24,16},{28,20},{1,9},{5... | collective-permute-start | bytes 688136 | tf_op jit(solution)/shard_map/ppermute | solution.py:34
  162.7 20.3 %collective-permute-start.28 = (bf16[7,128,128]{2,1,0:T(8,128)(2,1)}, bf16[7,128,128]{2,1,0:T(8,128)(2,1)}, u32[]{:S(2)}, u32[]{:S(2)}) collective-permute-start(bf16[7,128,128]{2,1,0:T(8,128)(2,1)} %get-tuple-element.152), channel_id=1, source_target_pairs={{0,16},{4,20},{8,24},{12,28},{16,0},{20,4},{24,8},{28,12},{1,17},{... | collective-permute-start | bytes 688136 | tf_op jit(solution)/shard_map/ppermute | solution.py:34
  163.6 19.4 %collective-permute-start.29 = (bf16[7,128,128]{2,1,0:T(8,128)(2,1)}, bf16[7,128,128]{2,1,0:T(8,128)(2,1)}, u32[]{:S(2)}, u32[]{:S(2)}) collective-permute-start(bf16[7,128,128]{2,1,0:T(8,128)(2,1)} %get-tuple-element.152), channel_id=1, source_target_pairs={{0,24},{4,28},{8,16},{12,20},{16,8},{20,12},{24,0},{28,4},{1,25},{... | collective-permute-start | bytes 688136 | tf_op jit(solution)/shard_map/ppermute | solution.py:34
  165.0 8.3 %copy-start.24 = (bf16[1024,768]{1,0:T(8,128)(2,1)S(1)}, bf16[1024,768]{1,0:T(8,128)(2,1)}, u32[]{:S(2)}) copy-start(bf16[1024,768]{1,0:T(8,128)(2,1)} %get-tuple-element.148) | copy-start | bytes 4718596
  165.0 8.3 %copy-start.25 = (bf16[1024,768]{1,0:T(8,128)(2,1)S(1)}, bf16[1024,768]{1,0:T(8,128)(2,1)}, u32[]{:S(2)}) copy-start(bf16[1024,768]{1,0:T(8,128)(2,1)} %get-tuple-element.149) | copy-start | bytes 4718596
  177.9 7.3 %copy-start.23 = (bf16[1,1024,768]{2,1,0:T(8,128)(2,1)S(1)}, bf16[1,1024,768]{2,1,0:T(8,128)(2,1)}, u32[]{:S(2)}) copy-start(bf16[1,1024,768]{2,1,0:T(8,128)(2,1)} %param.19) | copy-start | bytes 4718596
  181.7 17.3 %collective-permute-start.31 = (bf16[2,2,96,3968]{3,2,1,0:T(8,128)(2,1)}, bf16[2,2,96,3968]{3,2,1,0:T(8,128)(2,1)}, u32[]{:S(2)}, u32[]{:S(2)}) collective-permute-start(bf16[2,2,96,3968]{3,2,1,0:T(8,128)(2,1)} %pad_maximum_fusion), channel_id=1, source_target_pairs={{0,4},{4,0},{8,12},{12,8},{16,20},{20,16},{24,28},{28,24},{1,5},{5... | collective-permute-start | bytes 9142280 | tf_op jit(solution)/shard_map/ppermute | solution.py:34
  185.2 12.9 %collective-permute-start.33 = (bf16[4,7,128,128]{3,2,1,0:T(8,128)(2,1)}, bf16[4,7,128,128]{3,2,1,0:T(8,128)(2,1)}, u32[]{:S(2)}, u32[]{:S(2)}) collective-permute-start(bf16[4,7,128,128]{3,2,1,0:T(8,128)(2,1)} %pad_maximum_fusion.6.refs_0_), channel_id=1, source_target_pairs={{0,4},{4,0},{8,12},{12,8},{16,20},{20,16},{24,28},{28,24},{1,5},{5... | collective-permute-start | bytes 2752520 | tf_op jit(solution)/shard_map/ppermute | solution.py:34
  196.7 5.9 %collective-permute-start.30 = (bf16[2,2,384,768]{3,2,1,0:T(8,128)(2,1)}, bf16[2,2,384,768]{3,2,1,0:T(8,128)(2,1)}, u32[]{:S(2)}, u32[]{:S(2)}) collective-permute-start(bf16[2,2,384,768]{3,2,1,0:T(8,128)(2,1)} %dynamic-slice_bitcast_fusion.1), channel_id=1, source_target_pairs={{0,4},{4,0},{8,12},{12,8},{16,20},{20,16},{24,28},{28,24},{1,5},{5... | collective-permute-start | bytes 7077896 | tf_op jit(solution)/shard_map/ppermute | solution.py:34
  206.0 27.8 %collective-permute-start.32 = (bf16[2,384,768]{2,1,0:T(8,128)(2,1)}, bf16[2,384,768]{2,1,0:T(8,128)(2,1)}, u32[]{:S(2)}, u32[]{:S(2)}) collective-permute-start(bf16[2,384,768]{2,1,0:T(8,128)(2,1)} %dynamic-slice_bitcast_fusion.4), channel_id=1, source_target_pairs={{0,8},{4,12},{8,0},{12,4},{16,24},{20,28},{24,16},{28,20},{1,9},{5... | collective-permute-start | bytes 3538952 | tf_op jit(solution)/shard_map/ppermute | solution.py:34
  206.3 54.7 %collective-permute-start.35 = (bf16[2,96,3968]{2,1,0:T(8,128)(2,1)}, bf16[2,96,3968]{2,1,0:T(8,128)(2,1)}, u32[]{:S(2)}, u32[]{:S(2)}) collective-permute-start(bf16[2,96,3968]{2,1,0:T(8,128)(2,1)} %dynamic-slice_bitcast_fusion.3), channel_id=1, source_target_pairs={{0,16},{4,20},{8,24},{12,28},{16,0},{20,4},{24,8},{28,12},{1,17},{... | collective-permute-start | bytes 4571144 | tf_op jit(solution)/shard_map/ppermute | solution.py:34
  236.4 15.2 %copy-start.16 = (bf16[384,128]{1,0:T(8,128)(2,1)S(1)}, bf16[384,128]{1,0:T(8,128)(2,1)}, u32[]{:S(2)}) copy-start(bf16[384,128]{1,0:T(8,128)(2,1)} %get-tuple-element.169) | copy-start | bytes 294916
  236.5 28.2 %collective-permute-start.34 = (bf16[384,768]{1,0:T(8,128)(2,1)S(1)}, bf16[384,768]{1,0:T(8,128)(2,1)}, u32[]{:S(2)}, u32[]{:S(2)}) collective-permute-start(bf16[384,768]{1,0:T(8,128)(2,1)S(1)} %dynamic-slice_bitcast_fusion.10), channel_id=1, source_target_pairs={{0,16},{4,20},{8,24},{12,28},{16,0},{20,4},{24,8},{28,12},{1,17},{... | collective-permute-start | bytes 1769480 | tf_op jit(solution)/shard_map/ppermute | solution.py:34
  259.8 25.4 %collective-permute-start.36 = (bf16[2,2,96,2432]{3,2,1,0:T(8,128)(2,1)}, bf16[2,2,96,2432]{3,2,1,0:T(8,128)(2,1)}, u32[]{:S(2)}, u32[]{:S(2)}) collective-permute-start(bf16[2,2,96,2432]{3,2,1,0:T(8,128)(2,1)} %pad_maximum_fusion.4), channel_id=1, source_target_pairs={{0,4},{4,0},{8,12},{12,8},{16,20},{20,16},{24,28},{28,24},{1,5},{5... | collective-permute-start | bytes 5603336 | tf_op jit(solution)/shard_map/ppermute | solution.py:34
  263.7 25.9 %collective-permute-start.48 = (bf16[96,3968]{1,0:T(8,128)(2,1)}, bf16[96,3968]{1,0:T(8,128)(2,1)}, u32[]{:S(2)}, u32[]{:S(2)}) collective-permute-start(bf16[96,3968]{1,0:T(8,128)(2,1)} %dynamic-slice_bitcast_fusion.9), channel_id=1, source_target_pairs={{0,8},{4,12},{8,0},{12,4},{16,24},{20,28},{24,16},{28,20},{1,9},{5... | collective-permute-start | bytes 2285576 | tf_op jit(solution)/shard_map/ppermute | solution.py:34
  266.6 15.8 %collective-permute-start.37 = (bf16[96,768]{1,0:T(8,128)(2,1)}, bf16[96,768]{1,0:T(8,128)(2,1)S(1)}, u32[]{:S(2)}, u32[]{:S(2)}) collective-permute-start(bf16[96,768]{1,0:T(8,128)(2,1)} %get-tuple-element.229), channel_id=1, source_target_pairs={{0,1},{1,2},{2,3},{3,0},{4,5},{5,6},{6,7},{7,4},{8,9},{9,10},{10,1... | collective-permute-start | bytes 442376 | tf_op jit(solution)/shard_map/ppermute | solution.py:158
  266.6 16.9 %collective-permute-start.38 = (bf16[96,768]{1,0:T(8,128)(2,1)}, bf16[96,768]{1,0:T(8,128)(2,1)}, u32[]{:S(2)}, u32[]{:S(2)}) collective-permute-start(bf16[96,768]{1,0:T(8,128)(2,1)} %get-tuple-element.231), channel_id=1, source_target_pairs={{0,2},{1,3},{2,0},{3,1},{4,6},{5,7},{6,4},{7,5},{8,10},{9,11},{10,... | collective-permute-start | bytes 442376 | tf_op jit(solution)/shard_map/ppermute | solution.py:158
  269.2 14.3 %collective-permute-start.39 = (bf16[96,768]{1,0:T(8,128)(2,1)}, bf16[96,768]{1,0:T(8,128)(2,1)}, u32[]{:S(2)}, u32[]{:S(2)}) collective-permute-start(bf16[96,768]{1,0:T(8,128)(2,1)} %get-tuple-element.230), channel_id=1, source_target_pairs={{0,3},{1,0},{2,1},{3,2},{4,7},{5,4},{6,5},{7,6},{8,11},{9,8},{10,9... | collective-permute-start | bytes 442376 | tf_op jit(solution)/shard_map/ppermute | solution.py:158
  282.5 5.7 %collective-permute-start.42 = (bf16[2,2,96,128]{3,2,1,0:T(8,128)(2,1)S(1)}, bf16[2,2,96,128]{3,2,1,0:T(8,128)(2,1)S(1)}, u32[]{:S(2)}, u32[]{:S(2)}) collective-permute-start(bf16[2,2,96,128]{3,2,1,0:T(8,128)(2,1)S(1)} %dynamic-slice_bitcast_fusion.25), channel_id=1, source_target_pairs={{0,4},{4,0},{8,12},{12,8},{16,20},{20,16},{24,28},{28,24},{1,5},{5... | collective-permute-start | bytes 294920 | tf_op jit(solution)/shard_map/ppermute | solution.py:34
  287.6 12.5 %collective-permute-start.40 = (bf16[2,96,1280]{2,1,0:T(8,128)(2,1)S(1)}, bf16[2,96,1280]{2,1,0:T(8,128)(2,1)S(1)}, u32[]{:S(2)}, u32[]{:S(2)}) collective-permute-start(bf16[2,96,1280]{2,1,0:T(8,128)(2,1)S(1)} %dynamic-slice_bitcast_fusion.13), channel_id=1, source_target_pairs={{0,8},{4,12},{8,0},{12,4},{16,24},{20,28},{24,16},{28,20},{1,9},{5... | collective-permute-start | bytes 1474568 | tf_op jit(solution)/shard_map/ppermute | solution.py:34
  288.3 12.6 %collective-permute-start.43 = (bf16[2,96,1280]{2,1,0:T(8,128)(2,1)S(1)}, bf16[2,96,1280]{2,1,0:T(8,128)(2,1)S(1)}, u32[]{:S(2)}, u32[]{:S(2)}) collective-permute-start(bf16[2,96,1280]{2,1,0:T(8,128)(2,1)S(1)} %fusion.8), channel_id=1, source_target_pairs={{0,16},{4,20},{8,24},{12,28},{16,0},{20,4},{24,8},{28,12},{1,17},{... | collective-permute-start | bytes 1474568 | tf_op jit(solution)/shard_map/ppermute | solution.py:34
  290.9 16.3 %collective-permute-start.49 = (bf16[24,3968]{1,0:T(8,128)(2,1)S(1)}, bf16[24,3968]{1,0:T(8,128)(2,1)S(1)}, u32[]{:S(2)}, u32[]{:S(2)}) collective-permute-start(bf16[24,3968]{1,0:T(8,128)(2,1)S(1)} %get-tuple-element.226), channel_id=1, source_target_pairs={{0,1},{1,2},{2,3},{3,0},{4,5},{5,6},{6,7},{7,4},{8,9},{9,10},{10,1... | collective-permute-start | bytes 571400 | tf_op jit(solution)/shard_map/ppermute | solution.py:158
  292.7 15.8 %collective-permute-start.50 = (bf16[24,3968]{1,0:T(8,128)(2,1)S(1)}, bf16[24,3968]{1,0:T(8,128)(2,1)S(1)}, u32[]{:S(2)}, u32[]{:S(2)}) collective-permute-start(bf16[24,3968]{1,0:T(8,128)(2,1)S(1)} %get-tuple-element.228), channel_id=1, source_target_pairs={{0,2},{1,3},{2,0},{3,1},{4,6},{5,7},{6,4},{7,5},{8,10},{9,11},{10,... | collective-permute-start | bytes 571400 | tf_op jit(solution)/shard_map/ppermute | solution.py:158
  294.2 16.3 %collective-permute-start.51 = (bf16[24,3968]{1,0:T(8,128)(2,1)S(1)}, bf16[24,3968]{1,0:T(8,128)(2,1)S(1)}, u32[]{:S(2)}, u32[]{:S(2)}) collective-permute-start(bf16[24,3968]{1,0:T(8,128)(2,1)S(1)} %get-tuple-element.227), channel_id=1, source_target_pairs={{0,3},{1,0},{2,1},{3,2},{4,7},{5,4},{6,5},{7,6},{8,11},{9,8},{10,9... | collective-permute-start | bytes 571400 | tf_op jit(solution)/shard_map/ppermute | solution.py:158
  300.3 6.4 %collective-permute-start.41 = (bf16[96,1280]{1,0:T(8,128)(2,1)S(1)}, bf16[96,1280]{1,0:T(8,128)(2,1)S(1)}, u32[]{:S(2)}, u32[]{:S(2)}) collective-permute-start(bf16[96,1280]{1,0:T(8,128)(2,1)S(1)} %dynamic-slice_bitcast_fusion.15), channel_id=1, source_target_pairs={{0,16},{4,20},{8,24},{12,28},{16,0},{20,4},{24,8},{28,12},{1,17},{... | collective-permute-start | bytes 737288 | tf_op jit(solution)/shard_map/ppermute | solution.py:34
  301.1 6.1 %collective-permute-start.44 = (bf16[96,1280]{1,0:T(8,128)(2,1)S(1)}, bf16[96,1280]{1,0:T(8,128)(2,1)S(1)}, u32[]{:S(2)}, u32[]{:S(2)}) collective-permute-start(bf16[96,1280]{1,0:T(8,128)(2,1)S(1)} %dynamic-slice_bitcast_fusion.14), channel_id=1, source_target_pairs={{0,8},{4,12},{8,0},{12,4},{16,24},{20,28},{24,16},{28,20},{1,9},{5... | collective-permute-start | bytes 737288 | tf_op jit(solution)/shard_map/ppermute | solution.py:34
  312.1 3.8 %collective-permute-start.45 = (bf16[24,2560]{1,0:T(8,128)(2,1)S(1)}, bf16[24,2560]{1,0:T(8,128)(2,1)S(1)}, u32[]{:S(2)}, u32[]{:S(2)}) collective-permute-start(bf16[24,2560]{1,0:T(8,128)(2,1)S(1)} %get-tuple-element.232), channel_id=1, source_target_pairs={{0,1},{1,2},{2,3},{3,0},{4,5},{5,6},{6,7},{7,4},{8,9},{9,10},{10,1... | collective-permute-start | bytes 368648 | tf_op jit(solution)/shard_map/ppermute | solution.py:158
  312.2 5.4 %collective-permute-start.46 = (bf16[24,2560]{1,0:T(8,128)(2,1)S(1)}, bf16[24,2560]{1,0:T(8,128)(2,1)S(1)}, u32[]{:S(2)}, u32[]{:S(2)}) collective-permute-start(bf16[24,2560]{1,0:T(8,128)(2,1)S(1)} %get-tuple-element.234), channel_id=1, source_target_pairs={{0,2},{1,3},{2,0},{3,1},{4,6},{5,7},{6,4},{7,5},{8,10},{9,11},{10,... | collective-permute-start | bytes 368648 | tf_op jit(solution)/shard_map/ppermute | solution.py:158
  313.3 11.7 %collective-permute-start.47 = (bf16[24,2560]{1,0:T(8,128)(2,1)S(1)}, bf16[24,2560]{1,0:T(8,128)(2,1)S(1)}, u32[]{:S(2)}, u32[]{:S(2)}) collective-permute-start(bf16[24,2560]{1,0:T(8,128)(2,1)S(1)} %get-tuple-element.233), channel_id=1, source_target_pairs={{0,3},{1,0},{2,1},{3,2},{4,7},{5,4},{6,5},{7,6},{8,11},{9,8},{10,9... | collective-permute-start | bytes 368648 | tf_op jit(solution)/shard_map/ppermute | solution.py:158
  (14 other events, 41.8 us)
